TPU v7x, 256 devices: a whole 4x4x8 slice. The times are simulated.
256 devices in a mesh: tm: 32 (over y, z), space: 8 (over x, core).
Axes of the slice: x: 4, y: 4, z: 8, core: 2. Of those that a mesh axis runs over, the one named last changes fastest.
Arguments:
- start_states: float32 [32, 3, 16, 128, 256], P('tm', None, None, 'space'), may hold values from -6 to 6
- labels: int32 [16, 128, 256], P(None, 'space'), may hold values 0 or 1
Outputs:
- next_states: float32 [32, 3, 16, 128, 256], P('tm', None, None, 'space')
All inputs are finite; a program needn't handle non-finite values. No bound on the sum of `labels` on one device may be relied on, other than what follows from the above.
Results may differ from a plain program's by a relative error of at most 0.0001.
Values sent between devices are 32-bit elements; how exact they have to be, the bound alone decides.
No kernel may reach another device: no remote copies, remote signals or barrier semaphores. Data moves between devices by JAX's collectives and lax.ppermute only.
A program may use at most 128 MiB of HBM per device.

v0:
```python
import jax
import jax.numpy as jnp
from jax import lax
from jax.sharding import PartitionSpec as P

VCYCLES = 2
COARSE_SWEEPS = 4


viscosity = 0.1
buoyancy = 0.2
relaxation = 0.8
coarse_rate = 0.15


def with_halo(cells, sides, width):
    for axis, dim in sides:
        count = lax.axis_size(axis)
        ends = count - 1
        head = lax.slice_in_dim(cells, 0, width, axis=dim)
        tail = lax.slice_in_dim(cells, cells.shape[dim] - width, cells.shape[dim], axis=dim)
        cells = jnp.concatenate(
            [
                lax.ppermute(tail, axis, [(i, (i + 1) % count) for i in range(ends)]),
                cells,
                lax.ppermute(head, axis, [((i + 1) % count, i) for i in range(ends)]),
            ],
            axis=dim,
        )
    return cells


def passed_along(shard, axis, by):
    peers = lax.axis_size(axis)
    pairs = [(i, i + by) for i in range(peers) if 0 <= i + by < peers]
    return lax.ppermute(shard, axis, pairs)


def neighbour(values, direction, offset):
    position = values.ndim + direction
    padding = [(0, 0)] * values.ndim
    padding[position] = (1, 1)
    padded = jnp.pad(values, padding)
    length = values.shape[position]
    return lax.slice_in_dim(padded, 1 + offset, 1 + offset + length, axis=position)


def restrict(values):
    leading = values.shape[:-3]
    depth_cells, across_cells, height_cells = values.shape[-3:]
    shaped = values.reshape(
        leading + (depth_cells // 2, 2, across_cells // 2, 2, height_cells // 2, 2)
    )
    return jnp.mean(shaped, axis=(-5, -3, -1))


def prolong(values):
    return jnp.repeat(jnp.repeat(jnp.repeat(values, 2, axis=-3), 2, axis=-2), 2, axis=-1)


def laplace_with(values, upper_across, lower_across):
    summed = neighbour(values, -3, 1) + neighbour(values, -3, -1) + upper_across + lower_across
    summed = summed + neighbour(values, -1, 1) + neighbour(values, -1, -1)
    return summed - 6.0 * values


def face_weights(mobility, upper_across, lower_across):
    return (
        (
            0.5 * (mobility + neighbour(mobility, -3, 1)),
            0.5 * (mobility + neighbour(mobility, -3, -1)),
        ),
        (0.5 * (mobility + upper_across), 0.5 * (mobility + lower_across)),
        (
            0.5 * (mobility + neighbour(mobility, -1, 1)),
            0.5 * (mobility + neighbour(mobility, -1, -1)),
        ),
    )


def scaled_weights(weights):
    return tuple(((0.25 * upper_face, 0.25 * lower_face) for upper_face, lower_face in weights))


def weight_sum(weights):
    summed = weights[0][0] + weights[0][1]
    for upper_face, lower_face in weights[1:]:
        summed = summed + upper_face + lower_face
    return summed


def apply_weights(values, upper_across, lower_across, weights):
    depth_pair, across_pair, height_pair = weights
    summed = depth_pair[0] * (values - neighbour(values, -3, 1)) + depth_pair[1] * (
        values - neighbour(values, -3, -1)
    )
    summed = (
        summed + across_pair[0] * (values - upper_across) + across_pair[1] * (values - lower_across)
    )
    return (
        summed
        + height_pair[0] * (values - neighbour(values, -1, 1))
        + height_pair[1] * (values - neighbour(values, -1, -1))
    )


def pressure_sides(values):
    widened = with_halo(values, (("space", 1),), 1)
    extent = values.shape[1]
    return (widened[:, 2 : 2 + extent], widened[:, :extent])


def fine_operate(values, weights):
    upper_side, lower_side = pressure_sides(values)
    return apply_weights(values, upper_side, lower_side, weights)


def coarse_split(values, coarse_wide, mobility_coarse):
    widened = with_halo(values, (("space", 2),), 2)
    extent = values.shape[2]
    inner = widened[:, :, 1 : 3 + extent]
    mobility_inner = coarse_wide[:, 3 : 5 + extent]
    first_pass = inner + coarse_rate * mobility_inner * laplace_with(
        inner, widened[:, :, 2 : 4 + extent], widened[:, :, 0 : 2 + extent]
    )
    centre = first_pass[:, :, 1 : 1 + extent]
    return centre + coarse_rate * mobility_coarse * laplace_with(
        centre, first_pass[:, :, 2 : 2 + extent], first_pass[:, :, 0:extent]
    )


def body(start_states, labels):
    initial = start_states[0]
    mobility = 1.0 / (1.0 + 3.0 * labels.astype(jnp.float32))
    extent = mobility.shape[1]
    coarse_extent = extent // 2
    mobility_wide = with_halo(mobility, (("space", 1),), 8)
    weights = face_weights(
        mobility, mobility_wide[:, 9 : 9 + extent], mobility_wide[:, 7 : 7 + extent]
    )
    diagonal = weight_sum(weights)
    coarse_wide = restrict(mobility_wide)
    mobility_coarse = coarse_wide[:, 4 : 4 + coarse_extent]
    coarse_weights = scaled_weights(
        face_weights(
            mobility_coarse,
            coarse_wide[:, 5 : 5 + coarse_extent],
            coarse_wide[:, 3 : 3 + coarse_extent],
        )
    )
    coarse_diagonal = weight_sum(coarse_weights)
    velocity_wide = with_halo(initial, (("space", 2),), 1)
    zeros_field = jnp.zeros_like(mobility)
    predicted = initial + viscosity * laplace_with(
        initial, velocity_wide[:, :, 2 : 2 + extent], velocity_wide[:, :, :extent]
    )
    predicted = predicted + jnp.stack([buoyancy * (2.0 * mobility - 1.0), zeros_field, zeros_field])
    flux_wide = with_halo(predicted[1], (("space", 1),), 1)
    spread = (
        neighbour(predicted[0], -3, 1)
        - neighbour(predicted[0], -3, -1)
        + (flux_wide[:, 2 : 2 + extent] - flux_wide[:, :extent])
    )
    spread = spread + (neighbour(predicted[2], -1, 1) - neighbour(predicted[2], -1, -1))
    target = -0.5 * spread
    pressure = relaxation * target / diagonal
    for cycle_number in range(VCYCLES):
        if cycle_number > 0:
            pressure = pressure + relaxation * (target - fine_operate(pressure, weights)) / diagonal
        leftover = restrict(target - fine_operate(pressure, weights))
        correction = relaxation * leftover / coarse_diagonal
        for sweep_number in range(COARSE_SWEEPS - 1):
            widened = with_halo(correction, (("space", 1),), 1)
            applied = apply_weights(
                correction,
                widened[:, 2 : 2 + coarse_extent],
                widened[:, :coarse_extent],
                coarse_weights,
            )
            correction = correction + relaxation * (leftover - applied) / coarse_diagonal
        pressure = pressure + prolong(correction)
        pressure = pressure + relaxation * (target - fine_operate(pressure, weights)) / diagonal
    upper_side, lower_side = pressure_sides(pressure)
    gradient = jnp.stack(
        [
            0.5 * (neighbour(pressure, -3, 1) - neighbour(pressure, -3, -1)),
            0.5 * (upper_side - lower_side),
            0.5 * (neighbour(pressure, -1, 1) - neighbour(pressure, -1, -1)),
        ]
    )
    ending = predicted - mobility * gradient
    coarse_start = restrict(initial)
    coarse_end = restrict(ending)
    first_device = lax.axis_index("tm") == 0
    source, coarse_ends = (coarse_start, coarse_end)

    def advance(values):
        return coarse_split(values, coarse_wide, mobility_coarse)

    def handoff(values):
        return passed_along(values, "tm", 1)

    propagated = advance(source)
    offset_term = coarse_ends - propagated

    def advance_turn(turn_number, current):
        incoming = jnp.where(first_device, source, handoff(current))
        return advance(incoming) + offset_term

    final_state = lax.fori_loop(0, lax.axis_size("tm") - 1, advance_turn, propagated + offset_term)
    corrected = ending + prolong(final_state - coarse_end)
    return corrected[None]


def solution(mesh):
    in_specs = (P("tm", None, None, "space", None), P(None, "space", None))
    out_specs = P("tm", None, None, "space", None)
    return jax.shard_map(body, mesh=mesh, in_specs=in_specs, out_specs=out_specs, check_vma=False)
```

profile of v0, /device:TPU:24, one launch (start us, length us, event | category | flops | bytes accessed | tf_op | source)
XLA Modules:
  0.0 891.6 jit_solution(10043692311517419654)
XLA Ops:
  28.1 34.8 %reshape.48 = f32[8,2,16,2,128,2]{5,4,3,2,1,0:T(8,128)} reshape(f32[16,32,256]{2,1,0:T(8,128)S(1)} %pad_maximum_fusion.4) | data formatting | bytes 1048576 | tf_op jit(solution)/shard_map/reshape | solution.py:51
  63.0 12.2 %reduce_sum.46 = f32[8,16,128]{2,1,0:T(8,128)S(1)} reduce(f32[8,2,16,2,128,2]{5,4,3,2,1,0:T(8,128)} %reshape.48, f32[]{:T(128)} %constant.69.clone.1), dimensions={1,3,5}, to_apply=%region_1.2 | reduce | flops 114688 | bytes 589828 | tf_op jit(solution)/shard_map/reduce_sum | solution.py:54
  75.6 18.1 %reshape.47 = f32[8,2,8,2,128,2]{5,4,3,2,1,0:T(8,128)} reshape(f32[16,16,256]{2,1,0:T(8,128)S(1)} %fusion.41) | data formatting | bytes 524288 | tf_op jit(solution)/shard_map/reshape | solution.py:51
  93.7 7.0 reduce_sum.45
  153.7 51.6 %reshape_squeeze.3 = f32[3,8,2,8,2,128,2]{6,5,4,3,2,1,0:T(8,128)} reshape(f32[1,3,16,16,256]{4,3,2,1,0:T(8,128)S(1)} %copy-done) | data formatting | bytes 1572864 | tf_op jit(solution)/shard_map/reshape;squeeze | solution.py:51
  205.3 18.4 %reduce_sum.48 = f32[3,8,8,128]{3,2,1,0:T(8,128)} reduce(f32[3,8,2,8,2,128,2]{6,5,4,3,2,1,0:T(8,128)} %reshape_squeeze.3, f32[]{:T(128)} %constant.69.clone.1), dimensions={2,4,6}, to_apply=%region_3.4 | reduce | flops 172032 | bytes 884740 | tf_op jit(solution)/shard_map/reduce_sum | solution.py:54
  226.8 18.8 %reshape.52 = f32[8,2,8,2,128,2]{5,4,3,2,1,0:T(8,128)} reshape(f32[16,16,256]{2,1,0:T(8,128)} %fusion.77) | data formatting | bytes 524288 | tf_op jit(solution)/shard_map/reshape | solution.py:51
  245.6 7.0 reduce_sum.47
  307.8 51.6 %reshape.56 = f32[3,8,2,8,2,128,2]{6,5,4,3,2,1,0:T(8,128)} reshape(f32[3,16,16,256]{3,2,1,0:T(8,128)S(1)} %fusion.26) | data formatting | bytes 1572864 | tf_op jit(solution)/shard_map/reshape | solution.py:51
  359.4 17.8 %reduce_sum.49 = f32[3,8,8,128]{3,2,1,0:T(8,128)S(1)} reduce(f32[3,8,2,8,2,128,2]{6,5,4,3,2,1,0:T(8,128)} %reshape.56, f32[]{:T(128)} %constant.69.clone.1), dimensions={2,4,6}, to_apply=%region_4.5 | reduce | flops 172032 | bytes 884740 | tf_op jit(solution)/shard_map/reduce_sum | solution.py:54
  377.4 500.1 %while.12 = (s32[]{:T(128)}, f32[3,8,8,128]{3,2,1,0:T(8,128)S(1)}, pred[]{:T(512)}, f32[3,8,8,128]{3,2,1,0:T(8,128)S(1)}, f32[8,16,128]{2,1,0:T(8,128)S(1)}, /*i...) while((s32[]{:T(128)}, f32[3,8,8,128]{3,2,1,0:T(8,128)S(1)}, pred[]{:T(512)}, ...), condition=%wide.region_6.7_spmd, body=%wide.region_5.6_spmd.sunk | while | flops 688130 | bytes 2556110 | solution.py:210
  381.2 6.7 collective-permute-done
  411.4 6.7 collective-permute-done
  427.5 6.7 collective-permute-done
  443.7 6.7 collective-permute-done
  459.8 6.7 collective-permute-done
  605.1 6.7 collective-permute-done
  621.2 6.7 collective-permute-done
  637.4 6.7 collective-permute-done
  653.5 6.7 collective-permute-done
  669.6 6.7 collective-permute-done
  685.8 6.7 collective-permute-done
  701.9 6.7 collective-permute-done
  718.1 6.7 collective-permute-done
  (610 shorter events, 563.4 us)
Async XLA Ops:
  1.2 10.4 %collective-permute-start.3 = (f32[3,16,1,256]{3,1,2,0:T(8,128)S(1)}, f32[3,16,1,256]{3,1,2,0:T(8,128)S(1)}, u32[]{:S(2)}, u32[]{:S(2)}) collective-permute-start(f32[3,16,1,256]{3,1,2,0:T(8,128)S(1)} %copy.161), channel_id=1, source_target_pairs={{1,0},{2,1},{3,2},{4,3},{5,4},{6,5},{7,6},{9,8},{10,9},{11,10},{12... | collective-permute-start | bytes 147464 | tf_op jit(solution)/shard_map/ppermute | solution.py:26
  2.5 9.1 %collective-permute-start.4 = (f32[3,16,1,256]{3,1,2,0:T(8,128)S(1)}, f32[3,16,1,256]{3,1,2,0:T(8,128)S(1)}, u32[]{:S(2)}, u32[]{:S(2)}) collective-permute-start(f32[3,16,1,256]{3,1,2,0:T(8,128)S(1)} %copy.163), channel_id=1, source_target_pairs={{0,1},{1,2},{2,3},{3,4},{4,5},{5,6},{6,7},{8,9},{9,10},{10,11},{11... | collective-permute-start | bytes 147464 | tf_op jit(solution)/shard_map/ppermute | solution.py:24
  6.6 15.3 %collective-permute-start.7 = (f32[16,8,256]{2,1,0:T(8,128)S(1)}, f32[16,8,256]{2,1,0:T(8,128)S(1)}, u32[]{:S(2)}, u32[]{:S(2)}) collective-permute-start(f32[16,8,256]{2,1,0:T(8,128)S(1)} %get-tuple-element.149), channel_id=1, source_target_pairs={{1,0},{2,1},{3,2},{4,3},{5,4},{6,5},{7,6},{9,8},{10,9},{11,10},{12... | collective-permute-start | bytes 393224 | tf_op jit(solution)/shard_map/ppermute | solution.py:26
  7.9 14.0 %collective-permute-start.8 = (f32[16,8,256]{2,1,0:T(8,128)S(1)}, f32[16,8,256]{2,1,0:T(8,128)S(1)}, u32[]{:S(2)}, u32[]{:S(2)}) collective-permute-start(f32[16,8,256]{2,1,0:T(8,128)S(1)} %get-tuple-element.148), channel_id=1, source_target_pairs={{0,1},{1,2},{2,3},{3,4},{4,5},{5,6},{6,7},{8,9},{9,10},{10,11},{11... | collective-permute-start | bytes 393224 | tf_op jit(solution)/shard_map/ppermute | solution.py:24
  22.4 52.7 %collective-permute-start.9 = (f32[16,1,256]{2,0,1:T(8,128)S(1)}, f32[16,1,256]{2,0,1:T(8,128)S(1)}, u32[]{:S(2)}, u32[]{:S(2)}) collective-permute-start(f32[16,1,256]{2,0,1:T(8,128)S(1)} %copy.169), channel_id=1, source_target_pairs={{1,0},{2,1},{3,2},{4,3},{5,4},{6,5},{7,6},{9,8},{10,9},{11,10},{12... | collective-permute-start | bytes 49160 | tf_op jit(solution)/shard_map/ppermute | solution.py:26
  23.8 51.5 %collective-permute-start.10 = (f32[16,1,256]{2,0,1:T(8,128)S(1)}, f32[16,1,256]{2,0,1:T(8,128)S(1)}, u32[]{:S(2)}, u32[]{:S(2)}) collective-permute-start(f32[16,1,256]{2,0,1:T(8,128)S(1)} %copy.171), channel_id=1, source_target_pairs={{0,1},{1,2},{2,3},{3,4},{4,5},{5,6},{6,7},{8,9},{9,10},{10,11},{11... | collective-permute-start | bytes 49160 | tf_op jit(solution)/shard_map/ppermute | solution.py:24
  147.3 76.4 %collective-permute-start.21 = (f32[16,1,256]{2,0,1:T(8,128)S(1)}, f32[16,1,256]{2,0,1:T(8,128)S(1)}, u32[]{:S(2)}, u32[]{:S(2)}) collective-permute-start(f32[16,1,256]{2,0,1:T(8,128)S(1)} %copy.184), channel_id=1, source_target_pairs={{1,0},{2,1},{3,2},{4,3},{5,4},{6,5},{7,6},{9,8},{10,9},{11,10},{12... | collective-permute-start | bytes 49160 | tf_op jit(solution)/shard_map/ppermute | solution.py:26
  148.6 75.1 %collective-permute-start.22 = (f32[16,1,256]{2,0,1:T(8,128)S(1)}, f32[16,1,256]{2,0,1:T(8,128)S(1)}, u32[]{:S(2)}, u32[]{:S(2)}) collective-permute-start(f32[16,1,256]{2,0,1:T(8,128)S(1)} %copy.186), channel_id=1, source_target_pairs={{0,1},{1,2},{2,3},{3,4},{4,5},{5,6},{6,7},{8,9},{9,10},{10,11},{11... | collective-permute-start | bytes 49160 | tf_op jit(solution)/shard_map/ppermute | solution.py:24
  261.2 12.1 %collective-permute-start.25 = (f32[8,1,128]{2,1,0:T(1,128)S(1)}, f32[8,1,128]{2,1,0:T(1,128)S(1)}, u32[]{:S(2)}, u32[]{:S(2)}) collective-permute-start(f32[8,1,128]{2,1,0:T(1,128)S(1)} %get-tuple-element.159), channel_id=1, source_target_pairs={{1,0},{2,1},{3,2},{4,3},{5,4},{6,5},{7,6},{9,8},{10,9},{11,10},{12... | collective-permute-start | bytes 12296 | tf_op jit(solution)/shard_map/ppermute | solution.py:26
  262.4 10.8 %collective-permute-start.26 = (f32[8,1,128]{2,1,0:T(1,128)S(1)}, f32[8,1,128]{2,1,0:T(1,128)S(1)}, u32[]{:S(2)}, u32[]{:S(2)}) collective-permute-start(f32[8,1,128]{2,1,0:T(1,128)S(1)} %get-tuple-element.160), channel_id=1, source_target_pairs={{0,1},{1,2},{2,3},{3,4},{4,5},{5,6},{6,7},{8,9},{9,10},{10,11},{11... | collective-permute-start | bytes 12296 | tf_op jit(solution)/shard_map/ppermute | solution.py:24
  267.4 12.1 %collective-permute-start.33 = (f32[3,8,2,128]{3,2,1,0:T(2,128)}, f32[3,8,2,128]{3,2,1,0:T(2,128)}, u32[]{:S(2)}, u32[]{:S(2)}) collective-permute-start(f32[3,8,2,128]{3,2,1,0:T(2,128)} %get-tuple-element.154), channel_id=1, source_target_pairs={{0,1},{1,2},{2,3},{3,4},{4,5},{5,6},{6,7},{8,9},{9,10},{10,11},{11... | collective-permute-start | bytes 73736 | tf_op jit(solution)/shard_map/ppermute | solution.py:24
  377.4 10.5 %collective-permute-start = (f32[3,8,8,128]{3,2,1,0:T(8,128)S(1)}, f32[3,8,8,128]{3,2,1,0:T(8,128)S(1)}, u32[]{:S(2)}, u32[]{:S(2)}) collective-permute-start(f32[3,8,8,128]{3,2,1,0:T(8,128)S(1)} %get-tuple-element.225), channel_id=1, source_target_pairs={{0,8},{8,16},{16,24},{24,32},{32,40},{40,48},{48,56},{56,64},{64,7... | collective-permute-start | bytes 294920 | tf_op jit(solution)/shard_map/while/body/eval_jaxpr/ppermute | solution.py:36
  394.5 8.6 collective-permute-start
  409.4 8.6 collective-permute-start
  425.6 8.6 collective-permute-start
  441.7 8.6 collective-permute-start
  457.8 8.6 collective-permute-start
  474.0 8.6 collective-permute-start
  490.1 8.6 collective-permute-start
  506.3 8.6 collective-permute-start
  522.4 8.6 collective-permute-start
  538.6 8.6 collective-permute-start
  554.7 8.6 collective-permute-start
  570.8 8.6 collective-permute-start
  (114 other events, 863.6 us)
where the time goes:
time: 902 us; the launch traced here: 892 us
  starting transfers between devices  343 us (38%)
  waiting for transfers between devices  238 us (26%)
  local copies, waits for them, and re-layouts  211 us (23%)
  other arithmetic  96.2 us (11%)
    ppermute x47, starting transfers between devices, with_halo(): lax.ppermute(tail, axis, [(i, (i + 1) % count) for i in range(ends)])  221 us
    ppermute x31, waiting for transfers between devices, passed_along(): return lax.ppermute(shard, axis, pairs)  207 us
    reshape x4, local copies, waits for them, and re-layouts, restrict(): values.reshape(leading + (depth_cells // 2, 2, across_cells // 2, 2, heig...  123 us
    reduce_sum x5, other arithmetic, restrict(): return jnp.mean(shaped, axis=(-5, -3, -1))  62.4 us
    ppermute x31, starting transfers between devices, passed_along(): return lax.ppermute(shard, axis, pairs)  61.4 us
    ppermute x47, starting transfers between devices, with_halo(): lax.ppermute(head, axis, [((i + 1) % count, i) for i in range(ends)])  60.7 us
    another operation x1, local copies, waits for them, and re-layouts, restrict(): values.reshape(leading + (depth_cells // 2, 2, across_cells // 2, 2, heig...  51.6 us
    ppermute x47, waiting for transfers between devices, with_halo(): lax.ppermute(tail, axis, [(i, (i + 1) % count) for i in range(ends)])  30.5 us
  transfers between devices with their start and end apart: 125, of which 69 were waited for; matrix products, arithmetic and copies ran while one was open for 14% of the time, Pallas kernels for 0%

commit v1 on v0

v1 whole, which is shorter than its diff:
```python
import jax
import jax.numpy as jnp
from jax import lax
from jax.experimental import pallas as pl
from jax.experimental.pallas import tpu as pltpu
from jax.sharding import Mesh, PartitionSpec as P

F32 = jnp.float32
HIGH = lax.Precision.HIGHEST
VM = pl.BlockSpec(memory_space=pltpu.VMEM)
SM = pl.BlockSpec(memory_space=pltpu.SMEM)

NXB = 16
HS = 11
HP = 10
WN = NXB + 2 * HP
CN = WN // 2


def shape(*dims):
    return jax.ShapeDtypeStruct(dims, F32)


def call(kernel, outs, ins, scratch=(), flops=1000000):
    specs = [SM if a.dtype == jnp.int32 and a.ndim == 1 else VM for a in ins]
    moved = sum(a.size * 4 for a in ins) + sum(4 * _size(o) for o in outs)
    return pl.pallas_call(
        kernel,
        out_shape=outs,
        in_specs=specs,
        out_specs=[VM] * len(outs),
        scratch_shapes=list(scratch),
        compiler_params=pltpu.CompilerParams(vmem_limit_bytes=28 * 1024 * 1024),
        cost_estimate=pl.CostEstimate(flops=flops, bytes_accessed=moved, transcendentals=0),
    )(*ins)


def _size(o):
    n = 1
    for d in o.shape:
        n *= d
    return n


def loop(lo, hi, fn, unroll=2):
    assert (hi - lo) % unroll == 0

    def step(t, carry):
        for u in range(unroll):
            fn(lo + t * unroll + u)
        return carry

    lax.fori_loop(0, (hi - lo) // unroll, step, 0)


def iota(dim):
    return lax.broadcasted_iota(jnp.int32, (8, 128), dim)


def quad(ref, *at):
    return [[ref[(*at, zp, slice(None), slice(128 * yp, 128 * yp + 128))] for yp in (0, 1)] for zp in (0, 1)]


def put(ref, at, zp, yp, value):
    ref[(*at, zp, slice(None), slice(128 * yp, 128 * yp + 128))] = value


def z_up(v, fix=None):
    f = fix or (lambda r: r)
    return [v[1], [f(pltpu.roll(v[0][q], 7, 0)) for q in (0, 1)]]


def z_down(v, fix=None):
    f = fix or (lambda r: r)
    return [[f(pltpu.roll(v[1][q], 1, 0)) for q in (0, 1)], v[0]]


def y_up(v, fix=None):
    f = fix or (lambda r: r)
    return [[v[q][1], f(pltpu.roll(v[q][0], 127, 1))] for q in (0, 1)]


def y_down(v, fix=None):
    f = fix or (lambda r: r)
    return [[f(pltpu.roll(v[q][1], 1, 1)), v[q][0]] for q in (0, 1)]


class Fix:
    def __init__(self):
        k, j = iota(0), iota(1)
        self.zu = lambda r: jnp.where(k < 7, r, 0.0)
        self.zd = lambda r: jnp.where(k > 0, r, 0.0)
        self.yu = lambda r: jnp.where(j < 127, r, 0.0)
        self.yd = lambda r: jnp.where(j > 0, r, 0.0)


def coarse_near(v, fix):
    return (
        fix.zu(pltpu.roll(v, 7, 0)),
        fix.zd(pltpu.roll(v, 1, 0)),
        fix.yu(pltpu.roll(v, 127, 1)),
        fix.yd(pltpu.roll(v, 1, 1)),
    )


def near(v, fix):
    return (z_up(v, fix.zu), z_down(v, fix.zd), y_up(v, fix.yu), y_down(v, fix.yd))


def raw_near(v):
    return (z_up(v), z_down(v), y_up(v), y_down(v))


QUAD = [(zp, yp) for zp in (0, 1) for yp in (0, 1)]


def eight(ref, i):
    total = None
    for layer in (i, i + 1):
        v = quad(ref, layer)
        for zp, yp in QUAD:
            total = v[zp][yp] if total is None else total + v[zp][yp]
    return total


def split_matrix():
    r = lax.broadcasted_iota(jnp.int32, (256, 256), 0)
    c = lax.broadcasted_iota(jnp.int32, (256, 256), 1)
    return jnp.where(r == jnp.where(c < 128, 2 * c, 2 * c - 255), 1.0, 0.0).astype(F32)


def join_matrix():
    r = lax.broadcasted_iota(jnp.int32, (256, 256), 0)
    c = lax.broadcasted_iota(jnp.int32, (256, 256), 1)
    return jnp.where(c == jnp.where(r < 128, 2 * r, 2 * r - 255), 1.0, 0.0).astype(F32)


def rows_of(x, zp):
    return pl.ds(zp * NXB + x, 8, stride=2 * NXB)


def prepare(info, start, labels, s_out, m_out, outer, inner, rows):
    core = info[0]
    split = split_matrix()
    for c in range(4):
        for x in range(NXB):
            for zp in (0, 1):
                to = pl.ds((x * 2 + zp) * 8, 8)
                for q in (0, 1):
                    cols = slice(128 * q, 128 * q + 128)
                    if c < 3:
                        rows[to, cols] = start[c * 2 + q, rows_of(x, zp), :]
                    else:
                        rows[to, cols] = 1.0 / (1.0 + 3.0 * labels[q, rows_of(x, zp), :].astype(F32))
        done = jnp.dot(rows[...], split, precision=HIGH, preferred_element_type=F32)
        done = done.reshape(NXB, 2, 8, 256)
        if c < 3:
            s_out[c] = done
        else:
            m_out[...] = done
    for c in range(3):
        outer[pl.ds(c * HS, HS)] = s_out[c, pl.ds((NXB - HS) * core, HS)]
        inner[pl.ds(c * HS, HS)] = s_out[c, pl.ds((NXB - HS) * (1 - core), HS)]
    outer[pl.ds(3 * HS, HP)] = m_out[pl.ds((NXB - HP) * core, HP)]
    inner[pl.ds(3 * HS, HP)] = m_out[pl.ds((NXB - HP) * (1 - core), HP)]


def interleave(base, nat):
    join = join_matrix()
    for c in range(3):
        done = jnp.dot(base[c].reshape(256, 256), join, precision=HIGH, preferred_element_type=F32)
        for x in range(NXB):
            for zp in (0, 1):
                at = (x * 2 + zp) * 8
                for q in (0, 1):
                    nat[c * 2 + q, rows_of(x, zp), :] = done[at : at + 8, 128 * q : 128 * q + 128]


def finish(nat, w, out):
    r = lax.broadcasted_iota(jnp.int32, (128, 256), 0)
    c = lax.broadcasted_iota(jnp.int32, (128, 256), 1)
    spread = jnp.where(lax.div(c, 2) == r, 1.0, 0.0).astype(F32)
    done = jnp.dot(w[...].reshape(192, 128), spread, precision=HIGH, preferred_element_type=F32)
    for comp in range(3):
        for xc in range(NXB // 2):
            at = (comp * 8 + xc) * 8
            for q in (0, 1):
                value = done[at : at + 8, 128 * q : 128 * q + 128]
                for xp in (0, 1):
                    for zp in (0, 1):
                        sl = rows_of(2 * xc + xp, zp)
                        out[comp * 2 + q, sl, :] = nat[comp * 2 + q, sl, :] + value


def valid_of(info):
    left, right = info[1].astype(F32), info[2].astype(F32)
    return lambda i, halo: jnp.where(i < halo, left, jnp.where(i >= halo + NXB, right, 1.0))


def weigh(valid, mw, wt, dg, inv, mc, cw, cinv, fix):
    def layer(i):
        m = quad(mw, i)
        sides = near(m, fix) + (quad(mw, i + 1), quad(mw, i - 1))
        ok = valid(i, HP)
        for zp, yp in QUAD:
            faces = [0.5 * (m[zp][yp] + s[zp][yp]) for s in sides]
            total = faces[0] + faces[1] + faces[2] + faces[3] + faces[4] + faces[5]
            if zp == 1:
                faces[0] = fix.zu(faces[0])
            else:
                faces[1] = fix.zd(faces[1])
            if yp == 1:
                faces[2] = fix.yu(faces[2])
            else:
                faces[3] = fix.yd(faces[3])
            for f in range(6):
                put(wt, (f, i), zp, yp, faces[f])
            put(dg, (i,), zp, yp, total)
            put(inv, (i,), zp, yp, (0.8 * ok) / (total + (1.0 - ok)))

    loop(1, WN - 1, layer)

    def coarse(j):
        mc[j] = 0.125 * eight(mw, 2 * j)

    loop(0, CN, coarse)

    def coarse_layer(j):
        m = mc[j]
        sides = coarse_near(m, fix) + (mc[j + 1], mc[j - 1])
        ok = valid(2 * j, HP)
        faces = [0.125 * (m + s) for s in sides]
        total = faces[0] + faces[1] + faces[2] + faces[3] + faces[4] + faces[5]
        faces[0] = fix.zu(faces[0])
        faces[1] = fix.zd(faces[1])
        faces[2] = fix.yu(faces[2])
        faces[3] = fix.yd(faces[3])
        for f in range(6):
            cw[f, j] = faces[f]
        cinv[j] = (0.8 * ok) / (total + (1.0 - ok))

    loop(1, CN - 1, coarse_layer)


def gathered(p, i, wt):
    v = quad(p, i)
    sides = raw_near(v) + (quad(p, i + 1), quad(p, i - 1))
    ws = [quad(wt, f, i) for f in range(6)]
    total = [[None, None], [None, None]]
    for zp, yp in QUAD:
        terms = [ws[f][zp][yp] * sides[f][zp][yp] for f in range(6)]
        total[zp][yp] = ((terms[0] + terms[1]) + (terms[2] + terms[3])) + (terms[4] + terms[5])
    return v, total


def smooth(lo, hi, p, q, tw, wt, inv, unroll=2):
    def layer(i):
        v, total = gathered(p, i, wt)
        t, n = quad(tw, i), quad(inv, i)
        for zp, yp in QUAD:
            put(q, (i,), zp, yp, 0.2 * v[zp][yp] + n[zp][yp] * (t[zp][yp] + total[zp][yp]))

    loop(lo, hi, layer, unroll)


def correct(p, tw, wt, dg, lo, ca, cb, cw, cinv):
    def coarse(j):
        out = None
        for i in (2 * j, 2 * j + 1):
            v, total = gathered(p, i, wt)
            t, d = quad(tw, i), quad(dg, i)
            for zp, yp in QUAD:
                r = (t[zp][yp] + total[zp][yp]) - d[zp][yp] * v[zp][yp]
                out = r if out is None else out + r
        out = 0.125 * out
        lo[j] = out
        ca[j] = cinv[j] * out

    loop(1, CN - 1, coarse, 1)

    def sweep(first, last, a, b):
        def layer(j):
            v = a[j]
            sides = (
                pltpu.roll(v, 7, 0),
                pltpu.roll(v, 1, 0),
                pltpu.roll(v, 127, 1),
                pltpu.roll(v, 1, 1),
                a[j + 1],
                a[j - 1],
            )
            terms = [cw[f, j] * sides[f] for f in range(6)]
            total = ((terms[0] + terms[1]) + (terms[2] + terms[3])) + (terms[4] + terms[5])
            b[j] = 0.2 * v + cinv[j] * (lo[j] + total)

        loop(first, last, layer)

    sweep(2, CN - 2, ca, cb)
    sweep(3, CN - 3, cb, ca)
    sweep(4, CN - 4, ca, cb)

    def add(j):
        g = cb[j]
        for i in (2 * j, 2 * j + 1):
            v = quad(p, i)
            for zp, yp in QUAD:
                put(p, (i,), zp, yp, v[zp][yp] + g)

    loop(4, CN - 4, add)


def first_cycle(info, s_own, m_own, off, on, pred, tw, mw, p1, outer, inner, gs, sw, wt, dg, inv, pr, p, mc, cw, cinv, lo, ca, cb, rs, rt):
    fix = Fix()
    core = info[0]
    valid = valid_of(info)
    off_s, on_s = core * (HS + NXB), (1 - core) * (HS + NXB)
    off_m, on_m = core * (HP + NXB), (1 - core) * (HP + NXB)
    for c in range(3):
        sw[c, pl.ds(HS, NXB)] = s_own[c]
        sw[c, pl.ds(off_s, HS)] = off[pl.ds(c * HS, HS)]
        sw[c, pl.ds(on_s, HS)] = on[pl.ds(c * HS, HS)]
    mw[pl.ds(HP, NXB)] = m_own[...]
    mw[pl.ds(off_m, HP)] = off[pl.ds(3 * HS, HP)]
    mw[pl.ds(on_m, HP)] = on[pl.ds(3 * HS, HP)]
    weigh(valid, mw, wt, dg, inv, mc, cw, cinv, fix)

    def predict(i):
        ok = valid(i, HP)
        m = quad(mw, i)
        for c in range(3):
            v = quad(sw, c, i + 1)
            sides = near(v, fix) + (quad(sw, c, i + 2), quad(sw, c, i))
            for zp, yp in QUAD:
                n = [s[zp][yp] for s in sides]
                total = ((n[0] + n[1]) + (n[2] + n[3])) + (n[4] + n[5])
                value = 0.4 * v[zp][yp] + 0.1 * total
                if c == 0:
                    value = value + (0.4 * m[zp][yp] - 0.2)
                put(pr, (c, i), zp, yp, ok * value)

    loop(0, WN, predict, 1)

    def aim(i):
        a, b = quad(pr, 0, i), quad(pr, 2, i)
        zu, zd = z_up(a, fix.zu), z_down(a, fix.zd)
        yu, yd = y_up(b, fix.yu), y_down(b, fix.yd)
        xu, xd = quad(pr, 1, i + 1), quad(pr, 1, i - 1)
        n = quad(inv, i)
        for zp, yp in QUAD:
            t = (zu[zp][yp] - zd[zp][yp]) + (xu[zp][yp] - xd[zp][yp])
            t = -0.5 * (t + (yu[zp][yp] - yd[zp][yp]))
            put(tw, (i,), zp, yp, t)
            put(p, (i,), zp, yp, n[zp][yp] * t)

    loop(1, WN - 1, aim)
    for c in range(3):
        pred[c] = pr[c, pl.ds(HP, NXB)]

    correct(p, tw, wt, dg, lo, ca, cb, cw, cinv)

    def last(x):
        i = x + HP
        v, total = gathered(p, i, wt)
        t, n = quad(tw, i), quad(inv, i)
        for zp, yp in QUAD:
            put(p1, (x,), zp, yp, 0.2 * v[zp][yp] + n[zp][yp] * (t[zp][yp] + total[zp][yp]))

    loop(0, NXB, last)
    outer[...] = p1[pl.ds((NXB - HP) * core, HP)]
    inner[...] = p1[pl.ds((NXB - HP) * (1 - core), HP)]

    later = info[3].astype(F32)

    def shrink(q):
        for c in range(3):
            rs[c, q] = 0.125 * eight(sw.at[c], 2 * q + 7)

    loop(0, 12, shrink, 1)

    def coarse_step(a, b, scale):
        def layer(q):
            m = mc[q + 3]
            for c in range(3):
                v = a[c, q]
                n = coarse_near(v, fix) + (a[c, q + 1], a[c, q - 1])
                total = ((n[0] + n[1]) + (n[2] + n[3])) + (n[4] + n[5])
                b(c, q, scale * ((1.0 - 0.9 * m) * v + (0.15 * m) * total))

        return layer

    def to_rt(c, q, value):
        rt[c, q] = value

    def to_gs(c, q, value):
        gs[c, q - 2] = value

    loop(1, 11, coarse_step(rs, to_rt, 1.0), 1)
    loop(2, 10, coarse_step(rt, to_gs, later), 1)


def second_cycle(info, pred, tw, mw, p1, off, on, gs, base, send, wt, dg, inv, p, q, mc, cw, cinv, lo, ca, cb):
    fix = Fix()
    core, row = info[0], info[4]
    valid = valid_of(info)
    p[pl.ds(HP, NXB)] = p1[...]
    p[pl.ds(core * (HP + NXB), HP)] = off[...]
    p[pl.ds((1 - core) * (HP + NXB), HP)] = on[...]
    weigh(valid, mw, wt, dg, inv, mc, cw, cinv, fix)
    smooth(1, WN - 1, p, q, tw, wt, inv)
    correct(q, tw, wt, dg, lo, ca, cb, cw, cinv)
    smooth(HP - 1, HP + NXB + 1, q, p, tw, wt, inv)

    def finish_pair(j):
        sums = [None, None, None]
        held = []
        for i in (2 * j, 2 * j + 1):
            v = quad(p, i + HP)
            sides = near(v, fix)
            xu, xd = quad(p, i + HP + 1), quad(p, i + HP - 1)
            m = quad(mw, i + HP)
            up = (sides[0], xu, sides[2])
            down = (sides[1], xd, sides[3])
            for c in range(3):
                a = quad(pred, c, i)
                for zp, yp in QUAD:
                    e = a[zp][yp] - (0.5 * m[zp][yp]) * (up[c][zp][yp] - down[c][zp][yp])
                    held.append((c, i, zp, yp, e))
                    sums[c] = e if sums[c] is None else sums[c] + e
        means = [0.125 * s for s in sums]
        for c, i, zp, yp, e in held:
            put(base, (c, i), zp, yp, e - means[c])
        for c in range(3):
            r = means[c] - gs[c, j]
            for to in range(4):
                send[to, c, lax.div(j, 4), lax.rem(j, 4)] = r
                if c == 0:
                    send[to, 3, lax.div(j, 4), lax.rem(j, 4)] = jnp.zeros_like(r)

    loop(0, NXB // 2, finish_pair, 1)
    for half in (0, 1):
        g = mc[HP // 2 + 4 * half + row]
        for to in range(4):
            for chip in range(4):
                send[to, chip, half, 4] = g


NC = 64


def substep(a, b, wa, wb, fix):
    for i in range(NC):
        v = a[i]
        n = coarse_near(v, fix)
        total = (n[0] + n[1]) + (n[2] + n[3])
        if i > 0:
            total = total + a[i - 1]
        if i < NC - 1:
            total = total + a[i + 1]
        b[i] = wa[i] * v + wb[i] * total


def advance(times, a, b, wa, wb, fix):
    def turn(t, carry):
        substep(a, b, wa, wb, fix)
        substep(b, a, wa, wb, fix)
        return carry

    lax.fori_loop(0, times, turn, 0)


def rows_scan(info, got, swapped, acc, half, wa, wb, b):
    fix = Fix()
    core, row = info[0], info[4]
    for s in range(8):
        for l in range(4):
            for at, src in ((8 * s + 4 * core + l, got), (8 * s + 4 * (1 - core) + l, swapped)):
                m = src[l, s, 4]
                wa[at] = 1.0 - 0.9 * m
                wb[at] = 0.15 * m
                acc[at] = src[0, s, l]
    for t in range(1, 4):

        @pl.when(t <= row)
        def _():
            advance(8, acc, b, wa, wb, fix)
            for s in range(8):
                for l in range(4):
                    own, other = 8 * s + 4 * core + l, 8 * s + 4 * (1 - core) + l
                    acc[own] = acc[own] + got[t, s, l]
                    acc[other] = acc[other] + swapped[t, s, l]

    half[...] = acc[pl.ds(NC // 2 * core, NC // 2)]


def shift_scan(times, last):
    def kernel(info, acc, own, other, wa, wb, *rest):
        if last:
            half, a, b = rest
            out = a
        else:
            out, half, a, b = rest
        fix = Fix()
        core = info[0]
        a[pl.ds(NC // 2 * core, NC // 2)] = own[...]
        a[pl.ds(NC // 2 * (1 - core), NC // 2)] = other[...]
        advance(times, a, b, wa, wb, fix)
        for i in range(NC):
            out[i] = acc[i] + a[i]
        if last:
            for s in range(8):
                half[s] = out[pl.ds(8 * s + 4 * core, 4)]
        else:
            half[...] = out[pl.ds(NC // 2 * core, NC // 2)]

    return kernel


def body(ny, nz, start_states, labels):
    ns = lax.axis_size("space")
    s = lax.axis_index("space")
    y = lax.axis_index("y")
    z = lax.axis_index("z")
    core = lax.rem(s, 2)
    info = jnp.stack([core, s > 0, s < ns - 1, y * nz + z > 0, y, s, s, s]).astype(jnp.int32)
    swap = [(i, i ^ 1) for i in range(ns)]
    cross = [(i, i + 1) for i in range(1, ns - 1, 2)]
    cross = cross + [(b, a) for a, b in cross]

    def exchange(outer, inner):
        off = lax.ppermute(outer, "space", cross)
        on = lax.ppermute(inner, "space", swap)
        return off, on

    start = start_states[0].reshape(3, 256, 2, 128).transpose(0, 2, 1, 3).reshape(6, 256, 128)
    label = labels.reshape(256, 2, 128).transpose(1, 0, 2)
    layer = (2, 8, 256)
    edge = 3 * HS + HP
    vm = lambda *d: pltpu.VMEM(d, F32)
    s_own, m_own, outer, inner = call(
        prepare,
        [shape(3, NXB, *layer), shape(NXB, *layer), shape(edge, *layer), shape(edge, *layer)],
        [info, start, label],
        [vm(256, 256)],
    )
    off, on = exchange(outer, inner)
    coarse = [vm(CN, 8, 128), vm(6, CN, 8, 128), vm(CN, 8, 128), vm(CN, 8, 128), vm(CN, 8, 128), vm(CN, 8, 128)]
    fine = [vm(6, WN, *layer), vm(WN, *layer), vm(WN, *layer)]
    pred, tw, mw, p1, outer, inner, gs = call(
        first_cycle,
        [
            shape(3, NXB, *layer),
            shape(WN, *layer),
            shape(WN, *layer),
            shape(NXB, *layer),
            shape(HP, *layer),
            shape(HP, *layer),
            shape(3, 8, 8, 128),
        ],
        [info, s_own, m_own, off, on],
        [vm(3, NXB + 2 * HS, *layer)] + fine + [vm(3, WN, *layer), vm(WN, *layer)] + coarse + [vm(3, 12, 8, 128)] * 2,
    )
    off, on = exchange(outer, inner)
    base, send = call(
        second_cycle,
        [shape(3, NXB, *layer), shape(4, 4, 2, 5, 8, 128)],
        [info, pred, tw, mw, p1, off, on, gs],
        fine + [vm(WN, *layer), vm(WN, *layer)] + coarse,
    )
    got = lax.all_to_all(send.reshape(ny * ns, 5, 8, 128), ("y", "space"), 0, 0)
    got = got.reshape(ny, ns, 5, 8, 128)
    swapped = lax.ppermute(got, "space", swap)
    acc, half, wa, wb = call(
        rows_scan,
        [shape(NC, 8, 128), shape(NC // 2, 8, 128), shape(NC, 8, 128), shape(NC, 8, 128)],
        [info, got, swapped],
        [vm(NC, 8, 128)],
    )
    nt = ny * nz
    for k in (1, 2, 4):
        own = lax.ppermute(half, ("y", "z"), [(i, i + k) for i in range(nt - k)])
        other = lax.ppermute(own, "space", swap)
        last = k == 4
        outs = [shape(8, 4, 8, 128)] if last else [shape(NC, 8, 128), shape(NC // 2, 8, 128)]
        done = call(shift_scan(k, last), outs, [info, acc, own, other, wa, wb], [vm(NC, 8, 128)] * 2)
        if last:
            chunks = done[0]
        else:
            acc, half = done
    (nat,) = call(interleave, [shape(6, 256, 128)], [base])
    back = lax.all_to_all(chunks, "space", 0, 0)
    w = back[:6].reshape(3, 8, 8, 128)
    (out,) = call(finish, [shape(6, 256, 128)], [nat, w])
    out = out.reshape(3, 2, 256, 128).transpose(0, 2, 1, 3)
    return out.reshape(1, 3, 16, NXB, 256)


def solution(mesh):
    nz = 8
    ny = mesh.shape["tm"] // nz
    split = Mesh(mesh.devices.reshape(ny, nz, mesh.shape["space"]), ("y", "z", "space"))
    in_specs = (P(("y", "z"), None, None, "space", None), P(None, "space", None))
    out_specs = P(("y", "z"), None, None, "space", None)

    def run(start_states, labels):
        return body(ny, nz, start_states, labels)

    return jax.shard_map(run, mesh=split, in_specs=in_specs, out_specs=out_specs, check_vma=False)
```

time: 902 us -> 133 us (0.15); the launches traced: 892 us -> 132 us
  starting transfers between devices: 343 us -> 32.2 us
  local copies, waits for them, and re-layouts: 211 us -> 3.87 us
  waiting for transfers between devices: 238 us -> 35.4 us
  other arithmetic: 96.2 us -> 0 us
  Pallas kernels: 0 us -> 40.5 us
  blocking collectives: 0 us -> 19.9 us
    ppermute x125 -> x11, starting transfers between devices: 343 us -> 28.7 us  [the longest x3 14.2 us: body(): own = lax.ppermute(half, ('y', 'z'), [(i, i + k) for i in range(nt - k)])]
    ppermute x125 -> x11, waiting for transfers between devices: 238 us -> 31 us  [the longest x3 22.2 us: body(): own = lax.ppermute(half, ('y', 'z'), [(i, i + k) for i in range(nt - k)])]
    reshape x10 -> x3, local copies, waits for them, and re-layouts: 142 us -> 2.68 us  [the longest x1 1.51 us: body(): return out.reshape(1, 3, 16, NXB, 256)]
    reduce_sum x5 -> x0, other arithmetic: 62.4 us -> none  [restrict(): return jnp.mean(shaped, axis=(-5, -3, -1))]
    another operation x1 -> x3, local copies, waits for them, and re-layouts: 51.6 us -> 0.55 us  [the longest x2 0.46 us: body(): start_states[0].reshape(3, 256, 2, 128).transpose(0, 2, 1, 3)]
    pallas_call x0 -> x9, Pallas kernels: none -> 40.5 us  [call(): pl.pallas_call(kernel, out_shape=outs, in_specs=specs, out_specs=[VM] * l...]
    add x76 -> x0, other arithmetic: 21.2 us -> none  [the longest x32 7.23 us: coarse_split(): inner + coarse_rate * mobility_inner * laplace_with(inner, widened[:, :,...]
    all_to_all x0 -> x1, blocking collectives: none -> 19.9 us  [body(): got = lax.all_to_all(send.reshape(ny * ns, 5, 8, 128), ('y', 'space'), 0, 0)]
  transfers between devices with their start and end apart: 125 -> 12, of which waited for: 69 -> 10; matrix products, arithmetic and copies ran while one was open for 14% -> 0% of each run, Pallas kernels for 0% -> 1%
where the time goes in v1:
time: 133 us; the launch traced here: 132 us
  Pallas kernels  40.5 us (30%)
  waiting for transfers between devices  35.4 us (27%)
  starting transfers between devices  32.2 us (24%)
  blocking collectives  19.9 us (15%)
  local copies, waits for them, and re-layouts  3.87 us (3%)
    pallas_call x9, Pallas kernels, call(): pl.pallas_call(kernel, out_shape=outs, in_specs=specs, out_specs=[VM] * l...  40.5 us
    ppermute x3, waiting for transfers between devices, body(): own = lax.ppermute(half, ('y', 'z'), [(i, i + k) for i in range(nt - k)])  22.2 us
    all_to_all x1, blocking collectives, body(): got = lax.all_to_all(send.reshape(ny * ns, 5, 8, 128), ('y', 'space'), 0, 0)  19.9 us
    ppermute x3, starting transfers between devices, body(): own = lax.ppermute(half, ('y', 'z'), [(i, i + k) for i in range(nt - k)])  14.2 us
    ppermute x2, starting transfers between devices, exchange(): on = lax.ppermute(inner, 'space', swap)  12.9 us
    all_to_all x1, waiting for transfers between devices, body(): back = lax.all_to_all(chunks, 'space', 0, 0)  4.49 us
    ppermute x3, waiting for transfers between devices, body(): other = lax.ppermute(own, 'space', swap)  4.04 us
    all_to_all x1, starting transfers between devices, body(): back = lax.all_to_all(chunks, 'space', 0, 0)  3.55 us
  transfers between devices with their start and end apart: 12, of which 10 were waited for; matrix products, arithmetic and copies ran while one was open for 0% of the time, Pallas kernels for 1%

profile of v1, /device:TPU:24, one launch (start us, length us, event | category | flops | bytes accessed | tf_op | source)
XLA Modules:
  0.0 132.1 jit_solution(15051663631006735912)
XLA Ops:
  1.8 2.3 %shard_map.28 = (f32[3,16,2,8,256]{4,3,2,1,0:T(8,128)S(1)}, f32[16,2,8,256]{3,2,1,0:T(8,128)S(1)}, f32[43,2,8,256]{3,2,1,0:T(8,128)S(1)}, f32[43,2,8,256]{3,2,1,0:T(8,128)S(1)}) custom-call(s32[8]{0:T(128)S(1)} %stack.41.info, f32[6,256,128]{2,1,0:T(8,128)S(1)} %bitcast.21, s32[2,256,128]{2,1,0:T(8,128)S(1)} %bitcast.24), custom_call_target="tpu_custom_call" | custom-call | flops 1000000 | bytes 3506208 | tf_op jit(solution)/shard_map/pallas_call | solution.py:27
  4.8 2.9 %collective-permute-start.1 = (f32[43,2,8,256]{3,2,1,0:T(8,128)S(1)}, f32[43,2,8,256]{3,2,1,0:T(8,128)S(1)}, u32[]{:S(2)}, u32[]{:S(2)}) collective-permute-start(f32[43,2,8,256]{3,2,1,0:T(8,128)S(1)} %get-tuple-element.29), channel_id=1, source_target_pairs={{0,1},{1,0},{2,3},{3,2},{4,5},{5,4},{6,7},{7,6},{8,9},{9,8},{10,11... | collective-permute-start | bytes 2113544 | tf_op jit(solution)/shard_map/ppermute | solution.py:531
  7.7 1.8 %collective-permute-done.1.on = f32[43,2,8,256]{3,2,1,0:T(8,128)S(1)} collective-permute-done((f32[43,2,8,256]{3,2,1,0:T(8,128)S(1)}, f32[43,2,8,256]{3,2,1,0:T(8,128)S(1)}, u32[]{:S(2)}, u32[]{:S(2)}) %collective-permute-start.1) | collective-permute-done | bytes 704544 | tf_op jit(solution)/shard_map/ppermute | solution.py:531
  9.5 12.8 %shard_map.29 = (f32[3,16,2,8,256]{4,3,2,1,0:T(8,128)S(1)}, f32[36,2,8,256]{3,2,1,0:T(8,128)S(1)}, f32[36,2,8,256]{3,2,1,0:T(8,128)S(1)}, f32[16,2,8,256]{3,2,1,...) custom-call(s32[8]{0:T(128)S(1)} %stack.41.info, ...), custom_call_target="tpu_custom_call" | custom-call | flops 1000000 | bytes 5111840 | tf_op jit(solution)/shard_map/pallas_call | solution.py:27
  23.0 10.0 %collective-permute-start.3 = (f32[10,2,8,256]{3,2,1,0:T(8,128)S(1)}, f32[10,2,8,256]{3,2,1,0:T(8,128)S(1)}, u32[]{:S(2)}, u32[]{:S(2)}) collective-permute-start(f32[10,2,8,256]{3,2,1,0:T(8,128)S(1)} %get-tuple-element.35), channel_id=1, source_target_pairs={{0,1},{1,0},{2,3},{3,2},{4,5},{5,4},{6,7},{7,6},{8,9},{9,8},{10,11... | collective-permute-start | bytes 491528 | tf_op jit(solution)/shard_map/ppermute | solution.py:531
  33.9 8.7 %shard_map.30 = (f32[3,16,2,8,256]{4,3,2,1,0:T(8,128)S(1)}, f32[4,4,2,5,8,128]{5,4,3,2,1,0:T(8,128)S(1)}) custom-call(s32[8]{0:T(128)S(1)} %stack.41.info, f32[3,16,2,8,256]{4,3,2,1,0:T(8,128)S(1)} %get-tuple-element.30.pred, f32[36,2,8,256]{3,2,1,0:T(8,128)S(1)} %get-tuple-element.31.tw, f32[36,2,8,256]{3,2,1,0:T(8,128)S(1)} %get-tuple-element.32.mw, ...), custom_call_target="tpu_custom_call" | custom-call | flops 1000000 | bytes 4096032 | tf_op jit(solution)/shard_map/pallas_call | solution.py:27
  42.6 19.9 %all_to_all.10 = f32[32,5,8,128]{3,2,1,0:T(8,128)S(1)} all-to-all(f32[32,5,8,128]{3,2,1,0:T(8,128)S(1)} %bitcast.25), channel_id=1, replica_groups=mesh['y'=4,'z'=8,'space'=8] {'y','space'}, dimensions={0} | all-to-all | bytes 1310720 | tf_op jit(solution)/shard_map/all_to_all | solution.py:569
  62.8 1.9 %collective-permute-done.4.swapped = f32[4,8,5,8,128]{4,3,2,1,0:T(8,128)S(1)} collective-permute-done((f32[4,8,5,8,128]{4,3,2,1,0:T(8,128)S(1)}, f32[4,8,5,8,128]{4,3,2,1,0:T(8,128)S(1)}, u32[]{:S(2)}, u32[]{:S(2)}) %collective-permute-start.4) | collective-permute-done | bytes 655392 | tf_op jit(solution)/shard_map/ppermute | solution.py:571
  64.6 9.3 %shard_map.32 = (f32[64,8,128]{2,1,0:T(8,128)S(1)}, f32[32,8,128]{2,1,0:T(8,128)S(1)}, f32[64,8,128]{2,1,0:T(8,128)S(1)}, f32[64,8,128]{2,1,0:T(8,128)S(1)}) custom-call(s32[8]{0:T(128)S(1)} %stack.41.info, f32[4,8,5,8,128]{4,3,2,1,0:T(8,128)S(1)} %bitcast.23, f32[4,8,5,8,128]{4,3,2,1,0:T(8,128)S(1)} %collective-permute-done.4.swapped), custom_call_target="tpu_custom_call" | custom-call | flops 1000000 | bytes 2228256 | tf_op jit(solution)/shard_map/pallas_call | solution.py:27
  73.9 3.8 %collective-permute-start.5 = (f32[32,8,128]{2,1,0:T(8,128)S(1)}, f32[32,8,128]{2,1,0:T(8,128)S(1)}, u32[]{:S(2)}, u32[]{:S(2)}) collective-permute-start(f32[32,8,128]{2,1,0:T(8,128)S(1)} %get-tuple-element.40), channel_id=1, source_target_pairs={{0,8},{8,16},{16,24},{24,32},{32,40},{40,48},{48,56},{56,64},{64,7... | collective-permute-start | bytes 393224 | tf_op jit(solution)/shard_map/ppermute | solution.py:580
  77.8 5.8 %collective-permute-done.5.own = f32[32,8,128]{2,1,0:T(8,128)S(1)} collective-permute-done((f32[32,8,128]{2,1,0:T(8,128)S(1)}, f32[32,8,128]{2,1,0:T(8,128)S(1)}, u32[]{:S(2)}, u32[]{:S(2)}) %collective-permute-start.5) | collective-permute-done | bytes 131104 | tf_op jit(solution)/shard_map/ppermute | solution.py:580
  83.6 1.3 %collective-permute-done.6.other = f32[32,8,128]{2,1,0:T(8,128)S(1)} collective-permute-done((f32[32,8,128]{2,1,0:T(8,128)S(1)}, f32[32,8,128]{2,1,0:T(8,128)S(1)}, u32[]{:S(2)}, u32[]{:S(2)}) %collective-permute-start.6) | collective-permute-done | bytes 131104 | tf_op jit(solution)/shard_map/ppermute | solution.py:581
  85.9 3.1 %collective-permute-start.7 = (f32[32,8,128]{2,1,0:T(8,128)S(1)}, f32[32,8,128]{2,1,0:T(8,128)S(1)}, u32[]{:S(2)}, u32[]{:S(2)}) collective-permute-start(f32[32,8,128]{2,1,0:T(8,128)S(1)} %get-tuple-element.44), channel_id=1, source_target_pairs={{0,16},{8,24},{16,32},{24,40},{32,48},{40,56},{48,64},{56,72},{64,... | collective-permute-start | bytes 393224 | tf_op jit(solution)/shard_map/ppermute | solution.py:580
  89.0 9.7 %collective-permute-done.7.own = f32[32,8,128]{2,1,0:T(8,128)S(1)} collective-permute-done((f32[32,8,128]{2,1,0:T(8,128)S(1)}, f32[32,8,128]{2,1,0:T(8,128)S(1)}, u32[]{:S(2)}, u32[]{:S(2)}) %collective-permute-start.7) | collective-permute-done | bytes 131104 | tf_op jit(solution)/shard_map/ppermute | solution.py:580
  98.6 1.3 %collective-permute-done.8.other = f32[32,8,128]{2,1,0:T(8,128)S(1)} collective-permute-done((f32[32,8,128]{2,1,0:T(8,128)S(1)}, f32[32,8,128]{2,1,0:T(8,128)S(1)}, u32[]{:S(2)}, u32[]{:S(2)}) %collective-permute-start.8) | collective-permute-done | bytes 131104 | tf_op jit(solution)/shard_map/ppermute | solution.py:581
  100.0 1.3 %shard_map.34 = (f32[64,8,128]{2,1,0:T(8,128)S(1)}, f32[32,8,128]{2,1,0:T(8,128)S(1)}) custom-call(s32[8]{0:T(128)S(1)} %stack.41.info, f32[64,8,128]{2,1,0:T(8,128)S(1)} %get-tuple-element.43.acc, f32[32,8,128]{2,1,0:T(8,128)S(1)} %collective-permute-done.7.own, f32[32,8,128]{2,1,0:T(8,128)S(1)} %collective-permute-done.8.other, ...), custom_call_target="tpu_custom_call" | custom-call | flops 1000000 | bytes 1441824 | tf_op jit(solution)/shard_map/pallas_call | solution.py:27
  101.3 7.3 %collective-permute-start.9 = (f32[32,8,128]{2,1,0:T(8,128)S(1)}, f32[32,8,128]{2,1,0:T(8,128)S(1)}, u32[]{:S(2)}, u32[]{:S(2)}) collective-permute-start(f32[32,8,128]{2,1,0:T(8,128)S(1)} %get-tuple-element.46), channel_id=1, source_target_pairs={{0,32},{8,40},{16,48},{24,56},{32,64},{40,72},{48,80},{56,88},{64,... | collective-permute-start | bytes 393224 | tf_op jit(solution)/shard_map/ppermute | solution.py:580
  108.6 6.8 %collective-permute-done.9.own = f32[32,8,128]{2,1,0:T(8,128)S(1)} collective-permute-done((f32[32,8,128]{2,1,0:T(8,128)S(1)}, f32[32,8,128]{2,1,0:T(8,128)S(1)}, u32[]{:S(2)}, u32[]{:S(2)}) %collective-permute-start.9) | collective-permute-done | bytes 131104 | tf_op jit(solution)/shard_map/ppermute | solution.py:580
  115.4 1.3 %collective-permute-done.10.other = f32[32,8,128]{2,1,0:T(8,128)S(1)} collective-permute-done((f32[32,8,128]{2,1,0:T(8,128)S(1)}, f32[32,8,128]{2,1,0:T(8,128)S(1)}, u32[]{:S(2)}, u32[]{:S(2)}) %collective-permute-start.10) | collective-permute-done | bytes 131104 | tf_op jit(solution)/shard_map/ppermute | solution.py:581
  116.7 2.7 %shard_map.35 = f32[8,4,8,128]{3,2,1,0:T(8,128)} custom-call(s32[8]{0:T(128)S(1)} %stack.41.info, f32[64,8,128]{2,1,0:T(8,128)S(1)} %get-tuple-element.45.acc, f32[32,8,128]{2,1,0:T(8,128)S(1)} %collective-permute-done.9.own, f32[32,8,128]{2,1,0:T(8,128)S(1)} %collective-permute-done.10.other, f32[64,8,128]{2,1,0:T(8,128)S(1)} %get-tuple-element.41.wa, ...), custom_call_target="tpu_custom_call" | custom-call | flops 1000000 | bytes 1179680 | tf_op jit(solution)/shard_map/pallas_call | solution.py:27
  119.5 3.6 %all-to-all-start.1 = ((f32[8,4,8,128]{3,2,1,0:T(8,128)}), f32[8,4,8,128]{3,2,1,0:T(8,128)S(1)}, u32[]{:S(2)}, u32[]{:S(2)}) async-start(f32[8,4,8,128]{3,2,1,0:T(8,128)} %shard_map.35), calls=%async_computation.1 | async-start | bytes 262144 | tf_op jit(solution)/shard_map/all_to_all | solution.py:590
  123.0 1.3 %shard_map.31.nat = f32[6,256,128]{2,1,0:T(8,128)S(1)} custom-call(f32[3,16,2,8,256]{4,3,2,1,0:T(8,128)S(1)} %get-tuple-element.37.base), custom_call_target="tpu_custom_call" | custom-call | flops 1000000 | bytes 1572864 | tf_op jit(solution)/shard_map/pallas_call | solution.py:27
  124.4 4.5 %all-to-all-done.1 = f32[8,4,8,128]{3,2,1,0:T(8,128)S(1)} async-done(((f32[8,4,8,128]{3,2,1,0:T(8,128)}), f32[8,4,8,128]{3,2,1,0:T(8,128)S(1)}, u32[]{:S(2)}, u32[]{:S(2)}) %all-to-all-start.1) | async-done | bytes 131104 | tf_op jit(solution)/shard_map/all_to_all | solution.py:590
  130.6 1.5 %reshape.27 = f32[1,3,16,16,256]{4,3,2,1,0:T(8,128)} reshape(f32[3,256,2,128]{3,2,1,0:T(2,128)S(1)} %copy.7) | data formatting | bytes 1572864 | tf_op jit(solution)/shard_map/reshape | solution.py:594
  (20 shorter events, 7.0 us)
Async XLA Ops:
  0.0 1.2 copy-start
  4.1 3.6 %collective-permute-start = (f32[43,2,8,256]{3,2,1,0:T(8,128)S(1)}, f32[43,2,8,256]{3,2,1,0:T(8,128)S(1)}, u32[]{:S(2)}, u32[]{:S(2)}) collective-permute-start(f32[43,2,8,256]{3,2,1,0:T(8,128)S(1)} %get-tuple-element.28), channel_id=1, source_target_pairs={{1,2},{3,4},{5,6},{2,1},{4,3},{6,5},{9,10},{11,12},{13,14},{10,9},... | collective-permute-start | bytes 2113544 | tf_op jit(solution)/shard_map/ppermute | solution.py:530
  4.8 4.7 %collective-permute-start.1 = (f32[43,2,8,256]{3,2,1,0:T(8,128)S(1)}, f32[43,2,8,256]{3,2,1,0:T(8,128)S(1)}, u32[]{:S(2)}, u32[]{:S(2)}) collective-permute-start(f32[43,2,8,256]{3,2,1,0:T(8,128)S(1)} %get-tuple-element.29), channel_id=1, source_target_pairs={{0,1},{1,0},{2,3},{3,2},{4,5},{5,4},{6,7},{7,6},{8,9},{9,8},{10,11... | collective-permute-start | bytes 2113544 | tf_op jit(solution)/shard_map/ppermute | solution.py:531
  22.3 10.6 %collective-permute-start.2 = (f32[10,2,8,256]{3,2,1,0:T(8,128)S(1)}, f32[10,2,8,256]{3,2,1,0:T(8,128)S(1)}, u32[]{:S(2)}, u32[]{:S(2)}) collective-permute-start(f32[10,2,8,256]{3,2,1,0:T(8,128)S(1)} %get-tuple-element.34), channel_id=1, source_target_pairs={{1,2},{3,4},{5,6},{2,1},{4,3},{6,5},{9,10},{11,12},{13,14},{10,9},... | collective-permute-start | bytes 491528 | tf_op jit(solution)/shard_map/ppermute | solution.py:530
  23.0 11.0 %collective-permute-start.3 = (f32[10,2,8,256]{3,2,1,0:T(8,128)S(1)}, f32[10,2,8,256]{3,2,1,0:T(8,128)S(1)}, u32[]{:S(2)}, u32[]{:S(2)}) collective-permute-start(f32[10,2,8,256]{3,2,1,0:T(8,128)S(1)} %get-tuple-element.35), channel_id=1, source_target_pairs={{0,1},{1,0},{2,3},{3,2},{4,5},{5,4},{6,7},{7,6},{8,9},{9,8},{10,11... | collective-permute-start | bytes 491528 | tf_op jit(solution)/shard_map/ppermute | solution.py:531
  62.5 2.1 %collective-permute-start.4 = (f32[4,8,5,8,128]{4,3,2,1,0:T(8,128)S(1)}, f32[4,8,5,8,128]{4,3,2,1,0:T(8,128)S(1)}, u32[]{:S(2)}, u32[]{:S(2)}) collective-permute-start(f32[4,8,5,8,128]{4,3,2,1,0:T(8,128)S(1)} %bitcast.22), channel_id=1, source_target_pairs={{0,1},{1,0},{2,3},{3,2},{4,5},{5,4},{6,7},{7,6},{8,9},{9,8},{10,11... | collective-permute-start | bytes 1966088 | tf_op jit(solution)/shard_map/ppermute | solution.py:571
  73.9 9.6 %collective-permute-start.5 = (f32[32,8,128]{2,1,0:T(8,128)S(1)}, f32[32,8,128]{2,1,0:T(8,128)S(1)}, u32[]{:S(2)}, u32[]{:S(2)}) collective-permute-start(f32[32,8,128]{2,1,0:T(8,128)S(1)} %get-tuple-element.40), channel_id=1, source_target_pairs={{0,8},{8,16},{16,24},{24,32},{32,40},{40,48},{48,56},{56,64},{64,7... | collective-permute-start | bytes 393224 | tf_op jit(solution)/shard_map/ppermute | solution.py:580
  83.6 1.3 %collective-permute-start.6 = (f32[32,8,128]{2,1,0:T(8,128)S(1)}, f32[32,8,128]{2,1,0:T(8,128)S(1)}, u32[]{:S(2)}, u32[]{:S(2)}) collective-permute-start(f32[32,8,128]{2,1,0:T(8,128)S(1)} %collective-permute-done.5.own), channel_id=1, source_target_pairs={{0,1},{1,0},{2,3},{3,2},{4,5},{5,4},{6,7},{7,6},{8,9},{9,8},{10,11... | collective-permute-start | bytes 393224 | tf_op jit(solution)/shard_map/ppermute | solution.py:581
  85.9 12.7 %collective-permute-start.7 = (f32[32,8,128]{2,1,0:T(8,128)S(1)}, f32[32,8,128]{2,1,0:T(8,128)S(1)}, u32[]{:S(2)}, u32[]{:S(2)}) collective-permute-start(f32[32,8,128]{2,1,0:T(8,128)S(1)} %get-tuple-element.44), channel_id=1, source_target_pairs={{0,16},{8,24},{16,32},{24,40},{32,48},{40,56},{48,64},{56,72},{64,... | collective-permute-start | bytes 393224 | tf_op jit(solution)/shard_map/ppermute | solution.py:580
  98.6 1.3 %collective-permute-start.8 = (f32[32,8,128]{2,1,0:T(8,128)S(1)}, f32[32,8,128]{2,1,0:T(8,128)S(1)}, u32[]{:S(2)}, u32[]{:S(2)}) collective-permute-start(f32[32,8,128]{2,1,0:T(8,128)S(1)} %collective-permute-done.7.own), channel_id=1, source_target_pairs={{0,1},{1,0},{2,3},{3,2},{4,5},{5,4},{6,7},{7,6},{8,9},{9,8},{10,11... | collective-permute-start | bytes 393224 | tf_op jit(solution)/shard_map/ppermute | solution.py:581
  101.3 14.1 %collective-permute-start.9 = (f32[32,8,128]{2,1,0:T(8,128)S(1)}, f32[32,8,128]{2,1,0:T(8,128)S(1)}, u32[]{:S(2)}, u32[]{:S(2)}) collective-permute-start(f32[32,8,128]{2,1,0:T(8,128)S(1)} %get-tuple-element.46), channel_id=1, source_target_pairs={{0,32},{8,40},{16,48},{24,56},{32,64},{40,72},{48,80},{56,88},{64,... | collective-permute-start | bytes 393224 | tf_op jit(solution)/shard_map/ppermute | solution.py:580
  115.4 1.3 %collective-permute-start.10 = (f32[32,8,128]{2,1,0:T(8,128)S(1)}, f32[32,8,128]{2,1,0:T(8,128)S(1)}, u32[]{:S(2)}, u32[]{:S(2)}) collective-permute-start(f32[32,8,128]{2,1,0:T(8,128)S(1)} %collective-permute-done.9.own), channel_id=1, source_target_pairs={{0,1},{1,0},{2,3},{3,2},{4,5},{5,4},{6,7},{7,6},{8,9},{9,8},{10,11... | collective-permute-start | bytes 393224 | tf_op jit(solution)/shard_map/ppermute | solution.py:581
  119.5 9.4 %all-to-all-start.1 = ((f32[8,4,8,128]{3,2,1,0:T(8,128)}), f32[8,4,8,128]{3,2,1,0:T(8,128)S(1)}, u32[]{:S(2)}, u32[]{:S(2)}) async-start(f32[8,4,8,128]{3,2,1,0:T(8,128)} %shard_map.35), calls=%async_computation.1 | async-start | bytes 262144 | tf_op jit(solution)/shard_map/all_to_all | solution.py:590

commit v2 on v1

--- a/solution.py
+++ b/solution.py
@@ -9,6 +9,7 @@
 HIGH = lax.Precision.HIGHEST
 VM = pl.BlockSpec(memory_space=pltpu.VMEM)
 SM = pl.BlockSpec(memory_space=pltpu.SMEM)
+ANY = pl.BlockSpec(memory_space=pltpu.HBM)
 
 NXB = 16
 HS = 11
@@ -21,8 +22,8 @@
     return jax.ShapeDtypeStruct(dims, F32)
 
 
-def call(kernel, outs, ins, scratch=(), flops=1000000):
-    specs = [SM if a.dtype == jnp.int32 and a.ndim == 1 else VM for a in ins]
+def call(kernel, outs, ins, scratch=(), where=VM):
+    specs = [SM if a.dtype == jnp.int32 and a.ndim == 1 else where for a in ins]
     moved = sum(a.size * 4 for a in ins) + sum(4 * _size(o) for o in outs)
     return pl.pallas_call(
         kernel,
@@ -31,7 +32,7 @@
         out_specs=[VM] * len(outs),
         scratch_shapes=list(scratch),
         compiler_params=pltpu.CompilerParams(vmem_limit_bytes=28 * 1024 * 1024),
-        cost_estimate=pl.CostEstimate(flops=flops, bytes_accessed=moved, transcendentals=0),
+        cost_estimate=pl.CostEstimate(flops=1000000, bytes_accessed=moved, transcendentals=0),
     )(*ins)
 
 
@@ -42,7 +43,12 @@
     return n
 
 
-def loop(lo, hi, fn, unroll=2):
+def loop(lo, hi, fn, unroll=0):
+    unroll = unroll or hi - lo
+    if unroll == hi - lo:
+        for i in range(lo, hi):
+            fn(i)
+        return
     assert (hi - lo) % unroll == 0
 
     def step(t, carry):
@@ -135,34 +141,43 @@
     return jnp.where(c == jnp.where(r < 128, 2 * r, 2 * r - 255), 1.0, 0.0).astype(F32)
 
 
-def rows_of(x, zp):
-    return pl.ds(zp * NXB + x, 8, stride=2 * NXB)
-
-
-def prepare(info, start, labels, s_out, m_out, outer, inner, rows):
+def parity_matrix():
+    r = lax.broadcasted_iota(jnp.int32, (128, 128), 0)
+    c = lax.broadcasted_iota(jnp.int32, (128, 128), 1)
+    return jnp.where(r == jnp.where(c < 64, 2 * c, 2 * c - 127), 1.0, 0.0).astype(F32)
+
+
+def rows_of(x, zp, q):
+    return pl.ds((4 * zp + 2 * (x // 8) + q) * 8 + x % 8, 8, stride=64)
+
+
+def prepare(info, start, labels, s_out, m_out, outer, inner, s_in, l_in, rows, sems):
     core = info[0]
+    copies = [pltpu.make_async_copy(labels, l_in, sems.at[3])]
+    copies += [pltpu.make_async_copy(start.at[c], s_in.at[c], sems.at[c]) for c in range(3)]
+    for copy in copies:
+        copy.start()
     split = split_matrix()
-    for c in range(4):
+    copies[0].wait()
+    for x in range(NXB):
+        for zp in (0, 1):
+            for q in (0, 1):
+                mobility = 1.0 / (1.0 + 3.0 * l_in[rows_of(x, zp, q), :].astype(F32))
+                rows[3, pl.ds((x * 2 + zp) * 8, 8), 128 * q : 128 * q + 128] = mobility
+    done = jnp.dot(rows[3], split, precision=HIGH, preferred_element_type=F32)
+    m_out[...] = done.reshape(NXB, 2, 8, 256)
+    outer[pl.ds(3 * HS, HP)] = m_out[pl.ds((NXB - HP) * core, HP)]
+    inner[pl.ds(3 * HS, HP)] = m_out[pl.ds((NXB - HP) * (1 - core), HP)]
+    for c in range(3):
+        copies[1 + c].wait()
         for x in range(NXB):
             for zp in (0, 1):
-                to = pl.ds((x * 2 + zp) * 8, 8)
                 for q in (0, 1):
-                    cols = slice(128 * q, 128 * q + 128)
-                    if c < 3:
-                        rows[to, cols] = start[c * 2 + q, rows_of(x, zp), :]
-                    else:
-                        rows[to, cols] = 1.0 / (1.0 + 3.0 * labels[q, rows_of(x, zp), :].astype(F32))
-        done = jnp.dot(rows[...], split, precision=HIGH, preferred_element_type=F32)
-        done = done.reshape(NXB, 2, 8, 256)
-        if c < 3:
-            s_out[c] = done
-        else:
-            m_out[...] = done
-    for c in range(3):
+                    rows[c, pl.ds((x * 2 + zp) * 8, 8), 128 * q : 128 * q + 128] = s_in[c, rows_of(x, zp, q), :]
+        done = jnp.dot(rows[c], split, precision=HIGH, preferred_element_type=F32)
+        s_out[c] = done.reshape(NXB, 2, 8, 256)
         outer[pl.ds(c * HS, HS)] = s_out[c, pl.ds((NXB - HS) * core, HS)]
         inner[pl.ds(c * HS, HS)] = s_out[c, pl.ds((NXB - HS) * (1 - core), HS)]
-    outer[pl.ds(3 * HS, HP)] = m_out[pl.ds((NXB - HP) * core, HP)]
-    inner[pl.ds(3 * HS, HP)] = m_out[pl.ds((NXB - HP) * (1 - core), HP)]
 
 
 def interleave(base, nat):
@@ -173,28 +188,30 @@
             for zp in (0, 1):
                 at = (x * 2 + zp) * 8
                 for q in (0, 1):
-                    nat[c * 2 + q, rows_of(x, zp), :] = done[at : at + 8, 128 * q : 128 * q + 128]
+                    cols = slice(128 * q, 128 * q + 128)
+                    nat[c, rows_of(x, zp, q), :] = done[at : at + 8, cols]
 
 
 def finish(nat, w, out):
     r = lax.broadcasted_iota(jnp.int32, (128, 256), 0)
     c = lax.broadcasted_iota(jnp.int32, (128, 256), 1)
-    spread = jnp.where(lax.div(c, 2) == r, 1.0, 0.0).astype(F32)
+    spread = jnp.where(lax.div(c, 2) == jnp.where(r < 64, 2 * r, 2 * r - 127), 1.0, 0.0).astype(F32)
     done = jnp.dot(w[...].reshape(192, 128), spread, precision=HIGH, preferred_element_type=F32)
     for comp in range(3):
         for xc in range(NXB // 2):
             at = (comp * 8 + xc) * 8
             for q in (0, 1):
-                value = done[at : at + 8, 128 * q : 128 * q + 128]
+                cols = slice(128 * q, 128 * q + 128)
+                value = done[at : at + 8, cols]
                 for xp in (0, 1):
                     for zp in (0, 1):
-                        sl = rows_of(2 * xc + xp, zp)
-                        out[comp * 2 + q, sl, :] = nat[comp * 2 + q, sl, :] + value
+                        sl = rows_of(2 * xc + xp, zp, q)
+                        out[comp, sl, :] = nat[comp, sl, :] + value
 
 
 def valid_of(info):
     left, right = info[1].astype(F32), info[2].astype(F32)
-    return lambda i, halo: jnp.where(i < halo, left, jnp.where(i >= halo + NXB, right, 1.0))
+    return lambda i, halo: jnp.where(i < halo, left, jnp.where(i >= halo + NXB, right, jnp.float32(1.0)))
 
 
 def weigh(valid, mw, wt, dg, inv, mc, cw, cinv, fix):
@@ -218,7 +235,7 @@
             put(dg, (i,), zp, yp, total)
             put(inv, (i,), zp, yp, (0.8 * ok) / (total + (1.0 - ok)))
 
-    loop(1, WN - 1, layer)
+    loop(1, WN - 1, layer, 17)
 
     def coarse(j):
         mc[j] = 0.125 * eight(mw, 2 * j)
@@ -253,14 +270,14 @@
     return v, total
 
 
-def smooth(lo, hi, p, q, tw, wt, inv, unroll=2):
+def smooth(lo, hi, p, q, tw, wt, inv):
     def layer(i):
         v, total = gathered(p, i, wt)
         t, n = quad(tw, i), quad(inv, i)
         for zp, yp in QUAD:
             put(q, (i,), zp, yp, 0.2 * v[zp][yp] + n[zp][yp] * (t[zp][yp] + total[zp][yp]))
 
-    loop(lo, hi, layer, unroll)
+    loop(lo, hi, layer, (hi - lo) // 2)
 
 
 def correct(p, tw, wt, dg, lo, ca, cb, cw, cinv):
@@ -276,7 +293,7 @@
         lo[j] = out
         ca[j] = cinv[j] * out
 
-    loop(1, CN - 1, coarse, 1)
+    loop(1, CN - 1, coarse, 8)
 
     def sweep(first, last, a, b):
         def layer(j):
@@ -309,20 +326,23 @@
     loop(4, CN - 4, add)
 
 
-def first_cycle(info, s_own, m_own, off, on, pred, tw, mw, p1, outer, inner, gs, sw, wt, dg, inv, pr, p, mc, cw, cinv, lo, ca, cb, rs, rt):
+def weights(info, m_own, off, on, mw, wt, dg, inv, mc, cw, cinv):
+    core = info[0]
+    mw[pl.ds(HP, NXB)] = m_own[...]
+    mw[pl.ds(core * (HP + NXB), HP)] = off[pl.ds(3 * HS, HP)]
+    mw[pl.ds((1 - core) * (HP + NXB), HP)] = on[pl.ds(3 * HS, HP)]
+    weigh(valid_of(info), mw, wt, dg, inv, mc, cw, cinv, Fix())
+
+
+def first_cycle(info, s_own, off, on, mw, wt, dg, inv, mc, cw, cinv, pred, tw, p1, outer, inner, gs, sw, pr, p, lo, ca, cb, rs, rt):
     fix = Fix()
     core = info[0]
     valid = valid_of(info)
     off_s, on_s = core * (HS + NXB), (1 - core) * (HS + NXB)
-    off_m, on_m = core * (HP + NXB), (1 - core) * (HP + NXB)
     for c in range(3):
         sw[c, pl.ds(HS, NXB)] = s_own[c]
         sw[c, pl.ds(off_s, HS)] = off[pl.ds(c * HS, HS)]
         sw[c, pl.ds(on_s, HS)] = on[pl.ds(c * HS, HS)]
-    mw[pl.ds(HP, NXB)] = m_own[...]
-    mw[pl.ds(off_m, HP)] = off[pl.ds(3 * HS, HP)]
-    mw[pl.ds(on_m, HP)] = on[pl.ds(3 * HS, HP)]
-    weigh(valid, mw, wt, dg, inv, mc, cw, cinv, fix)
 
     def predict(i):
         ok = valid(i, HP)
@@ -338,7 +358,7 @@
                     value = value + (0.4 * m[zp][yp] - 0.2)
                 put(pr, (c, i), zp, yp, ok * value)
 
-    loop(0, WN, predict, 1)
+    loop(0, WN, predict, 6)
 
     def aim(i):
         a, b = quad(pr, 0, i), quad(pr, 2, i)
@@ -352,7 +372,7 @@
             put(tw, (i,), zp, yp, t)
             put(p, (i,), zp, yp, n[zp][yp] * t)
 
-    loop(1, WN - 1, aim)
+    loop(1, WN - 1, aim, 17)
     for c in range(3):
         pred[c] = pr[c, pl.ds(HP, NXB)]
 
@@ -365,7 +385,7 @@
         for zp, yp in QUAD:
             put(p1, (x,), zp, yp, 0.2 * v[zp][yp] + n[zp][yp] * (t[zp][yp] + total[zp][yp]))
 
-    loop(0, NXB, last)
+    loop(0, NXB, last, 8)
     outer[...] = p1[pl.ds((NXB - HP) * core, HP)]
     inner[...] = p1[pl.ds((NXB - HP) * (1 - core), HP)]
 
@@ -375,7 +395,7 @@
         for c in range(3):
             rs[c, q] = 0.125 * eight(sw.at[c], 2 * q + 7)
 
-    loop(0, 12, shrink, 1)
+    loop(0, 12, shrink)
 
     def coarse_step(a, b, scale):
         def layer(q):
@@ -394,18 +414,16 @@
     def to_gs(c, q, value):
         gs[c, q - 2] = value
 
-    loop(1, 11, coarse_step(rs, to_rt, 1.0), 1)
-    loop(2, 10, coarse_step(rt, to_gs, later), 1)
-
-
-def second_cycle(info, pred, tw, mw, p1, off, on, gs, base, send, wt, dg, inv, p, q, mc, cw, cinv, lo, ca, cb):
+    loop(1, 11, coarse_step(rs, to_rt, 1.0))
+    loop(2, 10, coarse_step(rt, to_gs, later))
+
+
+def second_cycle(info, pred, tw, p1, off, on, gs, mw, wt, dg, inv, mc, cw, cinv, base, send, p, q, lo, ca, cb, plain):
     fix = Fix()
     core, row = info[0], info[4]
-    valid = valid_of(info)
     p[pl.ds(HP, NXB)] = p1[...]
     p[pl.ds(core * (HP + NXB), HP)] = off[...]
     p[pl.ds((1 - core) * (HP + NXB), HP)] = on[...]
-    weigh(valid, mw, wt, dg, inv, mc, cw, cinv, fix)
     smooth(1, WN - 1, p, q, tw, wt, inv)
     correct(q, tw, wt, dg, lo, ca, cb, cw, cinv)
     smooth(HP - 1, HP + NXB + 1, q, p, tw, wt, inv)
@@ -430,89 +448,181 @@
         for c, i, zp, yp, e in held:
             put(base, (c, i), zp, yp, e - means[c])
         for c in range(3):
-            r = means[c] - gs[c, j]
+            plain[pl.ds((c * 8 + j) * 8, 8), :] = means[c] - gs[c, j]
+
+    loop(0, NXB // 2, finish_pair, 4)
+    for j in range(NXB // 2):
+        plain[192 + 8 * j : 200 + 8 * j, :] = mc[HP // 2 + j]
+    packed = jnp.dot(plain[...], parity_matrix(), precision=HIGH, preferred_element_type=F32)
+    plain[...] = packed
+    for half in (0, 1):
+        g = plain[pl.ds(192 + 8 * (4 * half + row), 8), :]
+        for chip in range(4):
+            for l in range(4):
+                at = (min(chip, 2) * 8 + 4 * half + l) * 8
+                for to in range(4):
+                    send[to, chip, half, l] = packed[at : at + 8, :]
             for to in range(4):
-                send[to, c, lax.div(j, 4), lax.rem(j, 4)] = r
-                if c == 0:
-                    send[to, 3, lax.div(j, 4), lax.rem(j, 4)] = jnp.zeros_like(r)
-
-    loop(0, NXB // 2, finish_pair, 1)
-    for half in (0, 1):
-        g = mc[HP // 2 + 4 * half + row]
-        for to in range(4):
-            for chip in range(4):
                 send[to, chip, half, 4] = g
 
 
 NC = 64
-
-
-def substep(a, b, wa, wb, fix):
-    for i in range(NC):
-        v = a[i]
-        n = coarse_near(v, fix)
-        total = (n[0] + n[1]) + (n[2] + n[3])
-        if i > 0:
-            total = total + a[i - 1]
-        if i < NC - 1:
-            total = total + a[i + 1]
-        b[i] = wa[i] * v + wb[i] * total
-
-
-def advance(times, a, b, wa, wb, fix):
+PAD = 9
+ROWS = 592
+
+
+def at_layer(i, off=0):
+    return pl.ds(PAD * i + 1 + off, 8)
+
+
+class Pack:
+    def __init__(self):
+        j = iota(1)
+        self.low = j < 64
+        self.not_first = lax.rem(j, 64) > 0
+        self.not_last = lax.rem(j, 64) < 63
+
+    def join(self, one, two):
+        return jnp.where(self.low, one, pltpu.roll(two, 64, 1)), jnp.where(self.low, pltpu.roll(one, 64, 1), two)
+
+
+def substep(a, b, wa, wb, pack, begin):
+    held = {}
+
+    def pair(i):
+        if i not in held:
+            held[i] = (a[at_layer(i), :], a[at_layer(32 + i), :])
+        return held[i]
+
+    def ends(i, keep_low):
+        zero = jnp.zeros((8, 128), F32)
+        out = []
+        for odd in (0, 1):
+            r = pltpu.roll(a[at_layer(32 * odd + i), :], 64, 1)
+            out.append(jnp.where(pack.low, r, zero) if keep_low else jnp.where(pack.low, zero, r))
+        return out
+
+    for n in range(32):
+        i = (begin + n) % 32
+        here = pair(i)
+        down = pair(i - 1) if i > 0 else ends(31, False)
+        up = pair(i + 1) if i < 31 else ends(0, True)
+        sides = (
+            jnp.where(pack.not_first, pltpu.roll(here[1], 1, 1), 0.0),
+            jnp.where(pack.not_last, pltpu.roll(here[0], 127, 1), 0.0),
+        )
+        for odd in (0, 1):
+            at = 32 * odd + i
+            total = (a[at_layer(at, 1), :] + a[at_layer(at, -1), :]) + (up[odd] + down[odd])
+            total = total + (here[1 - odd] + sides[odd])
+            b[at_layer(at), :] = wa[at] * here[odd] + wb[at] * total
+        held.pop(i - 1, None)
+
+
+def advance(times, a, b, wa, wb, pack):
+    each = 2 if times % 2 == 0 else 1
+
     def turn(t, carry):
-        substep(a, b, wa, wb, fix)
-        substep(b, a, wa, wb, fix)
+        for k in range(each):
+            substep(a, b, wa, wb, pack, 4 * k)
+            substep(b, a, wa, wb, pack, 4 * k + 2)
         return carry
 
-    lax.fori_loop(0, times, turn, 0)
-
-
-def rows_scan(info, got, swapped, acc, half, wa, wb, b):
-    fix = Fix()
+    if times == each:
+        turn(0, 0)
+    else:
+        lax.fori_loop(0, times // each, turn, 0)
+
+
+def take_half(half, src, core):
+    for odd in (0, 1):
+        half[16 * odd : 16 * odd + 16] = src[pl.ds(32 * odd + 16 * core, 16)]
+
+
+def rows_scan(info, got, swapped, acc, half, wa, wb, a, b):
+    pack = Pack()
     core, row = info[0], info[4]
-    for s in range(8):
-        for l in range(4):
-            for at, src in ((8 * s + 4 * core + l, got), (8 * s + 4 * (1 - core) + l, swapped)):
-                m = src[l, s, 4]
-                wa[at] = 1.0 - 0.9 * m
-                wb[at] = 0.15 * m
-                acc[at] = src[0, s, l]
+    a[...] = jnp.zeros_like(a)
+    b[...] = jnp.zeros_like(b)
+
+    def each(fn):
+        for s in range(4):
+            for l in range(4):
+                for part, src in ((core, got), (1 - core, swapped)):
+                    fn(s, l, 8 * s + 4 * part + l, src)
+
+    def begin(s, l, at, src):
+        even, odd = pack.join(src[l, s, 4], src[l, s + 4, 4])
+        for base, m in ((0, even), (32, odd)):
+            wa[base + at] = 1.0 - 0.9 * m
+            wb[base + at] = 0.15 * m
+        even, odd = pack.join(src[0, s, l], src[0, s + 4, l])
+        a[at_layer(at), :] = even
+        a[at_layer(32 + at), :] = odd
+
+    each(begin)
     for t in range(1, 4):
 
         @pl.when(t <= row)
         def _():
-            advance(8, acc, b, wa, wb, fix)
-            for s in range(8):
-                for l in range(4):
-                    own, other = 8 * s + 4 * core + l, 8 * s + 4 * (1 - core) + l
-                    acc[own] = acc[own] + got[t, s, l]
-                    acc[other] = acc[other] + swapped[t, s, l]
-
-    half[...] = acc[pl.ds(NC // 2 * core, NC // 2)]
-
-
-def shift_scan(times, last):
-    def kernel(info, acc, own, other, wa, wb, *rest):
-        if last:
-            half, a, b = rest
-            out = a
-        else:
-            out, half, a, b = rest
-        fix = Fix()
-        core = info[0]
-        a[pl.ds(NC // 2 * core, NC // 2)] = own[...]
-        a[pl.ds(NC // 2 * (1 - core), NC // 2)] = other[...]
-        advance(times, a, b, wa, wb, fix)
-        for i in range(NC):
-            out[i] = acc[i] + a[i]
-        if last:
-            for s in range(8):
-                half[s] = out[pl.ds(8 * s + 4 * core, 4)]
-        else:
-            half[...] = out[pl.ds(NC // 2 * core, NC // 2)]
-
-    return kernel
+            advance(8, a, b, wa, wb, pack)
+
+            def include(s, l, at, src):
+                even, odd = pack.join(src[t, s, l], src[t, s + 4, l])
+                a[at_layer(at), :] = a[at_layer(at), :] + even
+                a[at_layer(32 + at), :] = a[at_layer(32 + at), :] + odd
+
+            each(include)
+
+    for i in range(NC):
+        acc[i] = a[at_layer(i), :]
+    take_half(half, acc, core)
+
+
+def load_halves(a, own, other, core, add):
+    for odd in (0, 1):
+        for i in range(16):
+            for part, src in ((core, own), (1 - core, other)):
+                at = at_layer(32 * odd + 16 * part + i)
+                value = src[16 * odd + i]
+                a[at, :] = a[at, :] + value if add else value
+
+
+def one_scan(info, acc, own, other, wa, wb, out, half, a, b):
+    pack = Pack()
+    core = info[0]
+    a[...] = jnp.zeros_like(a)
+    b[...] = jnp.zeros_like(b)
+    load_halves(a, own, other, core, False)
+    advance(1, a, b, wa, wb, pack)
+    for i in range(NC):
+        out[i] = acc[i] + a[at_layer(i), :]
+    take_half(half, out, core)
+
+
+def even_scan(info, acc, own, other, wa, wb, chunk, out, a, b):
+    pack = Pack()
+    core = info[0]
+    a[...] = jnp.zeros_like(a)
+    b[...] = jnp.zeros_like(b)
+    load_halves(a, own.at[2], other.at[2], core, False)
+    advance(2, a, b, wa, wb, pack)
+    load_halves(a, own.at[1], other.at[1], core, True)
+    advance(2, a, b, wa, wb, pack)
+    load_halves(a, own.at[0], other.at[0], core, True)
+    advance(2, a, b, wa, wb, pack)
+    for i in range(NC):
+        out[i] = acc[i] + a[at_layer(i), :]
+    for s in range(4):
+        for l in range(4):
+            at = 8 * s + 4 * core + l
+            one, two = pack.join(out[at], out[32 + at])
+            chunk[s, l] = one
+            chunk[s + 4, l] = two
+
+
+def tiles(a):
+    return a.reshape(-1, 32, 8, 2, 128).transpose(0, 1, 3, 2, 4).reshape(-1, 512, 128)
 
 
 def body(ny, nz, start_states, labels):
@@ -531,40 +641,39 @@
         on = lax.ppermute(inner, "space", swap)
         return off, on
 
-    start = start_states[0].reshape(3, 256, 2, 128).transpose(0, 2, 1, 3).reshape(6, 256, 128)
-    label = labels.reshape(256, 2, 128).transpose(1, 0, 2)
+    start = tiles(start_states.reshape(3, 512, 128))
+    label = tiles(labels.reshape(1, 16 * NXB, 256))[0]
     layer = (2, 8, 256)
-    edge = 3 * HS + HP
     vm = lambda *d: pltpu.VMEM(d, F32)
+    window = shape(WN, *layer)
+    edge = shape(HP, *layer)
+    both = shape(3 * HS + HP, *layer)
     s_own, m_own, outer, inner = call(
         prepare,
-        [shape(3, NXB, *layer), shape(NXB, *layer), shape(edge, *layer), shape(edge, *layer)],
+        [shape(3, NXB, *layer), shape(NXB, *layer), both, both],
         [info, start, label],
-        [vm(256, 256)],
+        [vm(3, 512, 128), pltpu.VMEM((512, 128), jnp.int32), vm(4, 256, 256), pltpu.SemaphoreType.DMA((4,))],
+        ANY,
     )
     off, on = exchange(outer, inner)
-    coarse = [vm(CN, 8, 128), vm(6, CN, 8, 128), vm(CN, 8, 128), vm(CN, 8, 128), vm(CN, 8, 128), vm(CN, 8, 128)]
-    fine = [vm(6, WN, *layer), vm(WN, *layer), vm(WN, *layer)]
-    pred, tw, mw, p1, outer, inner, gs = call(
+    held = call(
+        weights,
+        [window, shape(6, WN, *layer), window, window, shape(CN, 8, 128), shape(6, CN, 8, 128), shape(CN, 8, 128)],
+        [info, m_own, off, on],
+    )
+    coarse = [vm(CN, 8, 128)] * 3
+    pred, tw, p1, outer, inner, gs = call(
         first_cycle,
-        [
-            shape(3, NXB, *layer),
-            shape(WN, *layer),
-            shape(WN, *layer),
-            shape(NXB, *layer),
-            shape(HP, *layer),
-            shape(HP, *layer),
-            shape(3, 8, 8, 128),
-        ],
-        [info, s_own, m_own, off, on],
-        [vm(3, NXB + 2 * HS, *layer)] + fine + [vm(3, WN, *layer), vm(WN, *layer)] + coarse + [vm(3, 12, 8, 128)] * 2,
+        [shape(3, NXB, *layer), window, shape(NXB, *layer), edge, edge, shape(3, 8, 8, 128)],
+        [info, s_own, off, on] + list(held),
+        [vm(3, NXB + 2 * HS, *layer), vm(3, WN, *layer), vm(WN, *layer)] + coarse + [vm(3, 12, 8, 128)] * 2,
     )
     off, on = exchange(outer, inner)
     base, send = call(
         second_cycle,
         [shape(3, NXB, *layer), shape(4, 4, 2, 5, 8, 128)],
-        [info, pred, tw, mw, p1, off, on, gs],
-        fine + [vm(WN, *layer), vm(WN, *layer)] + coarse,
+        [info, pred, tw, p1, off, on, gs] + list(held),
+        [vm(WN, *layer)] * 2 + coarse + [vm(256, 128)],
     )
     got = lax.all_to_all(send.reshape(ny * ns, 5, 8, 128), ("y", "space"), 0, 0)
     got = got.reshape(ny, ns, 5, 8, 128)
@@ -573,24 +682,29 @@
         rows_scan,
         [shape(NC, 8, 128), shape(NC // 2, 8, 128), shape(NC, 8, 128), shape(NC, 8, 128)],
         [info, got, swapped],
-        [vm(NC, 8, 128)],
+        [vm(ROWS, 128)] * 2,
     )
     nt = ny * nz
-    for k in (1, 2, 4):
-        own = lax.ppermute(half, ("y", "z"), [(i, i + k) for i in range(nt - k)])
-        other = lax.ppermute(own, "space", swap)
-        last = k == 4
-        outs = [shape(8, 4, 8, 128)] if last else [shape(NC, 8, 128), shape(NC // 2, 8, 128)]
-        done = call(shift_scan(k, last), outs, [info, acc, own, other, wa, wb], [vm(NC, 8, 128)] * 2)
-        if last:
-            chunks = done[0]
-        else:
-            acc, half = done
-    (nat,) = call(interleave, [shape(6, 256, 128)], [base])
+
+    def shifted(value, k):
+        return lax.ppermute(value, ("y", "z"), [(i, i + k) for i in range(nt - k)])
+
+    own = shifted(half, 1)
+    other = lax.ppermute(own, "space", swap)
+    state = [vm(ROWS, 128)] * 2
+    acc, half = call(
+        one_scan, [shape(NC, 8, 128), shape(NC // 2, 8, 128)], [info, acc, own, other, wa, wb], state
+    )
+    own = jnp.stack([shifted(half, k) for k in (2, 4, 6)])
+    other = lax.ppermute(own, "space", swap)
+    (chunks,) = call(
+        even_scan, [shape(8, 4, 8, 128)], [info, acc, own, other, wa, wb], [vm(NC, 8, 128)] + state
+    )
+    (nat,) = call(interleave, [shape(3, 512, 128)], [base])
     back = lax.all_to_all(chunks, "space", 0, 0)
     w = back[:6].reshape(3, 8, 8, 128)
-    (out,) = call(finish, [shape(6, 256, 128)], [nat, w])
-    out = out.reshape(3, 2, 256, 128).transpose(0, 2, 1, 3)
+    (out,) = call(finish, [shape(3, 512, 128)], [nat, w])
+    out = out.reshape(3, 32, 2, 8, 128).transpose(0, 1, 3, 2, 4)
     return out.reshape(1, 3, 16, NXB, 256)
 
 

time: 133 us -> 112 us (0.84)
  Pallas kernels: 40.5 us -> 25.8 us
  waiting for transfers between devices: 35.4 us -> 29.2 us
  local copies, waits for them, and re-layouts: 3.87 us -> 2.18 us
    pallas_call x9, Pallas kernels: 40.5 us -> 25.8 us  [call(): pl.pallas_call(kernel, out_shape=outs, in_specs=specs, out_specs=[VM] * l...]
    ppermute x3 -> x4, waiting for transfers between devices: 22.2 us -> 16.7 us  [shifted(): return lax.ppermute(value, ('y', 'z'), [(i, i + k) for i in range(nt - k)])]
    reshape x3 -> x0, local copies, waits for them, and re-layouts: 2.68 us -> none  [the longest x1 1.51 us: body(): return out.reshape(1, 3, 16, NXB, 256)]
    unnamed x2 -> x4, local copies, waits for them, and re-layouts: 0.03 us -> 2.09 us
    ppermute x3 -> x2, waiting for transfers between devices: 4.04 us -> 3.05 us  [body(): other = lax.ppermute(own, 'space', swap)]
    ppermute x3 -> x4, starting transfers between devices: 14.2 us -> 15.1 us  [shifted(): return lax.ppermute(value, ('y', 'z'), [(i, i + k) for i in range(nt - k)])]
  transfers between devices with their start and end apart: 12 -> 12, of which waited for: 10 -> 9; matrix products, arithmetic and copies ran while one was open for 0% -> 0% of each run, Pallas kernels for 1% -> 1%
where the time goes in v2:
time: 112 us; the launch traced here: 110 us
  starting transfers between devices  33.2 us (30%)
  waiting for transfers between devices  29.2 us (26%)
  Pallas kernels  25.8 us (23%)
  blocking collectives  19.9 us (18%)
  local copies, waits for them, and re-layouts  2.18 us (2%)
    pallas_call x9, Pallas kernels, call(): pl.pallas_call(kernel, out_shape=outs, in_specs=specs, out_specs=[VM] * l...  25.8 us
    all_to_all x1, blocking collectives, body(): got = lax.all_to_all(send.reshape(ny * ns, 5, 8, 128), ('y', 'space'), 0, 0)  19.9 us
    ppermute x4, waiting for transfers between devices, shifted(): return lax.ppermute(value, ('y', 'z'), [(i, i + k) for i in range(nt - k)])  16.7 us
    ppermute x4, starting transfers between devices, shifted(): return lax.ppermute(value, ('y', 'z'), [(i, i + k) for i in range(nt - k)])  15.1 us
    ppermute x2, starting transfers between devices, exchange(): on = lax.ppermute(inner, 'space', swap)  12.9 us
    all_to_all x1, waiting for transfers between devices, body(): back = lax.all_to_all(chunks, 'space', 0, 0)  4.76 us
    all_to_all x1, starting transfers between devices, body(): back = lax.all_to_all(chunks, 'space', 0, 0)  3.37 us
    ppermute x2, waiting for transfers between devices, body(): other = lax.ppermute(own, 'space', swap)  3.05 us
  transfers between devices with their start and end apart: 12, of which 9 were waited for; matrix products, arithmetic and copies ran while one was open for 0% of the time, Pallas kernels for 1%

profile of v2, /device:TPU:24, one launch (start us, length us, event | category | flops | bytes accessed | tf_op | source)
XLA Modules:
  0.0 110.4 jit_solution(9676857990192374974)
XLA Ops:
  2.2 3.4 %shard_map.28 = (f32[3,16,2,8,256]{4,3,2,1,0:T(8,128)S(1)}, f32[16,2,8,256]{3,2,1,0:T(8,128)S(1)}, f32[43,2,8,256]{3,2,1,0:T(8,128)S(1)}, f32[43,2,8,256]{3,2,1,0:T(8,128)S(1)}) custom-call(s32[8]{0:T(128)S(1)} %stack.53.info, f32[3,512,128]{2,1,0:T(8,128)S(1)} %bitcast.29, s32[512,128]{1,0:T(8,128)S(1)} %bitcast.32), custom_call_target="tpu_custom_call" | custom-call | flops 1000000 | bytes 3506208 | tf_op jit(solution)/shard_map/pallas_call | solution.py:28
  6.3 2.9 %collective-permute-start.1 = (f32[43,2,8,256]{3,2,1,0:T(8,128)S(1)}, f32[43,2,8,256]{3,2,1,0:T(8,128)S(1)}, u32[]{:S(2)}, u32[]{:S(2)}) collective-permute-start(f32[43,2,8,256]{3,2,1,0:T(8,128)S(1)} %get-tuple-element.32), channel_id=1, source_target_pairs={{0,1},{1,0},{2,3},{3,2},{4,5},{5,4},{6,7},{7,6},{8,9},{9,8},{10,11... | collective-permute-start | bytes 2113544 | tf_op jit(solution)/shard_map/ppermute | solution.py:641
  9.2 1.8 %collective-permute-done.1.on = f32[43,2,8,256]{3,2,1,0:T(8,128)S(1)} collective-permute-done((f32[43,2,8,256]{3,2,1,0:T(8,128)S(1)}, f32[43,2,8,256]{3,2,1,0:T(8,128)S(1)}, u32[]{:S(2)}, u32[]{:S(2)}) %collective-permute-start.1) | collective-permute-done | bytes 704544 | tf_op jit(solution)/shard_map/ppermute | solution.py:641
  11.0 1.2 %shard_map.29 = (f32[36,2,8,256]{3,2,1,0:T(8,128)S(1)}, f32[6,36,2,8,256]{4,3,2,1,0:T(8,128)S(1)}, f32[36,2,8,256]{3,2,1,0:T(8,128)S(1)}, f32[36,2,8,256]{3,2,1,...) custom-call(s32[8]{0:T(128)S(1)} %stack.53.info, ...), custom_call_target="tpu_custom_call" | custom-call | flops 1000000 | bytes 7569440 | tf_op jit(solution)/shard_map/pallas_call | solution.py:28
  12.2 3.3 %shard_map.30 = (f32[3,16,2,8,256]{4,3,2,1,0:T(8,128)S(1)}, f32[36,2,8,256]{3,2,1,0:T(8,128)S(1)}, f32[16,2,8,256]{3,2,1,0:T(8,128)S(1)}, f32[10,2,8,256]{3,2,1,...) custom-call(s32[8]{0:T(128)S(1)} %stack.53.info, ...), custom_call_target="tpu_custom_call" | custom-call | flops 1000000 | bytes 10158112 | tf_op jit(solution)/shard_map/pallas_call | solution.py:28
  16.2 10.0 %collective-permute-start.3 = (f32[10,2,8,256]{3,2,1,0:T(8,128)S(1)}, f32[10,2,8,256]{3,2,1,0:T(8,128)S(1)}, u32[]{:S(2)}, u32[]{:S(2)}) collective-permute-start(f32[10,2,8,256]{3,2,1,0:T(8,128)S(1)} %get-tuple-element.45), channel_id=1, source_target_pairs={{0,1},{1,0},{2,3},{3,2},{4,5},{5,4},{6,7},{7,6},{8,9},{9,8},{10,11... | collective-permute-start | bytes 491528 | tf_op jit(solution)/shard_map/ppermute | solution.py:641
  27.2 2.8 %shard_map.31 = (f32[3,16,2,8,256]{4,3,2,1,0:T(8,128)S(1)}, f32[4,4,2,5,8,128]{5,4,3,2,1,0:T(8,128)S(1)}) custom-call(s32[8]{0:T(128)S(1)} %stack.53.info, f32[3,16,2,8,256]{4,3,2,1,0:T(8,128)S(1)} %get-tuple-element.41.pred, f32[36,2,8,256]{3,2,1,0:T(8,128)S(1)} %get-tuple-element.42.tw, f32[16,2,8,256]{3,2,1,0:T(8,128)S(1)} %get-tuple-element.43.p1, ...), custom_call_target="tpu_custom_call" | custom-call | flops 1000000 | bytes 9404448 | tf_op jit(solution)/shard_map/pallas_call | solution.py:28
  30.0 19.9 %all_to_all.10 = f32[32,5,8,128]{3,2,1,0:T(8,128)S(1)} all-to-all(f32[32,5,8,128]{3,2,1,0:T(8,128)S(1)} %bitcast.30), channel_id=1, replica_groups=mesh['y'=4,'z'=8,'space'=8] {'y','space'}, dimensions={0} | all-to-all | bytes 1310720 | tf_op jit(solution)/shard_map/all_to_all | solution.py:678
  50.2 1.9 %collective-permute-done.4.swapped = f32[4,8,5,8,128]{4,3,2,1,0:T(8,128)S(1)} collective-permute-done((f32[4,8,5,8,128]{4,3,2,1,0:T(8,128)S(1)}, f32[4,8,5,8,128]{4,3,2,1,0:T(8,128)S(1)}, u32[]{:S(2)}, u32[]{:S(2)}) %collective-permute-start.4) | collective-permute-done | bytes 655392 | tf_op jit(solution)/shard_map/ppermute | solution.py:680
  52.0 7.5 %shard_map.33 = (f32[64,8,128]{2,1,0:T(8,128)S(1)}, f32[32,8,128]{2,1,0:T(8,128)S(1)}, f32[64,8,128]{2,1,0:T(8,128)S(1)}, f32[64,8,128]{2,1,0:T(8,128)S(1)}) custom-call(s32[8]{0:T(128)S(1)} %stack.53.info, f32[4,8,5,8,128]{4,3,2,1,0:T(8,128)S(1)} %bitcast.28, f32[4,8,5,8,128]{4,3,2,1,0:T(8,128)S(1)} %collective-permute-done.4.swapped), custom_call_target="tpu_custom_call" | custom-call | flops 1000000 | bytes 2228256 | tf_op jit(solution)/shard_map/pallas_call | solution.py:28
  59.6 3.8 %collective-permute-start.5 = (f32[32,8,128]{2,1,0:T(8,128)S(1)}, f32[32,8,128]{2,1,0:T(8,128)S(1)}, u32[]{:S(2)}, u32[]{:S(2)}) collective-permute-start(f32[32,8,128]{2,1,0:T(8,128)S(1)} %get-tuple-element.50), channel_id=1, source_target_pairs={{0,8},{8,16},{16,24},{24,32},{32,40},{40,48},{48,56},{56,64},{64,7... | collective-permute-start | bytes 393224 | tf_op jit(solution)/shard_map/ppermute | solution.py:690
  63.4 6.2 %collective-permute-done.5.own = f32[32,8,128]{2,1,0:T(8,128)S(1)} collective-permute-done((f32[32,8,128]{2,1,0:T(8,128)S(1)}, f32[32,8,128]{2,1,0:T(8,128)S(1)}, u32[]{:S(2)}, u32[]{:S(2)}) %collective-permute-start.5) | collective-permute-done | bytes 131104 | tf_op jit(solution)/shard_map/ppermute | solution.py:690
  69.6 1.3 %collective-permute-done.6.other = f32[32,8,128]{2,1,0:T(8,128)S(1)} collective-permute-done((f32[32,8,128]{2,1,0:T(8,128)S(1)}, f32[32,8,128]{2,1,0:T(8,128)S(1)}, u32[]{:S(2)}, u32[]{:S(2)}) %collective-permute-start.6) | collective-permute-done | bytes 131104 | tf_op jit(solution)/shard_map/ppermute | solution.py:693
  71.8 5.7 %collective-permute-start.9 = (f32[32,8,128]{2,1,0:T(8,128)S(1)}, f32[32,8,128]{2,1,0:T(8,128)S(1)}, u32[]{:S(2)}, u32[]{:S(2)}) collective-permute-start(f32[32,8,128]{2,1,0:T(8,128)S(1)} %get-tuple-element.54), channel_id=1, source_target_pairs={{0,48},{8,56},{16,64},{24,72},{32,80},{40,88},{48,96},{56,104},{64... | collective-permute-start | bytes 393224 | tf_op jit(solution)/shard_map/ppermute | solution.py:690
  77.6 3.4 %collective-permute-start.8 = (f32[32,8,128]{2,1,0:T(8,128)S(1)}, f32[32,8,128]{2,1,0:T(8,128)S(1)}, u32[]{:S(2)}, u32[]{:S(2)}) collective-permute-start(f32[32,8,128]{2,1,0:T(8,128)S(1)} %get-tuple-element.54), channel_id=1, source_target_pairs={{0,32},{8,40},{16,48},{24,56},{32,64},{40,72},{48,80},{56,88},{64,... | collective-permute-start | bytes 393224 | tf_op jit(solution)/shard_map/ppermute | solution.py:690
  81.0 2.2 %collective-permute-start.7 = (f32[32,8,128]{2,1,0:T(8,128)S(1)}, f32[32,8,128]{2,1,0:T(8,128)S(1)}, u32[]{:S(2)}, u32[]{:S(2)}) collective-permute-start(f32[32,8,128]{2,1,0:T(8,128)S(1)} %get-tuple-element.54), channel_id=1, source_target_pairs={{0,16},{8,24},{16,32},{24,40},{32,48},{40,56},{48,64},{56,72},{64,... | collective-permute-start | bytes 393224 | tf_op jit(solution)/shard_map/ppermute | solution.py:690
  83.2 5.9 %collective-permute-done.9 = f32[32,8,128]{2,1,0:T(8,128)S(1)} collective-permute-done((f32[32,8,128]{2,1,0:T(8,128)S(1)}, f32[32,8,128]{2,1,0:T(8,128)S(1)}, u32[]{:S(2)}, u32[]{:S(2)}) %collective-permute-start.9) | collective-permute-done | bytes 131104 | tf_op jit(solution)/shard_map/ppermute | solution.py:690
  89.1 4.6 %collective-permute-done.8 = f32[32,8,128]{2,1,0:T(8,128)S(1)} collective-permute-done((f32[32,8,128]{2,1,0:T(8,128)S(1)}, f32[32,8,128]{2,1,0:T(8,128)S(1)}, u32[]{:S(2)}, u32[]{:S(2)}) %collective-permute-start.8) | collective-permute-done | bytes 131104 | tf_op jit(solution)/shard_map/ppermute | solution.py:690
  94.0 1.7 %collective-permute-done.10.other = f32[3,32,8,128]{3,2,1,0:T(8,128)S(1)} collective-permute-done((f32[3,32,8,128]{3,2,1,0:T(8,128)S(1)}, f32[3,32,8,128]{3,2,1,0:T(8,128)S(1)}, u32[]{:S(2)}, u32[]{:S(2)}) %collective-permute-start.10) | collective-permute-done | bytes 393248 | tf_op jit(solution)/shard_map/ppermute | solution.py:699
  95.7 3.3 %shard_map.35 = f32[8,4,8,128]{3,2,1,0:T(8,128)} custom-call(s32[8]{0:T(128)S(1)} %stack.53.info, f32[64,8,128]{2,1,0:T(8,128)S(1)} %get-tuple-element.53.acc, f32[3,32,8,128]{3,2,1,0:T(8,128)S(1)} %pad_maximum_fusion.own, f32[3,32,8,128]{3,2,1,0:T(8,128)S(1)} %collective-permute-done.10.other, f32[64,8,128]{2,1,0:T(8,128)S(1)} %get-tuple-element.51.wa, ...), custom_call_target="tpu_custom_call" | custom-call | flops 1000000 | bytes 1703968 | tf_op jit(solution)/shard_map/pallas_call | solution.py:28
  99.0 3.4 %all-to-all-start.1 = ((f32[8,4,8,128]{3,2,1,0:T(8,128)}), f32[8,4,8,128]{3,2,1,0:T(8,128)S(1)}, u32[]{:S(2)}, u32[]{:S(2)}) async-start(f32[8,4,8,128]{3,2,1,0:T(8,128)} %shard_map.35), calls=%async_computation.1 | async-start | bytes 262144 | tf_op jit(solution)/shard_map/all_to_all | solution.py:704
  102.3 1.3 %shard_map.32.nat = f32[3,512,128]{2,1,0:T(8,128)S(1)} custom-call(f32[3,16,2,8,256]{4,3,2,1,0:T(8,128)S(1)} %get-tuple-element.47.base), custom_call_target="tpu_custom_call" | custom-call | flops 1000000 | bytes 1572864 | tf_op jit(solution)/shard_map/pallas_call | solution.py:28
  103.6 4.8 %all-to-all-done.1 = f32[8,4,8,128]{3,2,1,0:T(8,128)S(1)} async-done(((f32[8,4,8,128]{3,2,1,0:T(8,128)}), f32[8,4,8,128]{3,2,1,0:T(8,128)S(1)}, u32[]{:S(2)}, u32[]{:S(2)}) %all-to-all-start.1) | async-done | bytes 131104 | tf_op jit(solution)/shard_map/all_to_all | solution.py:704
  108.4 2.0 %shard_map.36 = f32[3,512,128]{2,1,0:T(8,128)} custom-call(f32[3,512,128]{2,1,0:T(8,128)S(1)} %shard_map.32.nat, f32[3,8,8,128]{3,2,1,0:T(8,128)S(1)} %bitcast.31), custom_call_target="tpu_custom_call" | custom-call | flops 1000000 | bytes 1671168 | tf_op jit(solution)/shard_map/pallas_call | solution.py:28
  (17 shorter events, 6.0 us)
Async XLA Ops:
  0.1 1.1 %copy-start = (f32[1,3,16,16,256]{4,3,2,1,0:T(8,128)S(1)}, f32[1,3,16,16,256]{4,3,2,1,0:T(8,128)}, u32[]{:S(2)}) copy-start(f32[1,3,16,16,256]{4,3,2,1,0:T(8,128)} %param.2) | copy-start | bytes 2359300
  1.2 0.9 copy-start.1
  5.6 3.6 %collective-permute-start = (f32[43,2,8,256]{3,2,1,0:T(8,128)S(1)}, f32[43,2,8,256]{3,2,1,0:T(8,128)S(1)}, u32[]{:S(2)}, u32[]{:S(2)}) collective-permute-start(f32[43,2,8,256]{3,2,1,0:T(8,128)S(1)} %get-tuple-element.31), channel_id=1, source_target_pairs={{1,2},{3,4},{5,6},{2,1},{4,3},{6,5},{9,10},{11,12},{13,14},{10,9},... | collective-permute-start | bytes 2113544 | tf_op jit(solution)/shard_map/ppermute | solution.py:640
  6.3 4.7 %collective-permute-start.1 = (f32[43,2,8,256]{3,2,1,0:T(8,128)S(1)}, f32[43,2,8,256]{3,2,1,0:T(8,128)S(1)}, u32[]{:S(2)}, u32[]{:S(2)}) collective-permute-start(f32[43,2,8,256]{3,2,1,0:T(8,128)S(1)} %get-tuple-element.32), channel_id=1, source_target_pairs={{0,1},{1,0},{2,3},{3,2},{4,5},{5,4},{6,7},{7,6},{8,9},{9,8},{10,11... | collective-permute-start | bytes 2113544 | tf_op jit(solution)/shard_map/ppermute | solution.py:641
  15.5 10.6 %collective-permute-start.2 = (f32[10,2,8,256]{3,2,1,0:T(8,128)S(1)}, f32[10,2,8,256]{3,2,1,0:T(8,128)S(1)}, u32[]{:S(2)}, u32[]{:S(2)}) collective-permute-start(f32[10,2,8,256]{3,2,1,0:T(8,128)S(1)} %get-tuple-element.44), channel_id=1, source_target_pairs={{1,2},{3,4},{5,6},{2,1},{4,3},{6,5},{9,10},{11,12},{13,14},{10,9},... | collective-permute-start | bytes 491528 | tf_op jit(solution)/shard_map/ppermute | solution.py:640
  16.2 11.0 %collective-permute-start.3 = (f32[10,2,8,256]{3,2,1,0:T(8,128)S(1)}, f32[10,2,8,256]{3,2,1,0:T(8,128)S(1)}, u32[]{:S(2)}, u32[]{:S(2)}) collective-permute-start(f32[10,2,8,256]{3,2,1,0:T(8,128)S(1)} %get-tuple-element.45), channel_id=1, source_target_pairs={{0,1},{1,0},{2,3},{3,2},{4,5},{5,4},{6,7},{7,6},{8,9},{9,8},{10,11... | collective-permute-start | bytes 491528 | tf_op jit(solution)/shard_map/ppermute | solution.py:641
  49.9 2.1 %collective-permute-start.4 = (f32[4,8,5,8,128]{4,3,2,1,0:T(8,128)S(1)}, f32[4,8,5,8,128]{4,3,2,1,0:T(8,128)S(1)}, u32[]{:S(2)}, u32[]{:S(2)}) collective-permute-start(f32[4,8,5,8,128]{4,3,2,1,0:T(8,128)S(1)} %bitcast.27), channel_id=1, source_target_pairs={{0,1},{1,0},{2,3},{3,2},{4,5},{5,4},{6,7},{7,6},{8,9},{9,8},{10,11... | collective-permute-start | bytes 1966088 | tf_op jit(solution)/shard_map/ppermute | solution.py:680
  59.6 10.0 %collective-permute-start.5 = (f32[32,8,128]{2,1,0:T(8,128)S(1)}, f32[32,8,128]{2,1,0:T(8,128)S(1)}, u32[]{:S(2)}, u32[]{:S(2)}) collective-permute-start(f32[32,8,128]{2,1,0:T(8,128)S(1)} %get-tuple-element.50), channel_id=1, source_target_pairs={{0,8},{8,16},{16,24},{24,32},{32,40},{40,48},{48,56},{56,64},{64,7... | collective-permute-start | bytes 393224 | tf_op jit(solution)/shard_map/ppermute | solution.py:690
  69.6 1.3 %collective-permute-start.6 = (f32[32,8,128]{2,1,0:T(8,128)S(1)}, f32[32,8,128]{2,1,0:T(8,128)S(1)}, u32[]{:S(2)}, u32[]{:S(2)}) collective-permute-start(f32[32,8,128]{2,1,0:T(8,128)S(1)} %collective-permute-done.5.own), channel_id=1, source_target_pairs={{0,1},{1,0},{2,3},{3,2},{4,5},{5,4},{6,7},{7,6},{8,9},{9,8},{10,11... | collective-permute-start | bytes 393224 | tf_op jit(solution)/shard_map/ppermute | solution.py:693
  71.8 17.2 %collective-permute-start.9 = (f32[32,8,128]{2,1,0:T(8,128)S(1)}, f32[32,8,128]{2,1,0:T(8,128)S(1)}, u32[]{:S(2)}, u32[]{:S(2)}) collective-permute-start(f32[32,8,128]{2,1,0:T(8,128)S(1)} %get-tuple-element.54), channel_id=1, source_target_pairs={{0,48},{8,56},{16,64},{24,72},{32,80},{40,88},{48,96},{56,104},{64... | collective-permute-start | bytes 393224 | tf_op jit(solution)/shard_map/ppermute | solution.py:690
  77.6 16.1 %collective-permute-start.8 = (f32[32,8,128]{2,1,0:T(8,128)S(1)}, f32[32,8,128]{2,1,0:T(8,128)S(1)}, u32[]{:S(2)}, u32[]{:S(2)}) collective-permute-start(f32[32,8,128]{2,1,0:T(8,128)S(1)} %get-tuple-element.54), channel_id=1, source_target_pairs={{0,32},{8,40},{16,48},{24,56},{32,64},{40,72},{48,80},{56,88},{64,... | collective-permute-start | bytes 393224 | tf_op jit(solution)/shard_map/ppermute | solution.py:690
  81.0 12.7 %collective-permute-start.7 = (f32[32,8,128]{2,1,0:T(8,128)S(1)}, f32[32,8,128]{2,1,0:T(8,128)S(1)}, u32[]{:S(2)}, u32[]{:S(2)}) collective-permute-start(f32[32,8,128]{2,1,0:T(8,128)S(1)} %get-tuple-element.54), channel_id=1, source_target_pairs={{0,16},{8,24},{16,32},{24,40},{32,48},{40,56},{48,64},{56,72},{64,... | collective-permute-start | bytes 393224 | tf_op jit(solution)/shard_map/ppermute | solution.py:690
  93.7 2.0 %collective-permute-start.10 = (f32[3,32,8,128]{3,2,1,0:T(8,128)S(1)}, f32[3,32,8,128]{3,2,1,0:T(8,128)S(1)}, u32[]{:S(2)}, u32[]{:S(2)}) collective-permute-start(f32[3,32,8,128]{3,2,1,0:T(8,128)S(1)} %pad_maximum_fusion.own), channel_id=1, source_target_pairs={{0,1},{1,0},{2,3},{3,2},{4,5},{5,4},{6,7},{7,6},{8,9},{9,8},{10,11... | collective-permute-start | bytes 1179656 | tf_op jit(solution)/shard_map/ppermute | solution.py:699
  99.0 9.4 %all-to-all-start.1 = ((f32[8,4,8,128]{3,2,1,0:T(8,128)}), f32[8,4,8,128]{3,2,1,0:T(8,128)S(1)}, u32[]{:S(2)}, u32[]{:S(2)}) async-start(f32[8,4,8,128]{3,2,1,0:T(8,128)} %shard_map.35), calls=%async_computation.1 | async-start | bytes 262144 | tf_op jit(solution)/shard_map/all_to_all | solution.py:704

commit v3 on v2

--- a/solution.py
+++ b/solution.py
@@ -6,7 +6,6 @@
 from jax.sharding import Mesh, PartitionSpec as P
 
 F32 = jnp.float32
-HIGH = lax.Precision.HIGHEST
 VM = pl.BlockSpec(memory_space=pltpu.VMEM)
 SM = pl.BlockSpec(memory_space=pltpu.SMEM)
 ANY = pl.BlockSpec(memory_space=pltpu.HBM)
@@ -22,15 +21,16 @@
     return jax.ShapeDtypeStruct(dims, F32)
 
 
-def call(kernel, outs, ins, scratch=(), where=VM):
+def call(kernel, outs, ins, scratch=(), where=VM, to=VM, aliases={}):
     specs = [SM if a.dtype == jnp.int32 and a.ndim == 1 else where for a in ins]
     moved = sum(a.size * 4 for a in ins) + sum(4 * _size(o) for o in outs)
     return pl.pallas_call(
         kernel,
         out_shape=outs,
         in_specs=specs,
-        out_specs=[VM] * len(outs),
+        out_specs=[to] * len(outs),
         scratch_shapes=list(scratch),
+        input_output_aliases=aliases,
         compiler_params=pltpu.CompilerParams(vmem_limit_bytes=28 * 1024 * 1024),
         cost_estimate=pl.CostEstimate(flops=1000000, bytes_accessed=moved, transcendentals=0),
     )(*ins)
@@ -129,22 +129,31 @@
     return total
 
 
+def exact_dot(x, chooser):
+    one = x.astype(jnp.bfloat16)
+    rest = x - one.astype(F32)
+    two = rest.astype(jnp.bfloat16)
+    three = (rest - two.astype(F32)).astype(jnp.bfloat16)
+    dot = lambda part: jnp.dot(part, chooser, preferred_element_type=F32)
+    return (dot(three) + dot(two)) + dot(one)
+
+
 def split_matrix():
     r = lax.broadcasted_iota(jnp.int32, (256, 256), 0)
     c = lax.broadcasted_iota(jnp.int32, (256, 256), 1)
-    return jnp.where(r == jnp.where(c < 128, 2 * c, 2 * c - 255), 1.0, 0.0).astype(F32)
+    return jnp.where(r == jnp.where(c < 128, 2 * c, 2 * c - 255), 1.0, 0.0).astype(jnp.bfloat16)
 
 
 def join_matrix():
     r = lax.broadcasted_iota(jnp.int32, (256, 256), 0)
     c = lax.broadcasted_iota(jnp.int32, (256, 256), 1)
-    return jnp.where(c == jnp.where(r < 128, 2 * r, 2 * r - 255), 1.0, 0.0).astype(F32)
+    return jnp.where(c == jnp.where(r < 128, 2 * r, 2 * r - 255), 1.0, 0.0).astype(jnp.bfloat16)
 
 
 def parity_matrix():
     r = lax.broadcasted_iota(jnp.int32, (128, 128), 0)
     c = lax.broadcasted_iota(jnp.int32, (128, 128), 1)
-    return jnp.where(r == jnp.where(c < 64, 2 * c, 2 * c - 127), 1.0, 0.0).astype(F32)
+    return jnp.where(r == jnp.where(c < 64, 2 * c, 2 * c - 127), 1.0, 0.0).astype(jnp.bfloat16)
 
 
 def rows_of(x, zp, q):
@@ -164,7 +173,7 @@
             for q in (0, 1):
                 mobility = 1.0 / (1.0 + 3.0 * l_in[rows_of(x, zp, q), :].astype(F32))
                 rows[3, pl.ds((x * 2 + zp) * 8, 8), 128 * q : 128 * q + 128] = mobility
-    done = jnp.dot(rows[3], split, precision=HIGH, preferred_element_type=F32)
+    done = jnp.dot(rows[3].astype(jnp.bfloat16), split, preferred_element_type=F32)
     m_out[...] = done.reshape(NXB, 2, 8, 256)
     outer[pl.ds(3 * HS, HP)] = m_out[pl.ds((NXB - HP) * core, HP)]
     inner[pl.ds(3 * HS, HP)] = m_out[pl.ds((NXB - HP) * (1 - core), HP)]
@@ -174,7 +183,7 @@
             for zp in (0, 1):
                 for q in (0, 1):
                     rows[c, pl.ds((x * 2 + zp) * 8, 8), 128 * q : 128 * q + 128] = s_in[c, rows_of(x, zp, q), :]
-        done = jnp.dot(rows[c], split, precision=HIGH, preferred_element_type=F32)
+        done = exact_dot(rows[c], split)
         s_out[c] = done.reshape(NXB, 2, 8, 256)
         outer[pl.ds(c * HS, HS)] = s_out[c, pl.ds((NXB - HS) * core, HS)]
         inner[pl.ds(c * HS, HS)] = s_out[c, pl.ds((NXB - HS) * (1 - core), HS)]
@@ -183,7 +192,7 @@
 def interleave(base, nat):
     join = join_matrix()
     for c in range(3):
-        done = jnp.dot(base[c].reshape(256, 256), join, precision=HIGH, preferred_element_type=F32)
+        done = exact_dot(base[c].reshape(256, 256), join)
         for x in range(NXB):
             for zp in (0, 1):
                 at = (x * 2 + zp) * 8
@@ -192,11 +201,12 @@
                     nat[c, rows_of(x, zp, q), :] = done[at : at + 8, cols]
 
 
-def finish(nat, w, out):
+def finish(nat, w, out, made, sems):
     r = lax.broadcasted_iota(jnp.int32, (128, 256), 0)
     c = lax.broadcasted_iota(jnp.int32, (128, 256), 1)
-    spread = jnp.where(lax.div(c, 2) == jnp.where(r < 64, 2 * r, 2 * r - 127), 1.0, 0.0).astype(F32)
-    done = jnp.dot(w[...].reshape(192, 128), spread, precision=HIGH, preferred_element_type=F32)
+    spread = jnp.where(lax.div(c, 2) == jnp.where(r < 64, 2 * r, 2 * r - 127), 1.0, 0.0).astype(jnp.bfloat16)
+    done = exact_dot(w[...].reshape(192, 128), spread)
+    copies = []
     for comp in range(3):
         for xc in range(NXB // 2):
             at = (comp * 8 + xc) * 8
@@ -206,7 +216,11 @@
                 for xp in (0, 1):
                     for zp in (0, 1):
                         sl = rows_of(2 * xc + xp, zp, q)
-                        out[comp, sl, :] = nat[comp, sl, :] + value
+                        made[comp, sl, :] = nat[comp, sl, :] + value
+        copies.append(pltpu.make_async_copy(made.at[comp], out.at[comp], sems.at[comp]))
+        copies[-1].start()
+    for copy in copies:
+        copy.wait()
 
 
 def valid_of(info):
@@ -214,7 +228,7 @@
     return lambda i, halo: jnp.where(i < halo, left, jnp.where(i >= halo + NXB, right, jnp.float32(1.0)))
 
 
-def weigh(valid, mw, wt, dg, inv, mc, cw, cinv, fix):
+def weigh(valid, mw, wt, dg, inv, mc, cw, cinv, fix, inside):
     def layer(i):
         m = quad(mw, i)
         sides = near(m, fix) + (quad(mw, i + 1), quad(mw, i - 1))
@@ -235,12 +249,19 @@
             put(dg, (i,), zp, yp, total)
             put(inv, (i,), zp, yp, (0.8 * ok) / (total + (1.0 - ok)))
 
-    loop(1, WN - 1, layer, 17)
+    if inside:
+        loop(HP + 1, HP + NXB - 1, layer, 7)
+    else:
+        loop(1, HP + 1, layer)
+        loop(HP + NXB - 1, WN - 1, layer)
 
     def coarse(j):
         mc[j] = 0.125 * eight(mw, 2 * j)
 
-    loop(0, CN, coarse)
+    mine = range(HP // 2, HP // 2 + NXB // 2)
+    for j in range(CN):
+        if (j in mine) == inside:
+            coarse(j)
 
     def coarse_layer(j):
         m = mc[j]
@@ -256,7 +277,28 @@
             cw[f, j] = faces[f]
         cinv[j] = (0.8 * ok) / (total + (1.0 - ok))
 
-    loop(1, CN - 1, coarse_layer)
+    mine = range(HP // 2 + 1, HP // 2 + NXB // 2 - 1)
+    for j in range(1, CN - 1):
+        if (j in mine) == inside:
+            coarse_layer(j)
+
+
+def predicting(valid, mw, sw, at, pr, fix):
+    def predict(i):
+        ok = valid(i, HP)
+        m = quad(mw, i)
+        for c in range(3):
+            v = quad(sw, c, i + 1 - at)
+            sides = near(v, fix) + (quad(sw, c, i + 2 - at), quad(sw, c, i - at))
+            for zp, yp in QUAD:
+                n = [s[zp][yp] for s in sides]
+                total = ((n[0] + n[1]) + (n[2] + n[3])) + (n[4] + n[5])
+                value = 0.4 * v[zp][yp] + 0.1 * total
+                if c == 0:
+                    value = value + (0.4 * m[zp][yp] - 0.2)
+                put(pr, (c, i), zp, yp, ok * value)
+
+    return predict
 
 
 def gathered(p, i, wt):
@@ -326,15 +368,16 @@
     loop(4, CN - 4, add)
 
 
-def weights(info, m_own, off, on, mw, wt, dg, inv, mc, cw, cinv):
-    core = info[0]
+def inside(info, s_own, m_own, mw, wt, dg, inv, mc, cw, cinv, pr):
+    fix = Fix()
+    valid = valid_of(info)
     mw[pl.ds(HP, NXB)] = m_own[...]
-    mw[pl.ds(core * (HP + NXB), HP)] = off[pl.ds(3 * HS, HP)]
-    mw[pl.ds((1 - core) * (HP + NXB), HP)] = on[pl.ds(3 * HS, HP)]
-    weigh(valid_of(info), mw, wt, dg, inv, mc, cw, cinv, Fix())
-
-
-def first_cycle(info, s_own, off, on, mw, wt, dg, inv, mc, cw, cinv, pred, tw, p1, outer, inner, gs, sw, pr, p, lo, ca, cb, rs, rt):
+    weigh(valid, mw, wt, dg, inv, mc, cw, cinv, fix, True)
+    loop(HP + 1, HP + NXB - 1, predicting(valid, mw, s_own, HS, pr, fix), 7)
+
+
+def first_cycle(info, s_own, off, on, *refs):
+    mw, wt, dg, inv, mc, cw, cinv, pr, pred, tw, p1, outer, inner, gs, sw, p, lo, ca, cb, rs, rt = refs[8:]
     fix = Fix()
     core = info[0]
     valid = valid_of(info)
@@ -343,22 +386,12 @@
         sw[c, pl.ds(HS, NXB)] = s_own[c]
         sw[c, pl.ds(off_s, HS)] = off[pl.ds(c * HS, HS)]
         sw[c, pl.ds(on_s, HS)] = on[pl.ds(c * HS, HS)]
-
-    def predict(i):
-        ok = valid(i, HP)
-        m = quad(mw, i)
-        for c in range(3):
-            v = quad(sw, c, i + 1)
-            sides = near(v, fix) + (quad(sw, c, i + 2), quad(sw, c, i))
-            for zp, yp in QUAD:
-                n = [s[zp][yp] for s in sides]
-                total = ((n[0] + n[1]) + (n[2] + n[3])) + (n[4] + n[5])
-                value = 0.4 * v[zp][yp] + 0.1 * total
-                if c == 0:
-                    value = value + (0.4 * m[zp][yp] - 0.2)
-                put(pr, (c, i), zp, yp, ok * value)
-
-    loop(0, WN, predict, 6)
+    mw[pl.ds(core * (HP + NXB), HP)] = off[pl.ds(3 * HS, HP)]
+    mw[pl.ds((1 - core) * (HP + NXB), HP)] = on[pl.ds(3 * HS, HP)]
+    weigh(valid, mw, wt, dg, inv, mc, cw, cinv, fix, False)
+    predict = predicting(valid, mw, sw, 0, pr, fix)
+    loop(0, HP + 1, predict)
+    loop(HP + NXB - 1, WN, predict)
 
     def aim(i):
         a, b = quad(pr, 0, i), quad(pr, 2, i)
@@ -453,7 +486,7 @@
     loop(0, NXB // 2, finish_pair, 4)
     for j in range(NXB // 2):
         plain[192 + 8 * j : 200 + 8 * j, :] = mc[HP // 2 + j]
-    packed = jnp.dot(plain[...], parity_matrix(), precision=HIGH, preferred_element_type=F32)
+    packed = exact_dot(plain[...], parity_matrix())
     plain[...] = packed
     for half in (0, 1):
         g = plain[pl.ds(192 + 8 * (4 * half + row), 8), :]
@@ -520,7 +553,7 @@
 
 
 def advance(times, a, b, wa, wb, pack):
-    each = 2 if times % 2 == 0 else 1
+    each = 4 if times % 4 == 0 else times
 
     def turn(t, carry):
         for k in range(each):
@@ -539,9 +572,10 @@
         half[16 * odd : 16 * odd + 16] = src[pl.ds(32 * odd + 16 * core, 16)]
 
 
-def rows_scan(info, got, swapped, acc, half, wa, wb, a, b):
+def rows_scan(info, got, swapped, acc, to, wa, wb, a, b, half, before):
     pack = Pack()
-    core, row = info[0], info[4]
+    core, row, quarter = info[0], info[4], info[5]
+    before[...] = jnp.zeros_like(before)
     a[...] = jnp.zeros_like(a)
     b[...] = jnp.zeros_like(b)
 
@@ -565,6 +599,9 @@
 
         @pl.when(t <= row)
         def _():
+            for odd in (0, 1):
+                for i in range(16):
+                    before[16 * odd + i] = a[at_layer(32 * odd + 16 * core + i), :]
             advance(8, a, b, wa, wb, pack)
 
             def include(s, l, at, src):
@@ -577,6 +614,15 @@
     for i in range(NC):
         acc[i] = a[at_layer(i), :]
     take_half(half, acc, core)
+    for d in range(4):
+
+        @pl.when(d >= quarter)
+        def _():
+            to[d] = half[...]
+
+        @pl.when(d < quarter)
+        def _():
+            to[d] = before[...]
 
 
 def load_halves(a, own, other, core, add):
@@ -588,7 +634,21 @@
                 a[at, :] = a[at, :] + value if add else value
 
 
-def one_scan(info, acc, own, other, wa, wb, out, half, a, b):
+def even_scan(info, acc, own, other, wa, wb, out, half, a, b):
+    pack = Pack()
+    core, quarter = info[0], info[5]
+    a[...] = jnp.zeros_like(a)
+    b[...] = jnp.zeros_like(b)
+    for back in (3, 2, 1):
+        src = lax.rem(quarter + 4 - back, 4)
+        load_halves(a, own.at[src], other.at[src], core, back < 3)
+        advance(2, a, b, wa, wb, pack)
+    for i in range(NC):
+        out[i] = acc[i] + a[at_layer(i), :]
+    take_half(half, out, core)
+
+
+def one_scan(info, acc, own, other, wa, wb, chunk, out, a, b):
     pack = Pack()
     core = info[0]
     a[...] = jnp.zeros_like(a)
@@ -597,22 +657,6 @@
     advance(1, a, b, wa, wb, pack)
     for i in range(NC):
         out[i] = acc[i] + a[at_layer(i), :]
-    take_half(half, out, core)
-
-
-def even_scan(info, acc, own, other, wa, wb, chunk, out, a, b):
-    pack = Pack()
-    core = info[0]
-    a[...] = jnp.zeros_like(a)
-    b[...] = jnp.zeros_like(b)
-    load_halves(a, own.at[2], other.at[2], core, False)
-    advance(2, a, b, wa, wb, pack)
-    load_halves(a, own.at[1], other.at[1], core, True)
-    advance(2, a, b, wa, wb, pack)
-    load_halves(a, own.at[0], other.at[0], core, True)
-    advance(2, a, b, wa, wb, pack)
-    for i in range(NC):
-        out[i] = acc[i] + a[at_layer(i), :]
     for s in range(4):
         for l in range(4):
             at = 8 * s + 4 * core + l
@@ -629,9 +673,10 @@
     ns = lax.axis_size("space")
     s = lax.axis_index("space")
     y = lax.axis_index("y")
-    z = lax.axis_index("z")
+    quarter = lax.axis_index("zq")
+    z = 2 * quarter + lax.axis_index("zp")
     core = lax.rem(s, 2)
-    info = jnp.stack([core, s > 0, s < ns - 1, y * nz + z > 0, y, s, s, s]).astype(jnp.int32)
+    info = jnp.stack([core, s > 0, s < ns - 1, y * nz + z > 0, y, quarter, s, s]).astype(jnp.int32)
     swap = [(i, i ^ 1) for i in range(ns)]
     cross = [(i, i + 1) for i in range(1, ns - 1, 2)]
     cross = cross + [(b, a) for a, b in cross]
@@ -651,23 +696,23 @@
     s_own, m_own, outer, inner = call(
         prepare,
         [shape(3, NXB, *layer), shape(NXB, *layer), both, both],
-        [info, start, label],
+        [info, pltpu.with_memory_space_constraint(start, pltpu.HBM), pltpu.with_memory_space_constraint(label, pltpu.HBM)],
         [vm(3, 512, 128), pltpu.VMEM((512, 128), jnp.int32), vm(4, 256, 256), pltpu.SemaphoreType.DMA((4,))],
         ANY,
     )
     off, on = exchange(outer, inner)
-    held = call(
-        weights,
-        [window, shape(6, WN, *layer), window, window, shape(CN, 8, 128), shape(6, CN, 8, 128), shape(CN, 8, 128)],
-        [info, m_own, off, on],
+    kept = [window, shape(6, WN, *layer), window, window, shape(CN, 8, 128), shape(6, CN, 8, 128), shape(CN, 8, 128)]
+    kept.append(shape(3, WN, *layer))
+    held = call(inside, kept, [info, s_own, m_own])
+    coarse = [vm(CN, 8, 128)] * 3
+    done = call(
+        first_cycle,
+        kept + [shape(3, NXB, *layer), window, shape(NXB, *layer), edge, edge, shape(3, 8, 8, 128)],
+        [info, s_own, off, on] + list(held),
+        [vm(3, NXB + 2 * HS, *layer), vm(WN, *layer)] + coarse + [vm(3, 12, 8, 128)] * 2,
+        aliases={4 + i: i for i in range(8)},
     )
-    coarse = [vm(CN, 8, 128)] * 3
-    pred, tw, p1, outer, inner, gs = call(
-        first_cycle,
-        [shape(3, NXB, *layer), window, shape(NXB, *layer), edge, edge, shape(3, 8, 8, 128)],
-        [info, s_own, off, on] + list(held),
-        [vm(3, NXB + 2 * HS, *layer), vm(3, WN, *layer), vm(WN, *layer)] + coarse + [vm(3, 12, 8, 128)] * 2,
-    )
+    held, (pred, tw, p1, outer, inner, gs) = done[:7], done[8:]
     off, on = exchange(outer, inner)
     base, send = call(
         second_cycle,
@@ -678,32 +723,28 @@
     got = lax.all_to_all(send.reshape(ny * ns, 5, 8, 128), ("y", "space"), 0, 0)
     got = got.reshape(ny, ns, 5, 8, 128)
     swapped = lax.ppermute(got, "space", swap)
-    acc, half, wa, wb = call(
+    state = [vm(ROWS, 128)] * 2
+    acc, to, wa, wb = call(
         rows_scan,
-        [shape(NC, 8, 128), shape(NC // 2, 8, 128), shape(NC, 8, 128), shape(NC, 8, 128)],
+        [shape(NC, 8, 128), shape(4, NC // 2, 8, 128), shape(NC, 8, 128), shape(NC, 8, 128)],
         [info, got, swapped],
-        [vm(ROWS, 128)] * 2,
+        state + [vm(NC // 2, 8, 128)] * 2,
+    )
+    own = lax.all_to_all(to, "zq", 0, 0)
+    other = lax.ppermute(own, "space", swap)
+    acc, half = call(
+        even_scan, [shape(NC, 8, 128), shape(NC // 2, 8, 128)], [info, acc, own, other, wa, wb], state
     )
     nt = ny * nz
-
-    def shifted(value, k):
-        return lax.ppermute(value, ("y", "z"), [(i, i + k) for i in range(nt - k)])
-
-    own = shifted(half, 1)
-    other = lax.ppermute(own, "space", swap)
-    state = [vm(ROWS, 128)] * 2
-    acc, half = call(
-        one_scan, [shape(NC, 8, 128), shape(NC // 2, 8, 128)], [info, acc, own, other, wa, wb], state
-    )
-    own = jnp.stack([shifted(half, k) for k in (2, 4, 6)])
+    own = lax.ppermute(half, ("y", "zq", "zp"), [(i, i + 1) for i in range(nt - 1)])
     other = lax.ppermute(own, "space", swap)
     (chunks,) = call(
-        even_scan, [shape(8, 4, 8, 128)], [info, acc, own, other, wa, wb], [vm(NC, 8, 128)] + state
+        one_scan, [shape(8, 4, 8, 128)], [info, acc, own, other, wa, wb], [vm(NC, 8, 128)] + state
     )
     (nat,) = call(interleave, [shape(3, 512, 128)], [base])
     back = lax.all_to_all(chunks, "space", 0, 0)
     w = back[:6].reshape(3, 8, 8, 128)
-    (out,) = call(finish, [shape(3, 512, 128)], [nat, w])
+    (out,) = call(finish, [shape(3, 512, 128)], [nat, w], [vm(3, 512, 128), pltpu.SemaphoreType.DMA((3,))], VM, ANY)
     out = out.reshape(3, 32, 2, 8, 128).transpose(0, 1, 3, 2, 4)
     return out.reshape(1, 3, 16, NXB, 256)
 
@@ -711,9 +752,9 @@
 def solution(mesh):
     nz = 8
     ny = mesh.shape["tm"] // nz
-    split = Mesh(mesh.devices.reshape(ny, nz, mesh.shape["space"]), ("y", "z", "space"))
-    in_specs = (P(("y", "z"), None, None, "space", None), P(None, "space", None))
-    out_specs = P(("y", "z"), None, None, "space", None)
+    split = Mesh(mesh.devices.reshape(ny, nz // 2, 2, mesh.shape["space"]), ("y", "zq", "zp", "space"))
+    in_specs = (P(("y", "zq", "zp"), None, None, "space", None), P(None, "space", None))
+    out_specs = P(("y", "zq", "zp"), None, None, "space", None)
 
     def run(start_states, labels):
         return body(ny, nz, start_states, labels)

time: 112 us -> 109 us (0.973); the launches traced: 110 us -> 109 us
  blocking collectives: 19.9 us -> 45.2 us
  starting transfers between devices: 33.2 us -> 20.8 us
  waiting for transfers between devices: 29.2 us -> 18.2 us
  local copies, waits for them, and re-layouts: 2.18 us -> 0.09 us
  Pallas kernels: 25.8 us -> 24.3 us
    all_to_all x0 -> x1, blocking collectives: none -> 25.3 us  [body(): own = lax.all_to_all(to, 'zq', 0, 0)]
    ppermute x4 -> x1, starting transfers between devices: 15.1 us -> 2.97 us  [body(): lax.ppermute(half, ('y', 'zq', 'zp'), [(i, i + 1) for i in range(nt - 1)])]
    ppermute x4 -> x1, waiting for transfers between devices: 16.7 us -> 6.55 us  [body(): lax.ppermute(half, ('y', 'zq', 'zp'), [(i, i + 1) for i in range(nt - 1)])]
    unnamed x4 -> x0, local copies, waits for them, and re-layouts: 2.09 us -> none
    pallas_call x9, Pallas kernels: 25.8 us -> 24.3 us  [call(): pl.pallas_call(kernel, out_shape=outs, in_specs=specs, out_specs=[to] * l...]
    ppermute x2, waiting for transfers between devices: 2.82 us -> 1.51 us  [exchange(): on = lax.ppermute(inner, 'space', swap)]
  transfers between devices with their start and end apart: 12 -> 9, of which waited for: 9 -> 7; matrix products, arithmetic and copies ran while one was open for 0% -> 0% of each run, Pallas kernels for 1% -> 2%
where the time goes in v3:
time: 109 us
  blocking collectives  45.2 us (41%)
  Pallas kernels  24.3 us (22%)
  starting transfers between devices  20.8 us (19%)
  waiting for transfers between devices  18.2 us (17%)
    all_to_all x1, blocking collectives, body(): own = lax.all_to_all(to, 'zq', 0, 0)  25.3 us
    pallas_call x9, Pallas kernels, call(): pl.pallas_call(kernel, out_shape=outs, in_specs=specs, out_specs=[to] * l...  24.3 us
    all_to_all x1, blocking collectives, body(): got = lax.all_to_all(send.reshape(ny * ns, 5, 8, 128), ('y', 'space'), 0, 0)  19.9 us
    ppermute x2, starting transfers between devices, exchange(): on = lax.ppermute(inner, 'space', swap)  12.9 us
    ppermute x1, waiting for transfers between devices, body(): lax.ppermute(half, ('y', 'zq', 'zp'), [(i, i + 1) for i in range(nt - 1)])  6.55 us
    all_to_all x1, waiting for transfers between devices, body(): back = lax.all_to_all(chunks, 'space', 0, 0)  5.03 us
    all_to_all x1, starting transfers between devices, body(): back = lax.all_to_all(chunks, 'space', 0, 0)  3.37 us
    ppermute x2, waiting for transfers between devices, body(): other = lax.ppermute(own, 'space', swap)  3.25 us
  transfers between devices with their start and end apart: 9, of which 7 were waited for; matrix products, arithmetic and copies ran while one was open for 0% of the time, Pallas kernels for 2%

profile of v3, /device:TPU:24, one launch (start us, length us, event | category | flops | bytes accessed | tf_op | source)
XLA Modules:
  0.0 108.9 jit_solution(9409426535378765149)
XLA Ops:
  0.1 3.1 %shard_map.28 = (f32[3,16,2,8,256]{4,3,2,1,0:T(8,128)S(1)}, f32[16,2,8,256]{3,2,1,0:T(8,128)S(1)}, f32[43,2,8,256]{3,2,1,0:T(8,128)S(1)}, f32[43,2,8,256]{3,2,1,0:T(8,128)S(1)}) custom-call(s32[8]{0:T(128)S(1)} %stack.44.info, f32[3,512,128]{2,1,0:T(8,128)} %bitcast.29, s32[512,128]{1,0:T(8,128)} %bitcast.30), custom_call_target="tpu_custom_call" | custom-call | flops 1000000 | bytes 3506208 | tf_op jit(solution)/shard_map/pallas_call | solution.py:27
  3.2 0.7 collective-permute-start
  3.9 2.9 %collective-permute-start.1 = (f32[43,2,8,256]{3,2,1,0:T(8,128)S(1)}, f32[43,2,8,256]{3,2,1,0:T(8,128)S(1)}, u32[]{:S(2)}, u32[]{:S(2)}) collective-permute-start(f32[43,2,8,256]{3,2,1,0:T(8,128)S(1)} %get-tuple-element.40), channel_id=1, source_target_pairs={{0,1},{1,0},{2,3},{3,2},{4,5},{5,4},{6,7},{7,6},{8,9},{9,8},{10,11... | collective-permute-start | bytes 2113544 | tf_op jit(solution)/shard_map/ppermute | solution.py:686
  6.8 1.3 %shard_map.29 = (f32[36,2,8,256]{3,2,1,0:T(8,128)S(1)}, f32[6,36,2,8,256]{4,3,2,1,0:T(8,128)S(1)}, f32[36,2,8,256]{3,2,1,0:T(8,128)S(1)}, f32[36,2,8,256]{3,2,1,...) custom-call(s32[8]{0:T(128)S(1)} %stack.44.info, ...), custom_call_target="tpu_custom_call" | custom-call | flops 1000000 | bytes 8716320 | tf_op jit(solution)/shard_map/pallas_call | solution.py:27
  8.1 0.5 collective-permute-done.1.on
  8.6 3.1 %shard_map.30 = (f32[36,2,8,256]{3,2,1,0:T(8,128)S(1)}, f32[6,36,2,8,256]{4,3,2,1,0:T(8,128)S(1)}, f32[36,2,8,256]{3,2,1,0:T(8,128)S(1)}, f32[36,2,8,256]{3,2,1,...) custom-call(s32[8]{0:T(128)S(1)} %stack.44.info, ...), custom_call_target="tpu_custom_call", output_to_operand_aliasing={{0}: (4, {}), {1}: (5, {}), {2}: (6, {}), {3}: (7, {}), {4}... | custom-call | flops 1000000 | bytes 19595296 | tf_op jit(solution)/shard_map/pallas_call | solution.py:27
  11.7 0.7 collective-permute-start.2
  12.4 10.0 %collective-permute-start.3 = (f32[10,2,8,256]{3,2,1,0:T(8,128)S(1)}, f32[10,2,8,256]{3,2,1,0:T(8,128)S(1)}, u32[]{:S(2)}, u32[]{:S(2)}) collective-permute-start(f32[10,2,8,256]{3,2,1,0:T(8,128)S(1)} %get-tuple-element.54), channel_id=1, source_target_pairs={{0,1},{1,0},{2,3},{3,2},{4,5},{5,4},{6,7},{7,6},{8,9},{9,8},{10,11... | collective-permute-start | bytes 491528 | tf_op jit(solution)/shard_map/ppermute | solution.py:686
  22.3 1.0 collective-permute-done.3.on
  23.4 2.7 %shard_map.31 = (f32[3,16,2,8,256]{4,3,2,1,0:T(8,128)S(1)}, f32[4,4,2,5,8,128]{5,4,3,2,1,0:T(8,128)S(1)}) custom-call(s32[8]{0:T(128)S(1)} %stack.44.info, f32[3,16,2,8,256]{4,3,2,1,0:T(8,128)S(1)} %get-tuple-element.50.pred, f32[36,2,8,256]{3,2,1,0:T(8,128)S(1)} %get-tuple-element.51.tw, f32[16,2,8,256]{3,2,1,0:T(8,128)S(1)} %get-tuple-element.52.p1, ...), custom_call_target="tpu_custom_call" | custom-call | flops 1000000 | bytes 9404448 | tf_op jit(solution)/shard_map/pallas_call | solution.py:27
  26.1 19.9 %all_to_all.15 = f32[32,5,8,128]{3,2,1,0:T(8,128)S(1)} all-to-all(f32[32,5,8,128]{3,2,1,0:T(8,128)S(1)} %bitcast.27), channel_id=1, replica_groups=mesh['y'=4,'zq'=4,'zp'=2,'space'=8] {'y','space'}, dimensions={0} | all-to-all | bytes 1310720 | tf_op jit(solution)/shard_map/all_to_all | solution.py:723
  46.3 1.9 %collective-permute-done.4.swapped = f32[4,8,5,8,128]{4,3,2,1,0:T(8,128)S(1)} collective-permute-done((f32[4,8,5,8,128]{4,3,2,1,0:T(8,128)S(1)}, f32[4,8,5,8,128]{4,3,2,1,0:T(8,128)S(1)}, u32[]{:S(2)}, u32[]{:S(2)}) %collective-permute-start.4) | collective-permute-done | bytes 655392 | tf_op jit(solution)/shard_map/ppermute | solution.py:725
  48.1 7.0 %shard_map.33 = (f32[64,8,128]{2,1,0:T(8,128)S(1)}, f32[4,32,8,128]{3,2,1,0:T(8,128)S(1)}, f32[64,8,128]{2,1,0:T(8,128)S(1)}, f32[64,8,128]{2,1,0:T(8,128)S(1)}) custom-call(s32[8]{0:T(128)S(1)} %stack.44.info, f32[4,8,5,8,128]{4,3,2,1,0:T(8,128)S(1)} %bitcast.26, f32[4,8,5,8,128]{4,3,2,1,0:T(8,128)S(1)} %collective-permute-done.4.swapped), custom_call_target="tpu_custom_call" | custom-call | flops 1000000 | bytes 2621472 | tf_op jit(solution)/shard_map/pallas_call | solution.py:27
  55.2 25.3 %all_to_all.16.own = f32[4,32,8,128]{3,2,1,0:T(8,128)S(1)} all-to-all(f32[4,32,8,128]{3,2,1,0:T(8,128)S(1)} %get-tuple-element.66), channel_id=1, replica_groups=mesh['y'=4,'zq'=4,'zp'=2,'space'=8] {'zq'}, dimensions={0} | all-to-all | bytes 1048576 | tf_op jit(solution)/shard_map/all_to_all | solution.py:733
  80.5 1.9 %collective-permute-done.5.other = f32[4,32,8,128]{3,2,1,0:T(8,128)S(1)} collective-permute-done((f32[4,32,8,128]{3,2,1,0:T(8,128)S(1)}, f32[4,32,8,128]{3,2,1,0:T(8,128)S(1)}, u32[]{:S(2)}, u32[]{:S(2)}) %collective-permute-start.5) | collective-permute-done | bytes 524320 | tf_op jit(solution)/shard_map/ppermute | solution.py:734
  82.4 2.5 %shard_map.34 = (f32[64,8,128]{2,1,0:T(8,128)S(1)}, f32[32,8,128]{2,1,0:T(8,128)S(1)}) custom-call(s32[8]{0:T(128)S(1)} %stack.44.info, f32[64,8,128]{2,1,0:T(8,128)S(1)} %get-tuple-element.65.acc, f32[4,32,8,128]{3,2,1,0:T(8,128)S(1)} %all_to_all.16.own, f32[4,32,8,128]{3,2,1,0:T(8,128)S(1)} %collective-permute-done.5.other, ...), custom_call_target="tpu_custom_call" | custom-call | flops 1000000 | bytes 2228256 | tf_op jit(solution)/shard_map/pallas_call | solution.py:27
  84.9 3.0 %collective-permute-start.6 = (f32[32,8,128]{2,1,0:T(8,128)S(1)}, f32[32,8,128]{2,1,0:T(8,128)S(1)}, u32[]{:S(2)}, u32[]{:S(2)}) collective-permute-start(f32[32,8,128]{2,1,0:T(8,128)S(1)} %get-tuple-element.70), channel_id=1, source_target_pairs={{0,8},{8,16},{16,24},{24,32},{32,40},{40,48},{48,56},{56,64},{64,7... | collective-permute-start | bytes 393224 | tf_op jit(solution)/shard_map/ppermute | solution.py:739
  87.9 6.6 %collective-permute-done.6.own = f32[32,8,128]{2,1,0:T(8,128)S(1)} collective-permute-done((f32[32,8,128]{2,1,0:T(8,128)S(1)}, f32[32,8,128]{2,1,0:T(8,128)S(1)}, u32[]{:S(2)}, u32[]{:S(2)}) %collective-permute-start.6) | collective-permute-done | bytes 131104 | tf_op jit(solution)/shard_map/ppermute | solution.py:739
  94.4 1.3 %collective-permute-done.7.other = f32[32,8,128]{2,1,0:T(8,128)S(1)} collective-permute-done((f32[32,8,128]{2,1,0:T(8,128)S(1)}, f32[32,8,128]{2,1,0:T(8,128)S(1)}, u32[]{:S(2)}, u32[]{:S(2)}) %collective-permute-start.7) | collective-permute-done | bytes 131104 | tf_op jit(solution)/shard_map/ppermute | solution.py:740
  95.8 1.7 %shard_map.35 = f32[8,4,8,128]{3,2,1,0:T(8,128)} custom-call(s32[8]{0:T(128)S(1)} %stack.44.info, f32[64,8,128]{2,1,0:T(8,128)S(1)} %get-tuple-element.69.acc, f32[32,8,128]{2,1,0:T(8,128)S(1)} %collective-permute-done.6.own, f32[32,8,128]{2,1,0:T(8,128)S(1)} %collective-permute-done.7.other, f32[64,8,128]{2,1,0:T(8,128)S(1)} %get-tuple-element.67.wa, ...), custom_call_target="tpu_custom_call" | custom-call | flops 1000000 | bytes 1179680 | tf_op jit(solution)/shard_map/pallas_call | solution.py:27
  97.5 3.4 %all-to-all-start.2 = ((f32[8,4,8,128]{3,2,1,0:T(8,128)}), f32[8,4,8,128]{3,2,1,0:T(8,128)S(1)}, u32[]{:S(2)}, u32[]{:S(2)}) async-start(f32[8,4,8,128]{3,2,1,0:T(8,128)} %shard_map.35), calls=%async_computation.2 | async-start | bytes 262144 | tf_op jit(solution)/shard_map/all_to_all | solution.py:745
  100.9 1.0 shard_map.32.nat
  101.9 5.0 %all-to-all-done.2 = f32[8,4,8,128]{3,2,1,0:T(8,128)S(1)} async-done(((f32[8,4,8,128]{3,2,1,0:T(8,128)}), f32[8,4,8,128]{3,2,1,0:T(8,128)S(1)}, u32[]{:S(2)}, u32[]{:S(2)}) %all-to-all-start.2) | async-done | bytes 131104 | tf_op jit(solution)/shard_map/all_to_all | solution.py:745
  106.9 1.8 %shard_map.36 = f32[3,512,128]{2,1,0:T(8,128)} custom-call(f32[3,512,128]{2,1,0:T(8,128)S(1)} %shard_map.32.nat, f32[3,8,8,128]{3,2,1,0:T(8,128)S(1)} %bitcast.28), custom_call_target="tpu_custom_call" | custom-call | flops 1000000 | bytes 1671168 | tf_op jit(solution)/shard_map/pallas_call | solution.py:27
  (7 shorter events, 0.3 us)
Async XLA Ops:
  3.2 4.9 %collective-permute-start = (f32[43,2,8,256]{3,2,1,0:T(8,128)S(1)}, f32[43,2,8,256]{3,2,1,0:T(8,128)S(1)}, u32[]{:S(2)}, u32[]{:S(2)}) collective-permute-start(f32[43,2,8,256]{3,2,1,0:T(8,128)S(1)} %get-tuple-element.39), channel_id=1, source_target_pairs={{1,2},{3,4},{5,6},{2,1},{4,3},{6,5},{9,10},{11,12},{13,14},{10,9},... | collective-permute-start | bytes 2113544 | tf_op jit(solution)/shard_map/ppermute | solution.py:685
  3.9 4.7 %collective-permute-start.1 = (f32[43,2,8,256]{3,2,1,0:T(8,128)S(1)}, f32[43,2,8,256]{3,2,1,0:T(8,128)S(1)}, u32[]{:S(2)}, u32[]{:S(2)}) collective-permute-start(f32[43,2,8,256]{3,2,1,0:T(8,128)S(1)} %get-tuple-element.40), channel_id=1, source_target_pairs={{0,1},{1,0},{2,3},{3,2},{4,5},{5,4},{6,7},{7,6},{8,9},{9,8},{10,11... | collective-permute-start | bytes 2113544 | tf_op jit(solution)/shard_map/ppermute | solution.py:686
  11.7 10.6 %collective-permute-start.2 = (f32[10,2,8,256]{3,2,1,0:T(8,128)S(1)}, f32[10,2,8,256]{3,2,1,0:T(8,128)S(1)}, u32[]{:S(2)}, u32[]{:S(2)}) collective-permute-start(f32[10,2,8,256]{3,2,1,0:T(8,128)S(1)} %get-tuple-element.53), channel_id=1, source_target_pairs={{1,2},{3,4},{5,6},{2,1},{4,3},{6,5},{9,10},{11,12},{13,14},{10,9},... | collective-permute-start | bytes 491528 | tf_op jit(solution)/shard_map/ppermute | solution.py:685
  12.4 11.0 %collective-permute-start.3 = (f32[10,2,8,256]{3,2,1,0:T(8,128)S(1)}, f32[10,2,8,256]{3,2,1,0:T(8,128)S(1)}, u32[]{:S(2)}, u32[]{:S(2)}) collective-permute-start(f32[10,2,8,256]{3,2,1,0:T(8,128)S(1)} %get-tuple-element.54), channel_id=1, source_target_pairs={{0,1},{1,0},{2,3},{3,2},{4,5},{5,4},{6,7},{7,6},{8,9},{9,8},{10,11... | collective-permute-start | bytes 491528 | tf_op jit(solution)/shard_map/ppermute | solution.py:686
  46.0 2.1 %collective-permute-start.4 = (f32[4,8,5,8,128]{4,3,2,1,0:T(8,128)S(1)}, f32[4,8,5,8,128]{4,3,2,1,0:T(8,128)S(1)}, u32[]{:S(2)}, u32[]{:S(2)}) collective-permute-start(f32[4,8,5,8,128]{4,3,2,1,0:T(8,128)S(1)} %bitcast.25), channel_id=1, source_target_pairs={{0,1},{1,0},{2,3},{3,2},{4,5},{5,4},{6,7},{7,6},{8,9},{9,8},{10,11... | collective-permute-start | bytes 1966088 | tf_op jit(solution)/shard_map/ppermute | solution.py:725
  80.5 1.9 %collective-permute-start.5 = (f32[4,32,8,128]{3,2,1,0:T(8,128)S(1)}, f32[4,32,8,128]{3,2,1,0:T(8,128)S(1)}, u32[]{:S(2)}, u32[]{:S(2)}) collective-permute-start(f32[4,32,8,128]{3,2,1,0:T(8,128)S(1)} %all_to_all.16.own), channel_id=1, source_target_pairs={{0,1},{1,0},{2,3},{3,2},{4,5},{5,4},{6,7},{7,6},{8,9},{9,8},{10,11... | collective-permute-start | bytes 1572872 | tf_op jit(solution)/shard_map/ppermute | solution.py:734
  84.9 9.5 %collective-permute-start.6 = (f32[32,8,128]{2,1,0:T(8,128)S(1)}, f32[32,8,128]{2,1,0:T(8,128)S(1)}, u32[]{:S(2)}, u32[]{:S(2)}) collective-permute-start(f32[32,8,128]{2,1,0:T(8,128)S(1)} %get-tuple-element.70), channel_id=1, source_target_pairs={{0,8},{8,16},{16,24},{24,32},{32,40},{40,48},{48,56},{56,64},{64,7... | collective-permute-start | bytes 393224 | tf_op jit(solution)/shard_map/ppermute | solution.py:739
  94.4 1.3 %collective-permute-start.7 = (f32[32,8,128]{2,1,0:T(8,128)S(1)}, f32[32,8,128]{2,1,0:T(8,128)S(1)}, u32[]{:S(2)}, u32[]{:S(2)}) collective-permute-start(f32[32,8,128]{2,1,0:T(8,128)S(1)} %collective-permute-done.6.own), channel_id=1, source_target_pairs={{0,1},{1,0},{2,3},{3,2},{4,5},{5,4},{6,7},{7,6},{8,9},{9,8},{10,11... | collective-permute-start | bytes 393224 | tf_op jit(solution)/shard_map/ppermute | solution.py:740
  97.5 9.4 %all-to-all-start.2 = ((f32[8,4,8,128]{3,2,1,0:T(8,128)}), f32[8,4,8,128]{3,2,1,0:T(8,128)S(1)}, u32[]{:S(2)}, u32[]{:S(2)}) async-start(f32[8,4,8,128]{3,2,1,0:T(8,128)} %shard_map.35), calls=%async_computation.2 | async-start | bytes 262144 | tf_op jit(solution)/shard_map/all_to_all | solution.py:745

commit v4 on v3

--- a/solution.py
+++ b/solution.py
@@ -572,10 +572,9 @@
         half[16 * odd : 16 * odd + 16] = src[pl.ds(32 * odd + 16 * core, 16)]
 
 
-def rows_scan(info, got, swapped, acc, to, wa, wb, a, b, half, before):
+def rows_scan(info, got, swapped, acc, half, wa, wb, a, b):
     pack = Pack()
-    core, row, quarter = info[0], info[4], info[5]
-    before[...] = jnp.zeros_like(before)
+    core, row = info[0], info[4]
     a[...] = jnp.zeros_like(a)
     b[...] = jnp.zeros_like(b)
 
@@ -599,9 +598,6 @@
 
         @pl.when(t <= row)
         def _():
-            for odd in (0, 1):
-                for i in range(16):
-                    before[16 * odd + i] = a[at_layer(32 * odd + 16 * core + i), :]
             advance(8, a, b, wa, wb, pack)
 
             def include(s, l, at, src):
@@ -614,15 +610,6 @@
     for i in range(NC):
         acc[i] = a[at_layer(i), :]
     take_half(half, acc, core)
-    for d in range(4):
-
-        @pl.when(d >= quarter)
-        def _():
-            to[d] = half[...]
-
-        @pl.when(d < quarter)
-        def _():
-            to[d] = before[...]
 
 
 def load_halves(a, own, other, core, add):
@@ -634,27 +621,29 @@
                 a[at, :] = a[at, :] + value if add else value
 
 
-def even_scan(info, acc, own, other, wa, wb, out, half, a, b):
-    pack = Pack()
-    core, quarter = info[0], info[5]
-    a[...] = jnp.zeros_like(a)
-    b[...] = jnp.zeros_like(b)
-    for back in (3, 2, 1):
-        src = lax.rem(quarter + 4 - back, 4)
-        load_halves(a, own.at[src], other.at[src], core, back < 3)
-        advance(2, a, b, wa, wb, pack)
-    for i in range(NC):
-        out[i] = acc[i] + a[at_layer(i), :]
-    take_half(half, out, core)
-
-
-def one_scan(info, acc, own, other, wa, wb, chunk, out, a, b):
+def one_scan(info, acc, own, other, wa, wb, out, half, a, b):
     pack = Pack()
     core = info[0]
     a[...] = jnp.zeros_like(a)
     b[...] = jnp.zeros_like(b)
     load_halves(a, own, other, core, False)
     advance(1, a, b, wa, wb, pack)
+    for i in range(NC):
+        out[i] = acc[i] + a[at_layer(i), :]
+    take_half(half, out, core)
+
+
+def even_scan(info, acc, own, other, wa, wb, chunk, out, a, b):
+    pack = Pack()
+    core = info[0]
+    a[...] = jnp.zeros_like(a)
+    b[...] = jnp.zeros_like(b)
+    load_halves(a, own.at[2], other.at[2], core, False)
+    advance(2, a, b, wa, wb, pack)
+    load_halves(a, own.at[1], other.at[1], core, True)
+    advance(2, a, b, wa, wb, pack)
+    load_halves(a, own.at[0], other.at[0], core, True)
+    advance(2, a, b, wa, wb, pack)
     for i in range(NC):
         out[i] = acc[i] + a[at_layer(i), :]
     for s in range(4):
@@ -723,23 +712,27 @@
     got = lax.all_to_all(send.reshape(ny * ns, 5, 8, 128), ("y", "space"), 0, 0)
     got = got.reshape(ny, ns, 5, 8, 128)
     swapped = lax.ppermute(got, "space", swap)
-    state = [vm(ROWS, 128)] * 2
-    acc, to, wa, wb = call(
+    acc, half, wa, wb = call(
         rows_scan,
-        [shape(NC, 8, 128), shape(4, NC // 2, 8, 128), shape(NC, 8, 128), shape(NC, 8, 128)],
+        [shape(NC, 8, 128), shape(NC // 2, 8, 128), shape(NC, 8, 128), shape(NC, 8, 128)],
         [info, got, swapped],
-        state + [vm(NC // 2, 8, 128)] * 2,
-    )
-    own = lax.all_to_all(to, "zq", 0, 0)
-    other = lax.ppermute(own, "space", swap)
-    acc, half = call(
-        even_scan, [shape(NC, 8, 128), shape(NC // 2, 8, 128)], [info, acc, own, other, wa, wb], state
+        [vm(ROWS, 128)] * 2,
     )
     nt = ny * nz
-    own = lax.ppermute(half, ("y", "zq", "zp"), [(i, i + 1) for i in range(nt - 1)])
+
+    def shifted(value, k):
+        return lax.ppermute(value, ("y", "zq", "zp"), [(i, i + k) for i in range(nt - k)])
+
+    own = shifted(half, 1)
+    other = lax.ppermute(own, "space", swap)
+    state = [vm(ROWS, 128)] * 2
+    acc, half = call(
+        one_scan, [shape(NC, 8, 128), shape(NC // 2, 8, 128)], [info, acc, own, other, wa, wb], state
+    )
+    own = jnp.stack([shifted(half, k) for k in (2, 4, 6)])
     other = lax.ppermute(own, "space", swap)
     (chunks,) = call(
-        one_scan, [shape(8, 4, 8, 128)], [info, acc, own, other, wa, wb], [vm(NC, 8, 128)] + state
+        even_scan, [shape(8, 4, 8, 128)], [info, acc, own, other, wa, wb], [vm(NC, 8, 128)] + state
     )
     (nat,) = call(interleave, [shape(3, 512, 128)], [base])
     back = lax.all_to_all(chunks, "space", 0, 0)

time: 109 us -> 108 us (level); the launches traced: 109 us -> 106 us
  blocking collectives: 45.2 us -> 19.9 us
  starting transfers between devices: 20.8 us -> 33 us
  waiting for transfers between devices: 18.2 us -> 28.3 us
    all_to_all x1 -> x0, blocking collectives: 25.3 us -> none  [body(): own = lax.all_to_all(to, 'zq', 0, 0)]
    ppermute x1 -> x4, starting transfers between devices: 2.97 us -> 14.9 us  [shifted(): lax.ppermute(value, ('y', 'zq', 'zp'), [(i, i + k) for i in range(nt - k)])]
    ppermute x1 -> x4, waiting for transfers between devices: 6.55 us -> 16.8 us  [shifted(): lax.ppermute(value, ('y', 'zq', 'zp'), [(i, i + k) for i in range(nt - k)])]
  transfers between devices with their start and end apart: 9 -> 12, of which waited for: 7 -> 9; matrix products, arithmetic and copies ran while one was open for 0% -> 0% of each run, Pallas kernels for 2% -> 2%
where the time goes in v4:
time: 108 us; the launch traced here: 106 us
  starting transfers between devices  33 us (31%)
  waiting for transfers between devices  28.3 us (26%)
  Pallas kernels  24.2 us (22%)
  blocking collectives  19.9 us (18%)
    pallas_call x9, Pallas kernels, call(): pl.pallas_call(kernel, out_shape=outs, in_specs=specs, out_specs=[to] * l...  24.2 us
    all_to_all x1, blocking collectives, body(): got = lax.all_to_all(send.reshape(ny * ns, 5, 8, 128), ('y', 'space'), 0, 0)  19.9 us
    ppermute x4, waiting for transfers between devices, shifted(): lax.ppermute(value, ('y', 'zq', 'zp'), [(i, i + k) for i in range(nt - k)])  16.8 us
    ppermute x4, starting transfers between devices, shifted(): lax.ppermute(value, ('y', 'zq', 'zp'), [(i, i + k) for i in range(nt - k)])  14.9 us
    ppermute x2, starting transfers between devices, exchange(): on = lax.ppermute(inner, 'space', swap)  12.9 us
    all_to_all x1, waiting for transfers between devices, body(): back = lax.all_to_all(chunks, 'space', 0, 0)  5.03 us
    all_to_all x1, starting transfers between devices, body(): back = lax.all_to_all(chunks, 'space', 0, 0)  3.37 us
    ppermute x2, waiting for transfers between devices, body(): other = lax.ppermute(own, 'space', swap)  3.05 us
  transfers between devices with their start and end apart: 12, of which 9 were waited for; matrix products, arithmetic and copies ran while one was open for 0% of the time, Pallas kernels for 2%

profile of v4, /device:TPU:24, one launch (start us, length us, event | category | flops | bytes accessed | tf_op | source)
XLA Modules:
  0.0 105.9 jit_solution(3587168597667501891)
XLA Ops:
  0.1 3.1 %shard_map.28 = (f32[3,16,2,8,256]{4,3,2,1,0:T(8,128)S(1)}, f32[16,2,8,256]{3,2,1,0:T(8,128)S(1)}, f32[43,2,8,256]{3,2,1,0:T(8,128)S(1)}, f32[43,2,8,256]{3,2,1,0:T(8,128)S(1)}) custom-call(s32[8]{0:T(128)S(1)} %stack.56.info, f32[3,512,128]{2,1,0:T(8,128)} %bitcast.32, s32[512,128]{1,0:T(8,128)} %bitcast.33), custom_call_target="tpu_custom_call" | custom-call | flops 1000000 | bytes 3506208 | tf_op jit(solution)/shard_map/pallas_call | solution.py:27
  3.9 2.9 %collective-permute-start.1 = (f32[43,2,8,256]{3,2,1,0:T(8,128)S(1)}, f32[43,2,8,256]{3,2,1,0:T(8,128)S(1)}, u32[]{:S(2)}, u32[]{:S(2)}) collective-permute-start(f32[43,2,8,256]{3,2,1,0:T(8,128)S(1)} %get-tuple-element.40), channel_id=1, source_target_pairs={{0,1},{1,0},{2,3},{3,2},{4,5},{5,4},{6,7},{7,6},{8,9},{9,8},{10,11... | collective-permute-start | bytes 2113544 | tf_op jit(solution)/shard_map/ppermute | solution.py:675
  6.8 1.3 %shard_map.29 = (f32[36,2,8,256]{3,2,1,0:T(8,128)S(1)}, f32[6,36,2,8,256]{4,3,2,1,0:T(8,128)S(1)}, f32[36,2,8,256]{3,2,1,0:T(8,128)S(1)}, f32[36,2,8,256]{3,2,1,...) custom-call(s32[8]{0:T(128)S(1)} %stack.56.info, ...), custom_call_target="tpu_custom_call" | custom-call | flops 1000000 | bytes 8716320 | tf_op jit(solution)/shard_map/pallas_call | solution.py:27
  8.6 3.1 %shard_map.30 = (f32[36,2,8,256]{3,2,1,0:T(8,128)S(1)}, f32[6,36,2,8,256]{4,3,2,1,0:T(8,128)S(1)}, f32[36,2,8,256]{3,2,1,0:T(8,128)S(1)}, f32[36,2,8,256]{3,2,1,...) custom-call(s32[8]{0:T(128)S(1)} %stack.56.info, ...), custom_call_target="tpu_custom_call", output_to_operand_aliasing={{0}: (4, {}), {1}: (5, {}), {2}: (6, {}), {3}: (7, {}), {4}... | custom-call | flops 1000000 | bytes 19595296 | tf_op jit(solution)/shard_map/pallas_call | solution.py:27
  12.4 10.0 %collective-permute-start.3 = (f32[10,2,8,256]{3,2,1,0:T(8,128)S(1)}, f32[10,2,8,256]{3,2,1,0:T(8,128)S(1)}, u32[]{:S(2)}, u32[]{:S(2)}) collective-permute-start(f32[10,2,8,256]{3,2,1,0:T(8,128)S(1)} %get-tuple-element.54), channel_id=1, source_target_pairs={{0,1},{1,0},{2,3},{3,2},{4,5},{5,4},{6,7},{7,6},{8,9},{9,8},{10,11... | collective-permute-start | bytes 491528 | tf_op jit(solution)/shard_map/ppermute | solution.py:675
  22.3 1.0 collective-permute-done.3.on
  23.4 2.7 %shard_map.31 = (f32[3,16,2,8,256]{4,3,2,1,0:T(8,128)S(1)}, f32[4,4,2,5,8,128]{5,4,3,2,1,0:T(8,128)S(1)}) custom-call(s32[8]{0:T(128)S(1)} %stack.56.info, f32[3,16,2,8,256]{4,3,2,1,0:T(8,128)S(1)} %get-tuple-element.50.pred, f32[36,2,8,256]{3,2,1,0:T(8,128)S(1)} %get-tuple-element.51.tw, f32[16,2,8,256]{3,2,1,0:T(8,128)S(1)} %get-tuple-element.52.p1, ...), custom_call_target="tpu_custom_call" | custom-call | flops 1000000 | bytes 9404448 | tf_op jit(solution)/shard_map/pallas_call | solution.py:27
  26.1 19.9 %all_to_all.10 = f32[32,5,8,128]{3,2,1,0:T(8,128)S(1)} all-to-all(f32[32,5,8,128]{3,2,1,0:T(8,128)S(1)} %bitcast.30), channel_id=1, replica_groups=mesh['y'=4,'zq'=4,'zp'=2,'space'=8] {'y','space'}, dimensions={0} | all-to-all | bytes 1310720 | tf_op jit(solution)/shard_map/all_to_all | solution.py:712
  46.3 1.9 %collective-permute-done.4.swapped = f32[4,8,5,8,128]{4,3,2,1,0:T(8,128)S(1)} collective-permute-done((f32[4,8,5,8,128]{4,3,2,1,0:T(8,128)S(1)}, f32[4,8,5,8,128]{4,3,2,1,0:T(8,128)S(1)}, u32[]{:S(2)}, u32[]{:S(2)}) %collective-permute-start.4) | collective-permute-done | bytes 655392 | tf_op jit(solution)/shard_map/ppermute | solution.py:714
  48.1 7.0 %shard_map.33 = (f32[64,8,128]{2,1,0:T(8,128)S(1)}, f32[32,8,128]{2,1,0:T(8,128)S(1)}, f32[64,8,128]{2,1,0:T(8,128)S(1)}, f32[64,8,128]{2,1,0:T(8,128)S(1)}) custom-call(s32[8]{0:T(128)S(1)} %stack.56.info, f32[4,8,5,8,128]{4,3,2,1,0:T(8,128)S(1)} %bitcast.29, f32[4,8,5,8,128]{4,3,2,1,0:T(8,128)S(1)} %collective-permute-done.4.swapped), custom_call_target="tpu_custom_call" | custom-call | flops 1000000 | bytes 2228256 | tf_op jit(solution)/shard_map/pallas_call | solution.py:27
  55.1 3.8 %collective-permute-start.5 = (f32[32,8,128]{2,1,0:T(8,128)S(1)}, f32[32,8,128]{2,1,0:T(8,128)S(1)}, u32[]{:S(2)}, u32[]{:S(2)}) collective-permute-start(f32[32,8,128]{2,1,0:T(8,128)S(1)} %get-tuple-element.66), channel_id=1, source_target_pairs={{0,8},{8,16},{16,24},{24,32},{32,40},{40,48},{48,56},{56,64},{64,7... | collective-permute-start | bytes 393224 | tf_op jit(solution)/shard_map/ppermute | solution.py:724
  58.9 6.3 %collective-permute-done.5.own = f32[32,8,128]{2,1,0:T(8,128)S(1)} collective-permute-done((f32[32,8,128]{2,1,0:T(8,128)S(1)}, f32[32,8,128]{2,1,0:T(8,128)S(1)}, u32[]{:S(2)}, u32[]{:S(2)}) %collective-permute-start.5) | collective-permute-done | bytes 131104 | tf_op jit(solution)/shard_map/ppermute | solution.py:724
  65.3 1.3 %collective-permute-done.6.other = f32[32,8,128]{2,1,0:T(8,128)S(1)} collective-permute-done((f32[32,8,128]{2,1,0:T(8,128)S(1)}, f32[32,8,128]{2,1,0:T(8,128)S(1)}, u32[]{:S(2)}, u32[]{:S(2)}) %collective-permute-start.6) | collective-permute-done | bytes 131104 | tf_op jit(solution)/shard_map/ppermute | solution.py:727
  67.6 5.5 %collective-permute-start.9 = (f32[32,8,128]{2,1,0:T(8,128)S(1)}, f32[32,8,128]{2,1,0:T(8,128)S(1)}, u32[]{:S(2)}, u32[]{:S(2)}) collective-permute-start(f32[32,8,128]{2,1,0:T(8,128)S(1)} %get-tuple-element.70), channel_id=1, source_target_pairs={{0,48},{8,56},{16,64},{24,72},{32,80},{40,88},{48,96},{56,104},{64... | collective-permute-start | bytes 393224 | tf_op jit(solution)/shard_map/ppermute | solution.py:724
  73.1 3.4 %collective-permute-start.8 = (f32[32,8,128]{2,1,0:T(8,128)S(1)}, f32[32,8,128]{2,1,0:T(8,128)S(1)}, u32[]{:S(2)}, u32[]{:S(2)}) collective-permute-start(f32[32,8,128]{2,1,0:T(8,128)S(1)} %get-tuple-element.70), channel_id=1, source_target_pairs={{0,32},{8,40},{16,48},{24,56},{32,64},{40,72},{48,80},{56,88},{64,... | collective-permute-start | bytes 393224 | tf_op jit(solution)/shard_map/ppermute | solution.py:724
  76.5 2.2 %collective-permute-start.7 = (f32[32,8,128]{2,1,0:T(8,128)S(1)}, f32[32,8,128]{2,1,0:T(8,128)S(1)}, u32[]{:S(2)}, u32[]{:S(2)}) collective-permute-start(f32[32,8,128]{2,1,0:T(8,128)S(1)} %get-tuple-element.70), channel_id=1, source_target_pairs={{0,16},{8,24},{16,32},{24,40},{32,48},{40,56},{48,64},{56,72},{64,... | collective-permute-start | bytes 393224 | tf_op jit(solution)/shard_map/ppermute | solution.py:724
  78.7 5.9 %collective-permute-done.9 = f32[32,8,128]{2,1,0:T(8,128)S(1)} collective-permute-done((f32[32,8,128]{2,1,0:T(8,128)S(1)}, f32[32,8,128]{2,1,0:T(8,128)S(1)}, u32[]{:S(2)}, u32[]{:S(2)}) %collective-permute-start.9) | collective-permute-done | bytes 131104 | tf_op jit(solution)/shard_map/ppermute | solution.py:724
  84.6 4.6 %collective-permute-done.8 = f32[32,8,128]{2,1,0:T(8,128)S(1)} collective-permute-done((f32[32,8,128]{2,1,0:T(8,128)S(1)}, f32[32,8,128]{2,1,0:T(8,128)S(1)}, u32[]{:S(2)}, u32[]{:S(2)}) %collective-permute-start.8) | collective-permute-done | bytes 131104 | tf_op jit(solution)/shard_map/ppermute | solution.py:724
  89.5 1.7 %collective-permute-done.10.other = f32[3,32,8,128]{3,2,1,0:T(8,128)S(1)} collective-permute-done((f32[3,32,8,128]{3,2,1,0:T(8,128)S(1)}, f32[3,32,8,128]{3,2,1,0:T(8,128)S(1)}, u32[]{:S(2)}, u32[]{:S(2)}) %collective-permute-start.10) | collective-permute-done | bytes 393248 | tf_op jit(solution)/shard_map/ppermute | solution.py:733
  91.2 3.3 %shard_map.35 = f32[8,4,8,128]{3,2,1,0:T(8,128)} custom-call(s32[8]{0:T(128)S(1)} %stack.56.info, f32[64,8,128]{2,1,0:T(8,128)S(1)} %get-tuple-element.69.acc, f32[3,32,8,128]{3,2,1,0:T(8,128)S(1)} %pad_maximum_fusion.own, f32[3,32,8,128]{3,2,1,0:T(8,128)S(1)} %collective-permute-done.10.other, f32[64,8,128]{2,1,0:T(8,128)S(1)} %get-tuple-element.67.wa, ...), custom_call_target="tpu_custom_call" | custom-call | flops 1000000 | bytes 1703968 | tf_op jit(solution)/shard_map/pallas_call | solution.py:27
  94.5 3.4 %all-to-all-start.1 = ((f32[8,4,8,128]{3,2,1,0:T(8,128)}), f32[8,4,8,128]{3,2,1,0:T(8,128)S(1)}, u32[]{:S(2)}, u32[]{:S(2)}) async-start(f32[8,4,8,128]{3,2,1,0:T(8,128)} %shard_map.35), calls=%async_computation.1 | async-start | bytes 262144 | tf_op jit(solution)/shard_map/all_to_all | solution.py:738
  97.9 1.0 shard_map.32.nat
  98.9 5.0 %all-to-all-done.1 = f32[8,4,8,128]{3,2,1,0:T(8,128)S(1)} async-done(((f32[8,4,8,128]{3,2,1,0:T(8,128)}), f32[8,4,8,128]{3,2,1,0:T(8,128)S(1)}, u32[]{:S(2)}, u32[]{:S(2)}) %all-to-all-start.1) | async-done | bytes 131104 | tf_op jit(solution)/shard_map/all_to_all | solution.py:738
  103.9 1.8 %shard_map.36 = f32[3,512,128]{2,1,0:T(8,128)} custom-call(f32[3,512,128]{2,1,0:T(8,128)S(1)} %shard_map.32.nat, f32[3,8,8,128]{3,2,1,0:T(8,128)S(1)} %bitcast.31), custom_call_target="tpu_custom_call" | custom-call | flops 1000000 | bytes 1671168 | tf_op jit(solution)/shard_map/pallas_call | solution.py:27
  (13 shorter events, 3.4 us)
Async XLA Ops:
  3.2 4.9 %collective-permute-start = (f32[43,2,8,256]{3,2,1,0:T(8,128)S(1)}, f32[43,2,8,256]{3,2,1,0:T(8,128)S(1)}, u32[]{:S(2)}, u32[]{:S(2)}) collective-permute-start(f32[43,2,8,256]{3,2,1,0:T(8,128)S(1)} %get-tuple-element.39), channel_id=1, source_target_pairs={{1,2},{3,4},{5,6},{2,1},{4,3},{6,5},{9,10},{11,12},{13,14},{10,9},... | collective-permute-start | bytes 2113544 | tf_op jit(solution)/shard_map/ppermute | solution.py:674
  3.9 4.7 %collective-permute-start.1 = (f32[43,2,8,256]{3,2,1,0:T(8,128)S(1)}, f32[43,2,8,256]{3,2,1,0:T(8,128)S(1)}, u32[]{:S(2)}, u32[]{:S(2)}) collective-permute-start(f32[43,2,8,256]{3,2,1,0:T(8,128)S(1)} %get-tuple-element.40), channel_id=1, source_target_pairs={{0,1},{1,0},{2,3},{3,2},{4,5},{5,4},{6,7},{7,6},{8,9},{9,8},{10,11... | collective-permute-start | bytes 2113544 | tf_op jit(solution)/shard_map/ppermute | solution.py:675
  11.7 10.6 %collective-permute-start.2 = (f32[10,2,8,256]{3,2,1,0:T(8,128)S(1)}, f32[10,2,8,256]{3,2,1,0:T(8,128)S(1)}, u32[]{:S(2)}, u32[]{:S(2)}) collective-permute-start(f32[10,2,8,256]{3,2,1,0:T(8,128)S(1)} %get-tuple-element.53), channel_id=1, source_target_pairs={{1,2},{3,4},{5,6},{2,1},{4,3},{6,5},{9,10},{11,12},{13,14},{10,9},... | collective-permute-start | bytes 491528 | tf_op jit(solution)/shard_map/ppermute | solution.py:674
  12.4 11.0 %collective-permute-start.3 = (f32[10,2,8,256]{3,2,1,0:T(8,128)S(1)}, f32[10,2,8,256]{3,2,1,0:T(8,128)S(1)}, u32[]{:S(2)}, u32[]{:S(2)}) collective-permute-start(f32[10,2,8,256]{3,2,1,0:T(8,128)S(1)} %get-tuple-element.54), channel_id=1, source_target_pairs={{0,1},{1,0},{2,3},{3,2},{4,5},{5,4},{6,7},{7,6},{8,9},{9,8},{10,11... | collective-permute-start | bytes 491528 | tf_op jit(solution)/shard_map/ppermute | solution.py:675
  46.0 2.1 %collective-permute-start.4 = (f32[4,8,5,8,128]{4,3,2,1,0:T(8,128)S(1)}, f32[4,8,5,8,128]{4,3,2,1,0:T(8,128)S(1)}, u32[]{:S(2)}, u32[]{:S(2)}) collective-permute-start(f32[4,8,5,8,128]{4,3,2,1,0:T(8,128)S(1)} %bitcast.28), channel_id=1, source_target_pairs={{0,1},{1,0},{2,3},{3,2},{4,5},{5,4},{6,7},{7,6},{8,9},{9,8},{10,11... | collective-permute-start | bytes 1966088 | tf_op jit(solution)/shard_map/ppermute | solution.py:714
  55.1 10.2 %collective-permute-start.5 = (f32[32,8,128]{2,1,0:T(8,128)S(1)}, f32[32,8,128]{2,1,0:T(8,128)S(1)}, u32[]{:S(2)}, u32[]{:S(2)}) collective-permute-start(f32[32,8,128]{2,1,0:T(8,128)S(1)} %get-tuple-element.66), channel_id=1, source_target_pairs={{0,8},{8,16},{16,24},{24,32},{32,40},{40,48},{48,56},{56,64},{64,7... | collective-permute-start | bytes 393224 | tf_op jit(solution)/shard_map/ppermute | solution.py:724
  65.3 1.3 %collective-permute-start.6 = (f32[32,8,128]{2,1,0:T(8,128)S(1)}, f32[32,8,128]{2,1,0:T(8,128)S(1)}, u32[]{:S(2)}, u32[]{:S(2)}) collective-permute-start(f32[32,8,128]{2,1,0:T(8,128)S(1)} %collective-permute-done.5.own), channel_id=1, source_target_pairs={{0,1},{1,0},{2,3},{3,2},{4,5},{5,4},{6,7},{7,6},{8,9},{9,8},{10,11... | collective-permute-start | bytes 393224 | tf_op jit(solution)/shard_map/ppermute | solution.py:727
  67.6 17.0 %collective-permute-start.9 = (f32[32,8,128]{2,1,0:T(8,128)S(1)}, f32[32,8,128]{2,1,0:T(8,128)S(1)}, u32[]{:S(2)}, u32[]{:S(2)}) collective-permute-start(f32[32,8,128]{2,1,0:T(8,128)S(1)} %get-tuple-element.70), channel_id=1, source_target_pairs={{0,48},{8,56},{16,64},{24,72},{32,80},{40,88},{48,96},{56,104},{64... | collective-permute-start | bytes 393224 | tf_op jit(solution)/shard_map/ppermute | solution.py:724
  73.1 16.1 %collective-permute-start.8 = (f32[32,8,128]{2,1,0:T(8,128)S(1)}, f32[32,8,128]{2,1,0:T(8,128)S(1)}, u32[]{:S(2)}, u32[]{:S(2)}) collective-permute-start(f32[32,8,128]{2,1,0:T(8,128)S(1)} %get-tuple-element.70), channel_id=1, source_target_pairs={{0,32},{8,40},{16,48},{24,56},{32,64},{40,72},{48,80},{56,88},{64,... | collective-permute-start | bytes 393224 | tf_op jit(solution)/shard_map/ppermute | solution.py:724
  76.5 12.7 %collective-permute-start.7 = (f32[32,8,128]{2,1,0:T(8,128)S(1)}, f32[32,8,128]{2,1,0:T(8,128)S(1)}, u32[]{:S(2)}, u32[]{:S(2)}) collective-permute-start(f32[32,8,128]{2,1,0:T(8,128)S(1)} %get-tuple-element.70), channel_id=1, source_target_pairs={{0,16},{8,24},{16,32},{24,40},{32,48},{40,56},{48,64},{56,72},{64,... | collective-permute-start | bytes 393224 | tf_op jit(solution)/shard_map/ppermute | solution.py:724
  89.2 2.0 %collective-permute-start.10 = (f32[3,32,8,128]{3,2,1,0:T(8,128)S(1)}, f32[3,32,8,128]{3,2,1,0:T(8,128)S(1)}, u32[]{:S(2)}, u32[]{:S(2)}) collective-permute-start(f32[3,32,8,128]{3,2,1,0:T(8,128)S(1)} %pad_maximum_fusion.own), channel_id=1, source_target_pairs={{0,1},{1,0},{2,3},{3,2},{4,5},{5,4},{6,7},{7,6},{8,9},{9,8},{10,11... | collective-permute-start | bytes 1179656 | tf_op jit(solution)/shard_map/ppermute | solution.py:733
  94.5 9.4 %all-to-all-start.1 = ((f32[8,4,8,128]{3,2,1,0:T(8,128)}), f32[8,4,8,128]{3,2,1,0:T(8,128)S(1)}, u32[]{:S(2)}, u32[]{:S(2)}) async-start(f32[8,4,8,128]{3,2,1,0:T(8,128)} %shard_map.35), calls=%async_computation.1 | async-start | bytes 262144 | tf_op jit(solution)/shard_map/all_to_all | solution.py:738

commit v5 on v4

--- a/solution.py
+++ b/solution.py
@@ -633,16 +633,18 @@
     take_half(half, out, core)
 
 
-def even_scan(info, acc, own, other, wa, wb, chunk, out, a, b):
+def even_scan(info, acc, *refs):
+    own, other = refs[:3], refs[3:6]
+    wa, wb, chunk, out, a, b = refs[6:]
     pack = Pack()
     core = info[0]
     a[...] = jnp.zeros_like(a)
     b[...] = jnp.zeros_like(b)
-    load_halves(a, own.at[2], other.at[2], core, False)
+    load_halves(a, own[2], other[2], core, False)
     advance(2, a, b, wa, wb, pack)
-    load_halves(a, own.at[1], other.at[1], core, True)
+    load_halves(a, own[1], other[1], core, True)
     advance(2, a, b, wa, wb, pack)
-    load_halves(a, own.at[0], other.at[0], core, True)
+    load_halves(a, own[0], other[0], core, True)
     advance(2, a, b, wa, wb, pack)
     for i in range(NC):
         out[i] = acc[i] + a[at_layer(i), :]
@@ -729,10 +731,10 @@
     acc, half = call(
         one_scan, [shape(NC, 8, 128), shape(NC // 2, 8, 128)], [info, acc, own, other, wa, wb], state
     )
-    own = jnp.stack([shifted(half, k) for k in (2, 4, 6)])
-    other = lax.ppermute(own, "space", swap)
+    own = [shifted(half, k) for k in (2, 4, 6)]
+    other = [lax.ppermute(part, "space", swap) for part in own]
     (chunks,) = call(
-        even_scan, [shape(8, 4, 8, 128)], [info, acc, own, other, wa, wb], [vm(NC, 8, 128)] + state
+        even_scan, [shape(8, 4, 8, 128)], [info, acc] + own + other + [wa, wb], [vm(NC, 8, 128)] + state
     )
     (nat,) = call(interleave, [shape(3, 512, 128)], [base])
     back = lax.all_to_all(chunks, "space", 0, 0)

time: 108 us -> 107 us (level)
    ppermute x2 -> x1, waiting for transfers between devices: 3.05 us -> 1.35 us  [body(): other = lax.ppermute(own, 'space', swap)]
  transfers between devices with their start and end apart: 12 -> 14, of which waited for: 9 -> 10; matrix products, arithmetic and copies ran while one was open for 0% -> 0% of each run, Pallas kernels for 2% -> 2%
where the time goes in v5:
time: 107 us; the launch traced here: 105 us
  starting transfers between devices  33.3 us (31%)
  waiting for transfers between devices  27.6 us (26%)
  Pallas kernels  24.2 us (23%)
  blocking collectives  19.9 us (19%)
    pallas_call x9, Pallas kernels, call(): pl.pallas_call(kernel, out_shape=outs, in_specs=specs, out_specs=[to] * l...  24.2 us
    all_to_all x1, blocking collectives, body(): got = lax.all_to_all(send.reshape(ny * ns, 5, 8, 128), ('y', 'space'), 0, 0)  19.9 us
    ppermute x4, waiting for transfers between devices, shifted(): lax.ppermute(value, ('y', 'zq', 'zp'), [(i, i + k) for i in range(nt - k)])  16.8 us
    ppermute x4, starting transfers between devices, shifted(): lax.ppermute(value, ('y', 'zq', 'zp'), [(i, i + k) for i in range(nt - k)])  14.9 us
    ppermute x2, starting transfers between devices, exchange(): on = lax.ppermute(inner, 'space', swap)  12.9 us
    all_to_all x1, waiting for transfers between devices, body(): back = lax.all_to_all(chunks, 'space', 0, 0)  5.03 us
    all_to_all x1, starting transfers between devices, body(): back = lax.all_to_all(chunks, 'space', 0, 0)  3.37 us
  transfers between devices with their start and end apart: 14, of which 10 were waited for; matrix products, arithmetic and copies ran while one was open for 0% of the time, Pallas kernels for 2%

profile of v5, /device:TPU:24, one launch (start us, length us, event | category | flops | bytes accessed | tf_op | source)
XLA Modules:
  0.0 105.4 jit_solution(11162870541249373140)
XLA Ops:
  0.1 3.1 %shard_map.28 = (f32[3,16,2,8,256]{4,3,2,1,0:T(8,128)S(1)}, f32[16,2,8,256]{3,2,1,0:T(8,128)S(1)}, f32[43,2,8,256]{3,2,1,0:T(8,128)S(1)}, f32[43,2,8,256]{3,2,1,0:T(8,128)S(1)}) custom-call(s32[8]{0:T(128)S(1)} %stack.44.info, f32[3,512,128]{2,1,0:T(8,128)} %bitcast.29, s32[512,128]{1,0:T(8,128)} %bitcast.30), custom_call_target="tpu_custom_call" | custom-call | flops 1000000 | bytes 3506208 | tf_op jit(solution)/shard_map/pallas_call | solution.py:27
  3.9 2.9 %collective-permute-start.1 = (f32[43,2,8,256]{3,2,1,0:T(8,128)S(1)}, f32[43,2,8,256]{3,2,1,0:T(8,128)S(1)}, u32[]{:S(2)}, u32[]{:S(2)}) collective-permute-start(f32[43,2,8,256]{3,2,1,0:T(8,128)S(1)} %get-tuple-element.40), channel_id=1, source_target_pairs={{0,1},{1,0},{2,3},{3,2},{4,5},{5,4},{6,7},{7,6},{8,9},{9,8},{10,11... | collective-permute-start | bytes 2113544 | tf_op jit(solution)/shard_map/ppermute | solution.py:677
  6.8 1.3 %shard_map.29 = (f32[36,2,8,256]{3,2,1,0:T(8,128)S(1)}, f32[6,36,2,8,256]{4,3,2,1,0:T(8,128)S(1)}, f32[36,2,8,256]{3,2,1,0:T(8,128)S(1)}, f32[36,2,8,256]{3,2,1,...) custom-call(s32[8]{0:T(128)S(1)} %stack.44.info, ...), custom_call_target="tpu_custom_call" | custom-call | flops 1000000 | bytes 8716320 | tf_op jit(solution)/shard_map/pallas_call | solution.py:27
  8.6 3.1 %shard_map.30 = (f32[36,2,8,256]{3,2,1,0:T(8,128)S(1)}, f32[6,36,2,8,256]{4,3,2,1,0:T(8,128)S(1)}, f32[36,2,8,256]{3,2,1,0:T(8,128)S(1)}, f32[36,2,8,256]{3,2,1,...) custom-call(s32[8]{0:T(128)S(1)} %stack.44.info, ...), custom_call_target="tpu_custom_call", output_to_operand_aliasing={{0}: (4, {}), {1}: (5, {}), {2}: (6, {}), {3}: (7, {}), {4}... | custom-call | flops 1000000 | bytes 19595296 | tf_op jit(solution)/shard_map/pallas_call | solution.py:27
  12.4 10.0 %collective-permute-start.3 = (f32[10,2,8,256]{3,2,1,0:T(8,128)S(1)}, f32[10,2,8,256]{3,2,1,0:T(8,128)S(1)}, u32[]{:S(2)}, u32[]{:S(2)}) collective-permute-start(f32[10,2,8,256]{3,2,1,0:T(8,128)S(1)} %get-tuple-element.54), channel_id=1, source_target_pairs={{0,1},{1,0},{2,3},{3,2},{4,5},{5,4},{6,7},{7,6},{8,9},{9,8},{10,11... | collective-permute-start | bytes 491528 | tf_op jit(solution)/shard_map/ppermute | solution.py:677
  22.3 1.0 collective-permute-done.3.on
  23.4 2.7 %shard_map.31 = (f32[3,16,2,8,256]{4,3,2,1,0:T(8,128)S(1)}, f32[4,4,2,5,8,128]{5,4,3,2,1,0:T(8,128)S(1)}) custom-call(s32[8]{0:T(128)S(1)} %stack.44.info, f32[3,16,2,8,256]{4,3,2,1,0:T(8,128)S(1)} %get-tuple-element.50.pred, f32[36,2,8,256]{3,2,1,0:T(8,128)S(1)} %get-tuple-element.51.tw, f32[16,2,8,256]{3,2,1,0:T(8,128)S(1)} %get-tuple-element.52.p1, ...), custom_call_target="tpu_custom_call" | custom-call | flops 1000000 | bytes 9404448 | tf_op jit(solution)/shard_map/pallas_call | solution.py:27
  26.1 19.9 %all_to_all.10 = f32[32,5,8,128]{3,2,1,0:T(8,128)S(1)} all-to-all(f32[32,5,8,128]{3,2,1,0:T(8,128)S(1)} %bitcast.27), channel_id=1, replica_groups=mesh['y'=4,'zq'=4,'zp'=2,'space'=8] {'y','space'}, dimensions={0} | all-to-all | bytes 1310720 | tf_op jit(solution)/shard_map/all_to_all | solution.py:714
  46.3 1.9 %collective-permute-done.4.swapped = f32[4,8,5,8,128]{4,3,2,1,0:T(8,128)S(1)} collective-permute-done((f32[4,8,5,8,128]{4,3,2,1,0:T(8,128)S(1)}, f32[4,8,5,8,128]{4,3,2,1,0:T(8,128)S(1)}, u32[]{:S(2)}, u32[]{:S(2)}) %collective-permute-start.4) | collective-permute-done | bytes 655392 | tf_op jit(solution)/shard_map/ppermute | solution.py:716
  48.1 7.0 %shard_map.33 = (f32[64,8,128]{2,1,0:T(8,128)S(1)}, f32[32,8,128]{2,1,0:T(8,128)S(1)}, f32[64,8,128]{2,1,0:T(8,128)S(1)}, f32[64,8,128]{2,1,0:T(8,128)S(1)}) custom-call(s32[8]{0:T(128)S(1)} %stack.44.info, f32[4,8,5,8,128]{4,3,2,1,0:T(8,128)S(1)} %bitcast.26, f32[4,8,5,8,128]{4,3,2,1,0:T(8,128)S(1)} %collective-permute-done.4.swapped), custom_call_target="tpu_custom_call" | custom-call | flops 1000000 | bytes 2228256 | tf_op jit(solution)/shard_map/pallas_call | solution.py:27
  55.1 3.8 %collective-permute-start.5 = (f32[32,8,128]{2,1,0:T(8,128)S(1)}, f32[32,8,128]{2,1,0:T(8,128)S(1)}, u32[]{:S(2)}, u32[]{:S(2)}) collective-permute-start(f32[32,8,128]{2,1,0:T(8,128)S(1)} %get-tuple-element.66), channel_id=1, source_target_pairs={{0,8},{8,16},{16,24},{24,32},{32,40},{40,48},{48,56},{56,64},{64,7... | collective-permute-start | bytes 393224 | tf_op jit(solution)/shard_map/ppermute | solution.py:726
  58.9 6.3 %collective-permute-done.5.own = f32[32,8,128]{2,1,0:T(8,128)S(1)} collective-permute-done((f32[32,8,128]{2,1,0:T(8,128)S(1)}, f32[32,8,128]{2,1,0:T(8,128)S(1)}, u32[]{:S(2)}, u32[]{:S(2)}) %collective-permute-start.5) | collective-permute-done | bytes 131104 | tf_op jit(solution)/shard_map/ppermute | solution.py:726
  65.3 1.3 %collective-permute-done.6.other = f32[32,8,128]{2,1,0:T(8,128)S(1)} collective-permute-done((f32[32,8,128]{2,1,0:T(8,128)S(1)}, f32[32,8,128]{2,1,0:T(8,128)S(1)}, u32[]{:S(2)}, u32[]{:S(2)}) %collective-permute-start.6) | collective-permute-done | bytes 131104 | tf_op jit(solution)/shard_map/ppermute | solution.py:729
  66.6 0.9 shard_map.34
  67.6 5.5 %collective-permute-start.9 = (f32[32,8,128]{2,1,0:T(8,128)S(1)}, f32[32,8,128]{2,1,0:T(8,128)S(1)}, u32[]{:S(2)}, u32[]{:S(2)}) collective-permute-start(f32[32,8,128]{2,1,0:T(8,128)S(1)} %get-tuple-element.70), channel_id=1, source_target_pairs={{0,48},{8,56},{16,64},{24,72},{32,80},{40,88},{48,96},{56,104},{64... | collective-permute-start | bytes 393224 | tf_op jit(solution)/shard_map/ppermute | solution.py:726
  73.1 3.4 %collective-permute-start.8 = (f32[32,8,128]{2,1,0:T(8,128)S(1)}, f32[32,8,128]{2,1,0:T(8,128)S(1)}, u32[]{:S(2)}, u32[]{:S(2)}) collective-permute-start(f32[32,8,128]{2,1,0:T(8,128)S(1)} %get-tuple-element.70), channel_id=1, source_target_pairs={{0,32},{8,40},{16,48},{24,56},{32,64},{40,72},{48,80},{56,88},{64,... | collective-permute-start | bytes 393224 | tf_op jit(solution)/shard_map/ppermute | solution.py:726
  76.5 2.2 %collective-permute-start.7 = (f32[32,8,128]{2,1,0:T(8,128)S(1)}, f32[32,8,128]{2,1,0:T(8,128)S(1)}, u32[]{:S(2)}, u32[]{:S(2)}) collective-permute-start(f32[32,8,128]{2,1,0:T(8,128)S(1)} %get-tuple-element.70), channel_id=1, source_target_pairs={{0,16},{8,24},{16,32},{24,40},{32,48},{40,56},{48,64},{56,72},{64,... | collective-permute-start | bytes 393224 | tf_op jit(solution)/shard_map/ppermute | solution.py:726
  78.7 5.9 %collective-permute-done.9.refs_2_ = f32[32,8,128]{2,1,0:T(8,128)S(1)} collective-permute-done((f32[32,8,128]{2,1,0:T(8,128)S(1)}, f32[32,8,128]{2,1,0:T(8,128)S(1)}, u32[]{:S(2)}, u32[]{:S(2)}) %collective-permute-start.9) | collective-permute-done | bytes 131104 | tf_op jit(solution)/shard_map/ppermute | solution.py:726
  84.6 4.6 %collective-permute-done.8.refs_1_ = f32[32,8,128]{2,1,0:T(8,128)S(1)} collective-permute-done((f32[32,8,128]{2,1,0:T(8,128)S(1)}, f32[32,8,128]{2,1,0:T(8,128)S(1)}, u32[]{:S(2)}, u32[]{:S(2)}) %collective-permute-start.8) | collective-permute-done | bytes 131104 | tf_op jit(solution)/shard_map/ppermute | solution.py:726
  90.7 3.3 %shard_map.35 = f32[8,4,8,128]{3,2,1,0:T(8,128)} custom-call(s32[8]{0:T(128)S(1)} %stack.44.info, f32[64,8,128]{2,1,0:T(8,128)S(1)} %get-tuple-element.69.acc, f32[32,8,128]{2,1,0:T(8,128)S(1)} %collective-permute-done.7.refs_0_, f32[32,8,128]{2,1,0:T(8,128)S(1)} %collective-permute-done.8.refs_1_, f32[32,8,128]{2,1,0:T(8,128)S(1)} %collective-permute-done.9.refs_2_, ...), custom_call_target="tpu_custom_call" | custom-call | flops 1000000 | bytes 1703968 | tf_op jit(solution)/shard_map/pallas_call | solution.py:27
  94.0 3.4 %all-to-all-start.1 = ((f32[8,4,8,128]{3,2,1,0:T(8,128)}), f32[8,4,8,128]{3,2,1,0:T(8,128)S(1)}, u32[]{:S(2)}, u32[]{:S(2)}) async-start(f32[8,4,8,128]{3,2,1,0:T(8,128)} %shard_map.35), calls=%async_computation.1 | async-start | bytes 262144 | tf_op jit(solution)/shard_map/all_to_all | solution.py:740
  97.4 1.0 shard_map.32.nat
  98.4 5.0 %all-to-all-done.1 = f32[8,4,8,128]{3,2,1,0:T(8,128)S(1)} async-done(((f32[8,4,8,128]{3,2,1,0:T(8,128)}), f32[8,4,8,128]{3,2,1,0:T(8,128)S(1)}, u32[]{:S(2)}, u32[]{:S(2)}) %all-to-all-start.1) | async-done | bytes 131104 | tf_op jit(solution)/shard_map/all_to_all | solution.py:740
  103.4 1.8 %shard_map.36 = f32[3,512,128]{2,1,0:T(8,128)} custom-call(f32[3,512,128]{2,1,0:T(8,128)S(1)} %shard_map.32.nat, f32[3,8,8,128]{3,2,1,0:T(8,128)S(1)} %bitcast.28), custom_call_target="tpu_custom_call" | custom-call | flops 1000000 | bytes 1671168 | tf_op jit(solution)/shard_map/pallas_call | solution.py:27
  (16 shorter events, 3.7 us)
Async XLA Ops:
  3.2 4.9 %collective-permute-start = (f32[43,2,8,256]{3,2,1,0:T(8,128)S(1)}, f32[43,2,8,256]{3,2,1,0:T(8,128)S(1)}, u32[]{:S(2)}, u32[]{:S(2)}) collective-permute-start(f32[43,2,8,256]{3,2,1,0:T(8,128)S(1)} %get-tuple-element.39), channel_id=1, source_target_pairs={{1,2},{3,4},{5,6},{2,1},{4,3},{6,5},{9,10},{11,12},{13,14},{10,9},... | collective-permute-start | bytes 2113544 | tf_op jit(solution)/shard_map/ppermute | solution.py:676
  3.9 4.7 %collective-permute-start.1 = (f32[43,2,8,256]{3,2,1,0:T(8,128)S(1)}, f32[43,2,8,256]{3,2,1,0:T(8,128)S(1)}, u32[]{:S(2)}, u32[]{:S(2)}) collective-permute-start(f32[43,2,8,256]{3,2,1,0:T(8,128)S(1)} %get-tuple-element.40), channel_id=1, source_target_pairs={{0,1},{1,0},{2,3},{3,2},{4,5},{5,4},{6,7},{7,6},{8,9},{9,8},{10,11... | collective-permute-start | bytes 2113544 | tf_op jit(solution)/shard_map/ppermute | solution.py:677
  11.7 10.6 %collective-permute-start.2 = (f32[10,2,8,256]{3,2,1,0:T(8,128)S(1)}, f32[10,2,8,256]{3,2,1,0:T(8,128)S(1)}, u32[]{:S(2)}, u32[]{:S(2)}) collective-permute-start(f32[10,2,8,256]{3,2,1,0:T(8,128)S(1)} %get-tuple-element.53), channel_id=1, source_target_pairs={{1,2},{3,4},{5,6},{2,1},{4,3},{6,5},{9,10},{11,12},{13,14},{10,9},... | collective-permute-start | bytes 491528 | tf_op jit(solution)/shard_map/ppermute | solution.py:676
  12.4 11.0 %collective-permute-start.3 = (f32[10,2,8,256]{3,2,1,0:T(8,128)S(1)}, f32[10,2,8,256]{3,2,1,0:T(8,128)S(1)}, u32[]{:S(2)}, u32[]{:S(2)}) collective-permute-start(f32[10,2,8,256]{3,2,1,0:T(8,128)S(1)} %get-tuple-element.54), channel_id=1, source_target_pairs={{0,1},{1,0},{2,3},{3,2},{4,5},{5,4},{6,7},{7,6},{8,9},{9,8},{10,11... | collective-permute-start | bytes 491528 | tf_op jit(solution)/shard_map/ppermute | solution.py:677
  46.0 2.1 %collective-permute-start.4 = (f32[4,8,5,8,128]{4,3,2,1,0:T(8,128)S(1)}, f32[4,8,5,8,128]{4,3,2,1,0:T(8,128)S(1)}, u32[]{:S(2)}, u32[]{:S(2)}) collective-permute-start(f32[4,8,5,8,128]{4,3,2,1,0:T(8,128)S(1)} %bitcast.25), channel_id=1, source_target_pairs={{0,1},{1,0},{2,3},{3,2},{4,5},{5,4},{6,7},{7,6},{8,9},{9,8},{10,11... | collective-permute-start | bytes 1966088 | tf_op jit(solution)/shard_map/ppermute | solution.py:716
  55.1 10.2 %collective-permute-start.5 = (f32[32,8,128]{2,1,0:T(8,128)S(1)}, f32[32,8,128]{2,1,0:T(8,128)S(1)}, u32[]{:S(2)}, u32[]{:S(2)}) collective-permute-start(f32[32,8,128]{2,1,0:T(8,128)S(1)} %get-tuple-element.66), channel_id=1, source_target_pairs={{0,8},{8,16},{16,24},{24,32},{32,40},{40,48},{48,56},{56,64},{64,7... | collective-permute-start | bytes 393224 | tf_op jit(solution)/shard_map/ppermute | solution.py:726
  65.3 1.3 %collective-permute-start.6 = (f32[32,8,128]{2,1,0:T(8,128)S(1)}, f32[32,8,128]{2,1,0:T(8,128)S(1)}, u32[]{:S(2)}, u32[]{:S(2)}) collective-permute-start(f32[32,8,128]{2,1,0:T(8,128)S(1)} %collective-permute-done.5.own), channel_id=1, source_target_pairs={{0,1},{1,0},{2,3},{3,2},{4,5},{5,4},{6,7},{7,6},{8,9},{9,8},{10,11... | collective-permute-start | bytes 393224 | tf_op jit(solution)/shard_map/ppermute | solution.py:729
  67.6 17.0 %collective-permute-start.9 = (f32[32,8,128]{2,1,0:T(8,128)S(1)}, f32[32,8,128]{2,1,0:T(8,128)S(1)}, u32[]{:S(2)}, u32[]{:S(2)}) collective-permute-start(f32[32,8,128]{2,1,0:T(8,128)S(1)} %get-tuple-element.70), channel_id=1, source_target_pairs={{0,48},{8,56},{16,64},{24,72},{32,80},{40,88},{48,96},{56,104},{64... | collective-permute-start | bytes 393224 | tf_op jit(solution)/shard_map/ppermute | solution.py:726
  73.1 16.1 %collective-permute-start.8 = (f32[32,8,128]{2,1,0:T(8,128)S(1)}, f32[32,8,128]{2,1,0:T(8,128)S(1)}, u32[]{:S(2)}, u32[]{:S(2)}) collective-permute-start(f32[32,8,128]{2,1,0:T(8,128)S(1)} %get-tuple-element.70), channel_id=1, source_target_pairs={{0,32},{8,40},{16,48},{24,56},{32,64},{40,72},{48,80},{56,88},{64,... | collective-permute-start | bytes 393224 | tf_op jit(solution)/shard_map/ppermute | solution.py:726
  76.5 12.7 %collective-permute-start.7 = (f32[32,8,128]{2,1,0:T(8,128)S(1)}, f32[32,8,128]{2,1,0:T(8,128)S(1)}, u32[]{:S(2)}, u32[]{:S(2)}) collective-permute-start(f32[32,8,128]{2,1,0:T(8,128)S(1)} %get-tuple-element.70), channel_id=1, source_target_pairs={{0,16},{8,24},{16,32},{24,40},{32,48},{40,56},{48,64},{56,72},{64,... | collective-permute-start | bytes 393224 | tf_op jit(solution)/shard_map/ppermute | solution.py:726
  84.6 5.1 %collective-permute-start.12 = (f32[32,8,128]{2,1,0:T(8,128)S(1)}, f32[32,8,128]{2,1,0:T(8,128)S(1)}, u32[]{:S(2)}, u32[]{:S(2)}) collective-permute-start(f32[32,8,128]{2,1,0:T(8,128)S(1)} %collective-permute-done.9.refs_2_), channel_id=1, source_target_pairs={{0,1},{1,0},{2,3},{3,2},{4,5},{5,4},{6,7},{7,6},{8,9},{9,8},{10,11... | collective-permute-start | bytes 393224 | tf_op jit(solution)/shard_map/ppermute | solution.py:735
  89.2 1.3 %collective-permute-start.11 = (f32[32,8,128]{2,1,0:T(8,128)S(1)}, f32[32,8,128]{2,1,0:T(8,128)S(1)}, u32[]{:S(2)}, u32[]{:S(2)}) collective-permute-start(f32[32,8,128]{2,1,0:T(8,128)S(1)} %collective-permute-done.8.refs_1_), channel_id=1, source_target_pairs={{0,1},{1,0},{2,3},{3,2},{4,5},{5,4},{6,7},{7,6},{8,9},{9,8},{10,11... | collective-permute-start | bytes 393224 | tf_op jit(solution)/shard_map/ppermute | solution.py:735
  89.2 1.5 %collective-permute-start.10 = (f32[32,8,128]{2,1,0:T(8,128)S(1)}, f32[32,8,128]{2,1,0:T(8,128)S(1)}, u32[]{:S(2)}, u32[]{:S(2)}) collective-permute-start(f32[32,8,128]{2,1,0:T(8,128)S(1)} %collective-permute-done.7.refs_0_), channel_id=1, source_target_pairs={{0,1},{1,0},{2,3},{3,2},{4,5},{5,4},{6,7},{7,6},{8,9},{9,8},{10,11... | collective-permute-start | bytes 393224 | tf_op jit(solution)/shard_map/ppermute | solution.py:735
  94.0 9.4 %all-to-all-start.1 = ((f32[8,4,8,128]{3,2,1,0:T(8,128)}), f32[8,4,8,128]{3,2,1,0:T(8,128)S(1)}, u32[]{:S(2)}, u32[]{:S(2)}) async-start(f32[8,4,8,128]{3,2,1,0:T(8,128)} %shard_map.35), calls=%async_computation.1 | async-start | bytes 262144 | tf_op jit(solution)/shard_map/all_to_all | solution.py:740
